TPU v7x, 32 devices: a whole 2x2x4 slice. The times are simulated.
32 devices in a mesh: seq: 8 (over z, x), tp: 4 (over y, core).
Axes of the slice: x: 2, y: 2, z: 4, core: 2. Of those that a mesh axis runs over, the one named last changes fastest.
Arguments:
- inputs: bfloat16 [8192, 2048], P(('seq', 'tp')), may hold values from -6 to 6
- lengths: int32 [3], replicated, may hold values from 512 to 7168, as said below
- gain_attn: float32 [2048], P('seq'), may hold values from 0.5 to 1.5
- w_query: float32 [2048, 256], P('seq', 'tp'), may hold values from -0.25 to 0.25
- w_key: float32 [2048, 256], P('seq', 'tp'), may hold values from -0.25 to 0.25
- w_value: float32 [2048, 2048], P('seq', 'tp'), may hold values from -0.125 to 0.125
- w_out: float32 [2048, 2048], P('tp', 'seq'), may hold values from -0.5 to 0.5
- gain_mlp: float32 [2048], P('seq'), may hold values from 0.5 to 1.5
- w_gate: float32 [2048, 5504], P('seq', 'tp'), may hold values from -0.125 to 0.125
- w_up: float32 [2048, 5504], P('seq', 'tp'), may hold values from -0.125 to 0.125
- w_down: float32 [5504, 2048], P('tp', 'seq'), may hold values from -0.078125 to 0.078125
- cotangent: bfloat16 [8192, 2048], P(('seq', 'tp')), may hold values from -6 to 6
Outputs:
- block_output: bfloat16 [8192, 2048], P(('seq', 'tp'))
- input_grad: float32 [8192, 2048], P(('seq', 'tp'))
- grad_gain_attn: float32 [2048], P('seq')
- grad_w_query: float32 [2048, 256], P('seq', 'tp')
- grad_w_key: float32 [2048, 256], P('seq', 'tp')
- grad_w_value: float32 [2048, 2048], P('seq', 'tp')
- grad_w_out: float32 [2048, 2048], P('tp', 'seq')
- grad_gain_mlp: float32 [2048], P('seq')
- grad_w_gate: float32 [2048, 5504], P('seq', 'tp')
- grad_w_up: float32 [2048, 5504], P('seq', 'tp')
- grad_w_down: float32 [5504, 2048], P('tp', 'seq')
Inputs may be any that keep to these rules, and one draw needn't show every extreme that they name: `lengths`: 3 rows laid end to end from token 0: 2 of 512 tokens and one of 7168; the long row is the second of them, and it starts in the first block of 1024 tokens and ends in the last.
All inputs are finite; a program needn't handle non-finite values.
Results may differ from a plain program's by a relative error of at most 0.022.
Values may be sent and summed in bfloat16 or wider, within the bound.
A program may use at most 256 MiB of HBM per device.

v0:
```python
import jax
import jax.numpy as jnp
from jax import lax
from jax.sharding import PartitionSpec as P

FEAT = 16
VHEAD = 128


epsilon = 1e-05
linear_coef = 0.5
square_coef = 0.17677669529663687
highest = lax.Precision.HIGHEST


def prefix(array, axis, join, neutral):
    place = lax.axis_index(axis)
    gathered = jax.tree.map(
        lambda a, kind: lax.all_gather(a.astype(kind), axis),
        array,
        (jnp.bfloat16, jnp.bfloat16, jnp.bfloat16),
    )
    state = jax.tree.map(lambda a, e: jnp.zeros_like(a) + jnp.asarray(e, a.dtype), array, neutral)

    def prefix_one(turn, state):
        return join(
            state,
            jax.tree.map(
                lambda a, own: lax.dynamic_index_in_dim(a, turn, 0, False).astype(own.dtype),
                gathered,
                array,
            ),
        )

    return lax.fori_loop(0, place, prefix_one, state)


def carried_in(array, axis, join, neutral):
    count = lax.axis_size(axis)
    place = lax.axis_index(axis)
    ahead = count - 1 - place
    gathered = jax.tree.map(
        lambda a, kind: lax.all_gather(a.astype(kind), axis),
        array,
        jax.tree.map(lambda a: jnp.bfloat16 if a.dtype == jnp.float32 else a.dtype, array),
    )
    state = jax.tree.map(lambda a, e: jnp.zeros_like(a) + jnp.asarray(e, a.dtype), array, neutral)

    def carried_one(turn, state):
        source = count - 1 - turn
        return join(
            state,
            jax.tree.map(
                lambda a, own: lax.dynamic_index_in_dim(a, source, 0, False).astype(own.dtype),
                gathered,
                array,
            ),
        )

    return lax.fori_loop(0, ahead, carried_one, state)


def features(vector):
    squares = (vector[..., :, None] * vector[..., None, :]).reshape(
        vector.shape[:-1] + (vector.shape[-1] * vector.shape[-1],)
    )
    return jnp.concatenate(
        [jnp.ones_like(vector[..., :1]), vector * linear_coef, squares * square_coef], axis=-1
    )


def feature_grad(vector, grad_feat):
    feat_width = vector.shape[-1]
    linear_part = grad_feat[..., 1 : 1 + feat_width]
    square_part = grad_feat[..., 1 + feat_width :].reshape(vector.shape + (feat_width,))
    mixed_part = jnp.sum(square_part * vector[..., None, :], axis=-1) + jnp.sum(
        square_part * vector[..., :, None], axis=-2
    )
    return linear_coef * linear_part + square_coef * mixed_part


def segment_masks(anchor, starts, length):
    positions = anchor + jnp.arange(length, dtype=jnp.int32)
    start_le = starts[None, :] <= positions[:, None]
    row_ids = jnp.sum(start_le.astype(jnp.int32), axis=1)
    inside = (starts >= anchor) & (starts < anchor + length)
    carried = jnp.sum(((starts[None, :] >= anchor) & start_le).astype(jnp.int32), axis=1) == 0
    after_last = (
        jnp.sum(
            ((starts[None, :] > positions[:, None]) & inside[None, :]).astype(jnp.int32), axis=1
        )
        == 0
    )
    resets = jnp.sum(inside.astype(jnp.int32)) > 0
    return (positions, row_ids, carried, after_last, resets)


def segment_combine(earlier, later):
    persist = 1.0 - later[2]
    return (
        later[0] + persist * earlier[0],
        later[1] + persist * earlier[1],
        jnp.maximum(earlier[2], later[2]),
    )


def rms_scale(values):
    return lax.rsqrt(jnp.mean(values * values, axis=-1, keepdims=True) + epsilon)


def norm_back(grad_out, normed, scale, gain):
    grad_normed = grad_out * gain
    return scale * (grad_normed - normed * jnp.mean(grad_normed * normed, axis=-1, keepdims=True))


def pair_block(query_part, key_heads, row_ids, positions, first_row, span_rows):
    scores = (
        jnp.einsum("thf,shf->hts", query_part, key_heads, preferred_element_type=jnp.float32) * 0.25
    )
    rows_here = row_ids[first_row : first_row + span_rows]
    place_here = positions[first_row : first_row + span_rows]
    allowed = (
        (rows_here[:, None] == row_ids[None, :]) & (positions[None, :] <= place_here[:, None])
    ).astype(jnp.float32)
    kernel = (1.0 + scores + 0.5 * scores * scores) * allowed[None]
    return (scores, allowed, kernel)


def on_device(
    inputs,
    lengths,
    gain_attn,
    w_query,
    w_key,
    w_value,
    w_out,
    gain_mlp,
    w_gate,
    w_up,
    w_down,
    cotangent,
):
    lowered = (
        gain_attn.astype(jnp.bfloat16),
        w_query.astype(jnp.bfloat16),
        w_key.astype(jnp.bfloat16),
        w_value.astype(jnp.bfloat16),
        w_out.astype(jnp.bfloat16),
        gain_mlp.astype(jnp.bfloat16),
        w_gate.astype(jnp.bfloat16),
        w_up.astype(jnp.bfloat16),
        w_down.astype(jnp.bfloat16),
    )
    (
        gain_first,
        query_proj,
        key_proj,
        value_proj,
        out_proj,
        gain_second,
        gate_proj,
        up_proj,
        down_proj,
    ) = (
        lax.all_gather(lowered[0], "seq", axis=0, tiled=True),
        lax.all_gather(lowered[1], "seq", axis=0, tiled=True),
        lax.all_gather(lowered[2], "seq", axis=0, tiled=True),
        lax.all_gather(lowered[3], "seq", axis=0, tiled=True),
        lax.all_gather(lowered[4], "seq", axis=1, tiled=True),
        lax.all_gather(lowered[5], "seq", axis=0, tiled=True),
        lax.all_gather(lowered[6], "seq", axis=0, tiled=True),
        lax.all_gather(lowered[7], "seq", axis=0, tiled=True),
        lax.all_gather(lowered[8], "seq", axis=1, tiled=True),
    )
    rows_own = inputs.shape[0]
    tp_count = lax.axis_size("tp")
    block_len = rows_own * tp_count
    seq_index = lax.axis_index("seq")
    tp_index = lax.axis_index("tp")
    starts = jnp.cumsum(lengths) - lengths
    anchor = seq_index * block_len
    positions, row_ids, carried, after_last, resets = segment_masks(anchor, starts, block_len)
    carry_mask = carried.astype(jnp.float32)
    last_mask = after_last.astype(jnp.float32)
    reset_flag = resets.astype(jnp.float32).reshape(1)
    gain_first_f = gain_first.astype(jnp.float32)
    gain_second_f = gain_second.astype(jnp.float32)
    inputs_full = lax.all_gather(inputs, "tp", axis=0, tiled=True).astype(jnp.float32)
    scale_first = rms_scale(inputs_full)
    normed_first = inputs_full * scale_first
    hidden_first = (normed_first * gain_first_f).astype(jnp.bfloat16)
    queries = jnp.dot(hidden_first, query_proj, preferred_element_type=jnp.float32).astype(
        jnp.bfloat16
    )
    key_flat = jnp.dot(hidden_first, key_proj, preferred_element_type=jnp.float32).astype(
        jnp.bfloat16
    )
    value_flat = jnp.dot(hidden_first, value_proj, preferred_element_type=jnp.float32).astype(
        jnp.bfloat16
    )
    heads_local = queries.shape[1] // FEAT
    query_heads = queries.reshape(block_len, heads_local, FEAT)
    key_heads = key_flat.reshape(block_len, heads_local, FEAT)
    value_heads = value_flat.reshape(block_len, heads_local, VHEAD)
    query_float = query_heads.astype(jnp.float32)
    key_float = key_heads.astype(jnp.float32)
    value_float = value_heads.astype(jnp.float32)
    key_feat = features(key_float) * last_mask[:, None, None]
    local_state = jnp.einsum("thn,thv->hnv", key_feat, value_float, precision=highest)
    local_sum = jnp.sum(key_feat, axis=0)
    zero_state = jnp.zeros_like(local_state)
    zero_sum = jnp.zeros_like(local_sum)
    carry_state, carry_sum, unused_flag = prefix(
        (local_state, local_sum, reset_flag),
        "seq",
        segment_combine,
        (zero_state, zero_sum, jnp.zeros_like(reset_flag)),
    )
    step_rows = 512
    query_feat = features(query_float)
    carry_weight = carry_mask[:, None]
    numer_parts = []
    denom_parts = []
    for first_row in range(0, block_len, step_rows):
        query_part = query_heads[first_row : first_row + step_rows]
        scores, allowed, kernel = pair_block(
            query_part, key_heads, row_ids, positions, first_row, step_rows
        )
        numer_parts.append(
            jnp.einsum(
                "hts,shv->thv",
                kernel.astype(jnp.bfloat16),
                value_heads,
                preferred_element_type=jnp.float32,
            )
        )
        denom_parts.append(jnp.sum(kernel, axis=-1).T)
    numerator = (
        jnp.concatenate(numer_parts, axis=0)
        + jnp.einsum("thn,hnv->thv", query_feat, carry_state, precision=highest)
        * carry_weight[:, :, None]
    )
    denominator = (
        jnp.concatenate(denom_parts, axis=0)
        + jnp.einsum("thn,hn->th", query_feat, carry_sum, precision=highest) * carry_weight
    )
    attended = numerator / denominator[:, :, None]
    attended_low = attended.reshape(block_len, heads_local * VHEAD).astype(jnp.bfloat16)
    attn_partial = jnp.dot(attended_low, out_proj, preferred_element_type=jnp.float32)
    branch = lax.psum(attn_partial.astype(jnp.bfloat16), "tp").astype(jnp.float32)
    middle = inputs_full + branch
    scale_second_all = rms_scale(middle)
    normed_second_all = middle * scale_second_all
    hidden_second = (normed_second_all * gain_second_f).astype(jnp.bfloat16)
    middle_own = lax.dynamic_slice_in_dim(middle, tp_index * rows_own, rows_own, 0)
    normed_second = lax.dynamic_slice_in_dim(normed_second_all, tp_index * rows_own, rows_own, 0)
    gate_value = jnp.dot(hidden_second, gate_proj, preferred_element_type=jnp.float32)
    upward = jnp.dot(hidden_second, up_proj, preferred_element_type=jnp.float32)
    sigmoid_gate = jax.nn.sigmoid(gate_value)
    silu_gate = gate_value * sigmoid_gate
    mixed_rows = (silu_gate * upward).astype(jnp.bfloat16)
    mlp_own = lax.psum_scatter(
        jnp.dot(mixed_rows, down_proj, preferred_element_type=jnp.float32).astype(jnp.bfloat16),
        "tp",
        scatter_dimension=0,
        tiled=True,
    ).astype(jnp.float32)
    block_output = (middle_own + mlp_own).astype(jnp.bfloat16)
    grad_full = lax.all_gather(cotangent, "tp", axis=0, tiled=True)
    grad_mixed = jnp.dot(grad_full, down_proj.T, preferred_element_type=jnp.float32).astype(
        jnp.bfloat16
    )
    grad_down = jnp.dot(mixed_rows.T, grad_full, preferred_element_type=jnp.float32)
    grad_mixed_float = grad_mixed.astype(jnp.float32)
    grad_gate = (
        grad_mixed_float * upward * sigmoid_gate * (1.0 + gate_value * (1.0 - sigmoid_gate))
    ).astype(jnp.bfloat16)
    grad_upward = (grad_mixed_float * silu_gate).astype(jnp.bfloat16)
    grad_gate_w = jnp.dot(hidden_second.T, grad_gate, preferred_element_type=jnp.float32)
    grad_up_w = jnp.dot(hidden_second.T, grad_upward, preferred_element_type=jnp.float32)
    hidden_partial = jnp.dot(grad_gate, gate_proj.T, preferred_element_type=jnp.float32) + jnp.dot(
        grad_upward, up_proj.T, preferred_element_type=jnp.float32
    )
    grad_hidden_all = lax.psum(hidden_partial.astype(jnp.bfloat16), "tp").astype(jnp.float32)
    grad_middle_all = grad_full.astype(jnp.float32) + norm_back(
        grad_hidden_all, normed_second_all, scale_second_all, gain_second_f
    )
    grad_branch = grad_middle_all.astype(jnp.bfloat16)
    grad_middle_own = lax.dynamic_slice_in_dim(grad_middle_all, tp_index * rows_own, rows_own, 0)
    grad_hidden_own = lax.dynamic_slice_in_dim(grad_hidden_all, tp_index * rows_own, rows_own, 0)
    gain_second_part = jnp.sum(grad_hidden_own * normed_second, axis=0)
    grad_out_w = jnp.dot(attended_low.T, grad_branch, preferred_element_type=jnp.float32)
    grad_attended = jnp.dot(grad_branch, out_proj.T, preferred_element_type=jnp.float32).reshape(
        block_len, heads_local, VHEAD
    )
    grad_numer = (grad_attended / denominator[:, :, None]).astype(jnp.bfloat16)
    grad_denom = -jnp.sum(grad_attended * attended, axis=-1) / denominator
    grad_numer_carried = grad_numer.astype(jnp.float32) * carry_weight[:, :, None]
    grad_denom_carried = grad_denom * carry_weight
    grad_state_in = jnp.einsum("thn,thv->hnv", query_feat, grad_numer_carried, precision=highest)
    grad_sum_in = jnp.einsum("thn,th->hn", query_feat, grad_denom_carried, precision=highest)
    grad_query_feat = (
        jnp.einsum("thv,hnv->thn", grad_numer_carried, carry_state, precision=highest)
        + grad_denom_carried[:, :, None] * carry_sum[None]
    )
    grad_state_out, grad_sum_out, unused_back = carried_in(
        (grad_state_in, grad_sum_in, reset_flag),
        "seq",
        segment_combine,
        (zero_state, zero_sum, jnp.zeros_like(reset_flag)),
    )
    grad_key_feat = (
        jnp.einsum("thv,hnv->thn", value_float, grad_state_out, precision=highest)
        + grad_sum_out[None]
    ) * last_mask[:, None, None]
    grad_value_state = jnp.einsum("thn,hnv->thv", key_feat, grad_state_out, precision=highest)
    grad_query_parts = []
    grad_key_inner = jnp.zeros((block_len, heads_local, FEAT), jnp.float32)
    grad_value_inner = jnp.zeros((block_len, heads_local, VHEAD), jnp.float32)
    for first_row in range(0, block_len, step_rows):
        query_part = query_heads[first_row : first_row + step_rows]
        scores, allowed, kernel = pair_block(
            query_part, key_heads, row_ids, positions, first_row, step_rows
        )
        numer_grad_part = grad_numer[first_row : first_row + step_rows]
        grad_weights = jnp.einsum(
            "thv,shv->hts", numer_grad_part, value_heads, preferred_element_type=jnp.float32
        )
        grad_scores = (
            (grad_weights + grad_denom[first_row : first_row + step_rows].T[:, :, None])
            * allowed[None]
            * (1.0 + scores)
        ).astype(jnp.bfloat16)
        grad_query_parts.append(
            jnp.einsum("hts,shf->thf", grad_scores, key_heads, preferred_element_type=jnp.float32)
            * 0.25
        )
        grad_key_inner = (
            grad_key_inner
            + jnp.einsum(
                "hts,thf->shf", grad_scores, query_part, preferred_element_type=jnp.float32
            )
            * 0.25
        )
        grad_value_inner = grad_value_inner + jnp.einsum(
            "hts,thv->shv",
            kernel.astype(jnp.bfloat16),
            numer_grad_part,
            preferred_element_type=jnp.float32,
        )
    grad_query = (
        jnp.concatenate(grad_query_parts, axis=0) + feature_grad(query_float, grad_query_feat)
    ).astype(jnp.bfloat16)
    grad_key = (grad_key_inner + feature_grad(key_float, grad_key_feat)).astype(jnp.bfloat16)
    grad_value = (grad_value_inner + grad_value_state).astype(jnp.bfloat16)
    grad_query = grad_query.reshape(block_len, heads_local * FEAT)
    grad_key = grad_key.reshape(block_len, heads_local * FEAT)
    grad_value = grad_value.reshape(block_len, heads_local * VHEAD)
    grad_query_w = jnp.dot(hidden_first.T, grad_query, preferred_element_type=jnp.float32)
    grad_key_w = jnp.dot(hidden_first.T, grad_key, preferred_element_type=jnp.float32)
    grad_value_w = jnp.dot(hidden_first.T, grad_value, preferred_element_type=jnp.float32)
    first_partial = (
        jnp.dot(grad_query, query_proj.T, preferred_element_type=jnp.float32)
        + jnp.dot(grad_key, key_proj.T, preferred_element_type=jnp.float32)
        + jnp.dot(grad_value, value_proj.T, preferred_element_type=jnp.float32)
    )
    gain_first_part = jnp.sum(first_partial * normed_first, axis=0)
    gain_tiles = jnp.broadcast_to(
        jnp.stack([gain_first_part, gain_second_part])[None],
        (tp_count, 2, gain_first_part.shape[0]),
    )
    grad_hidden_first, gain_rows = (
        lax.psum_scatter(
            first_partial.astype(jnp.bfloat16), "tp", scatter_dimension=0, tiled=True
        ).astype(jnp.float32),
        lax.psum_scatter(
            gain_tiles.astype(jnp.bfloat16), "tp", scatter_dimension=0, tiled=True
        ).astype(jnp.float32),
    )
    normed_first_own = lax.dynamic_slice_in_dim(normed_first, tp_index * rows_own, rows_own, 0)
    scale_first_own = lax.dynamic_slice_in_dim(scale_first, tp_index * rows_own, rows_own, 0)
    grad_input_own = grad_middle_own + norm_back(
        grad_hidden_first, normed_first_own, scale_first_own, gain_first_f
    )
    summed = (
        lax.psum_scatter(
            gain_rows[0, 0].astype(jnp.bfloat16), "seq", scatter_dimension=0, tiled=True
        ).astype(jnp.float32),
        lax.psum_scatter(
            grad_query_w.astype(jnp.bfloat16), "seq", scatter_dimension=0, tiled=True
        ).astype(jnp.float32),
        lax.psum_scatter(
            grad_key_w.astype(jnp.bfloat16), "seq", scatter_dimension=0, tiled=True
        ).astype(jnp.float32),
        lax.psum_scatter(
            grad_value_w.astype(jnp.bfloat16), "seq", scatter_dimension=0, tiled=True
        ).astype(jnp.float32),
        lax.psum_scatter(
            grad_out_w.astype(jnp.bfloat16), "seq", scatter_dimension=1, tiled=True
        ).astype(jnp.float32),
        lax.psum_scatter(
            gain_rows[0, 1].astype(jnp.bfloat16), "seq", scatter_dimension=0, tiled=True
        ).astype(jnp.float32),
        lax.psum_scatter(
            grad_gate_w.astype(jnp.bfloat16), "seq", scatter_dimension=0, tiled=True
        ).astype(jnp.float32),
        lax.psum_scatter(
            grad_up_w.astype(jnp.bfloat16), "seq", scatter_dimension=0, tiled=True
        ).astype(jnp.float32),
        lax.psum_scatter(
            grad_down.astype(jnp.bfloat16), "seq", scatter_dimension=1, tiled=True
        ).astype(jnp.float32),
    )
    return (
        block_output,
        grad_input_own,
        summed[0],
        summed[1],
        summed[2],
        summed[3],
        summed[4],
        summed[5],
        summed[6],
        summed[7],
        summed[8],
    )


def solution(mesh):
    in_specs = (
        P(("seq", "tp"), None),
        P(),
        P("seq"),
        P("seq", "tp"),
        P("seq", "tp"),
        P("seq", "tp"),
        P("tp", "seq"),
        P("seq"),
        P("seq", "tp"),
        P("seq", "tp"),
        P("tp", "seq"),
        P(("seq", "tp"), None),
    )
    out_specs = (
        P(("seq", "tp"), None),
        P(("seq", "tp"), None),
        P("seq"),
        P("seq", "tp"),
        P("seq", "tp"),
        P("seq", "tp"),
        P("tp", "seq"),
        P("seq"),
        P("seq", "tp"),
        P("seq", "tp"),
        P("tp", "seq"),
    )
    return jax.shard_map(
        on_device, mesh=mesh, in_specs=in_specs, out_specs=out_specs, check_vma=False
    )
```

profile of v0, /device:TPU:0, one launch (start us, length us, event | category | flops | bytes accessed | tf_op | source)
XLA Modules:
  0.0 1523.1 jit_solution(9272533839789808211)
XLA Ops:
  10.5 22.2 %all-gather.4 = bf16[8,1,256]{2,1,0:T(2,128)(2,1)S(1)} all-gather(bf16[1,1,256]{2,1,0:T(2,128)(2,1)S(1)} %reshape.346), channel_id=1, replica_groups=mesh['seq'=8,'tp'=4] {'seq'}, dimensions={0}, use_global_device_ids=true | all-gather | bytes 4608 | tf_op jit(solution)/shard_map/all_gather | solution.py:165
  34.4 31.3 %all_gather.67 = bf16[2048,64]{0,1:T(8,128)(2,1)S(1)} all-gather(bf16[256,64]{0,1:T(8,128)(2,1)S(1)} %convert_element_type.353), channel_id=1, replica_groups=mesh['seq'=8,'tp'=4] {'seq'}, dimensions={0}, use_global_device_ids=true | all-gather | bytes 294912 | tf_op jit(solution)/shard_map/all_gather | solution.py:167
  77.3 21.8 %all-gather.20.cloned.1.call-done = bf16[2048,512]{1,0:T(8,128)(2,1)} async-done(((bf16[256,512]{1,0:T(8,128)(2,1)}), bf16[2048,512]{1,0:T(8,128)(2,1)}) %all-gather.20.cloned.1.call-update) | async-done | bytes 2097168 | tf_op jit(solution)/shard_map/all_gather | solution.py:168
  113.6 19.1 %all-reduce = bf16[8]{0:T(256)(128)(2,1)S(1)} all-reduce(bf16[8]{0:T(256)(128)(2,1)S(1)} %dynamic-update-slice), channel_id=1, replica_groups=mesh['seq'=8,'tp'=4] {'seq'}, use_global_device_ids=true, to_apply=%add | all-reduce | flops 8 | bytes 32
  132.7 31.8 %all_gather.66 = bf16[2048,64]{0,1:T(8,128)(2,1)S(1)} all-gather(bf16[256,64]{0,1:T(8,128)(2,1)S(1)} %convert_element_type.351), channel_id=1, replica_groups=mesh['seq'=8,'tp'=4] {'seq'}, dimensions={0}, use_global_device_ids=true | all-gather | bytes 294912 | tf_op jit(solution)/shard_map/all_gather | solution.py:166
  169.8 31.0 %all-gather.5 = bf16[8,4,273]{2,1,0:T(4,128)(2,1)S(1)} all-gather(bf16[1,4,273]{2,1,0:T(4,128)(2,1)S(1)} %bitcast.210), channel_id=3, replica_groups=mesh['seq'=8,'tp'=4] {'seq'}, dimensions={0}, use_global_device_ids=true | all-gather | bytes 19656 | tf_op jit(solution)/shard_map/all_gather | solution.py:19
  242.3 38.0 %all-gather.6 = bf16[8,1,256]{2,1,0:T(2,128)(2,1)S(1)} all-gather(bf16[1,1,256]{2,1,0:T(2,128)(2,1)S(1)} %reshape.350), channel_id=1, replica_groups=mesh['seq'=8,'tp'=4] {'seq'}, dimensions={0}, use_global_device_ids=true | all-gather | bytes 4608 | tf_op jit(solution)/shard_map/all_gather | solution.py:170
  280.4 62.0 %all-gather.28.cloned.1.call-done = bf16[1376,2048]{1,0:T(8,128)(2,1)} async-done(((bf16[1376,256]{1,0:T(8,128)(2,1)}), bf16[1376,2048]{1,0:T(8,128)(2,1)}) %all-gather.28.cloned.1.call-update) | async-done | bytes 5636112 | tf_op jit(solution)/shard_map/all_gather | solution.py:173
  352.8 75.6 %all-reduce.8.cloned.1.call-done = bf16[1024,2048]{1,0:T(8,128)(2,1)} async-done(((bf16[1024,2048]{1,0:T(8,128)(2,1)}), bf16[1024,2048]{1,0:T(8,128)(2,1)}) %all-reduce.8.cloned.1.call-update) | async-done | bytes 4194320 | tf_op jit(solution)/shard_map/psum | solution.py:250
  442.8 80.6 %all-gather.24.cloned.1.call-done = bf16[2048,1376]{0,1:T(8,128)(2,1)} async-done(((bf16[256,1376]{0,1:T(8,128)(2,1)}), bf16[2048,1376]{0,1:T(8,128)(2,1)}) %all-gather.24.cloned.1.call-update) | async-done | bytes 5636112 | tf_op jit(solution)/shard_map/all_gather | solution.py:171
  534.3 82.2 %all-gather.26.cloned.1.call-done = bf16[2048,1376]{0,1:T(8,128)(2,1)} async-done(((bf16[256,1376]{0,1:T(8,128)(2,1)}), bf16[2048,1376]{0,1:T(8,128)(2,1)}) %all-gather.26.cloned.1.call-update) | async-done | bytes 5636112 | tf_op jit(solution)/shard_map/all_gather | solution.py:172
  616.5 14.0 fusion.3
  637.3 12.4 add_convert_fusion
  649.7 83.8 %all-reduce.10.cloned.1.call-done = bf16[1024,2048]{1,0:T(8,128)(2,1)} async-done(((bf16[1024,2048]{1,0:T(8,128)(2,1)}), bf16[1024,2048]{1,0:T(8,128)(2,1)}) %all-reduce.10.cloned.1.call-update) | async-done | bytes 4194320 | tf_op jit(solution)/shard_map/psum | solution.py:284
  794.6 30.7 %all-gather.7 = bf16[8,4,273]{2,1,0:T(4,128)(2,1)S(1)} all-gather(bf16[1,4,273]{2,1,0:T(4,128)(2,1)S(1)} %bitcast.211), channel_id=5, replica_groups=mesh['seq'=8,'tp'=4] {'seq'}, dimensions={0}, use_global_device_ids=true | all-gather | bytes 19656 | tf_op jit(solution)/shard_map/all_gather | solution.py:43
  826.1 21.8 %while.31 = (s32[]{:T(128)}, f32[4,273,128]{2,1,0:T(8,128)S(1)}, f32[4,273]{1,0:T(4,128)S(1)}, s32[]{:T(128)}, bf16[8,4,273,128]{3,2,1,0:T(8,128)(2,1)}, /*index...) while((s32[]{:T(128)}, f32[4,273,128]{2,1,0:T(8,128)S(1)}, ...), condition=%wide.region_20.21_spmd, body=%wide.region_19.20_spmd.sunk | while | flops 422611 | bytes 1408869 | solution.py:60
  950.5 17.4 %all-reduce.4 = (bf16[2048]{0:T(1024)(128)(2,1)S(1)}, bf16[2048]{0:T(1024)(128)(2,1)S(1)}) all-reduce(bf16[2048]{0:T(1024)(128)(2,1)S(1)} %get-tuple-element.192, bf16[2048]{0:T(1024)(128)(2,1)S(1)} %get-tuple-element.191), channel_id=9, replica_groups=mesh['seq'=8,'tp'=4] {'seq'}, use_global_device_ids=true, to_apply=%region_28.29.clone | all-reduce | flops 4096 | bytes 16384
  970.3 37.9 %reduce-scatter.16.cloned.1.call-done = bf16[256,64]{0,1:T(8,128)(2,1)} async-done(((bf16[2048,64]{0,1:T(8,128)(2,1)}), bf16[256,64]{0,1:T(8,128)(2,1)}) %reduce-scatter.16.cloned.1.call-update) | async-done | bytes 32784 | tf_op jit(solution)/shard_map/reduce_scatter | solution.py:392
  1009.6 44.5 %reduce-scatter.10.cloned.1.call-done = bf16[256,2048]{1,0:T(8,128)(2,1)} async-done(((bf16[1024,2048]{1,0:T(8,128)(2,1)}), bf16[256,2048]{1,0:T(8,128)(2,1)}) %reduce-scatter.10.cloned.1.call-update) | async-done | bytes 1048592 | tf_op jit(solution)/shard_map/reduce_scatter | solution.py:262
  1057.4 69.1 %reduce-scatter.18.cloned.1.call-done = bf16[256,512]{1,0:T(8,128)(2,1)} async-done(((bf16[2048,512]{1,0:T(8,128)(2,1)}), bf16[256,512]{1,0:T(8,128)(2,1)}) %reduce-scatter.18.cloned.1.call-update) | async-done | bytes 262160 | tf_op jit(solution)/shard_map/reduce_scatter | solution.py:395
  1128.3 109.7 %reduce-scatter.22.cloned.1.call-done = bf16[256,1376]{0,1:T(8,128)(2,1)} async-done(((bf16[2048,1376]{0,1:T(8,128)(2,1)}), bf16[256,1376]{0,1:T(8,128)(2,1)}) %reduce-scatter.22.cloned.1.call-update) | async-done | bytes 704528 | tf_op jit(solution)/shard_map/reduce_scatter | solution.py:404
  1240.2 109.9 %reduce-scatter.24.cloned.1.call-done = bf16[256,1376]{0,1:T(8,128)(2,1)} async-done(((bf16[2048,1376]{0,1:T(8,128)(2,1)}), bf16[256,1376]{0,1:T(8,128)(2,1)}) %reduce-scatter.24.cloned.1.call-update) | async-done | bytes 704528 | tf_op jit(solution)/shard_map/reduce_scatter | solution.py:407
  1352.5 110.1 %reduce-scatter.26.cloned.1.call-done = bf16[1376,256]{1,0:T(8,128)(2,1)} async-done(((bf16[1376,2048]{1,0:T(8,128)(2,1)}), bf16[1376,256]{1,0:T(8,128)(2,1)}) %reduce-scatter.26.cloned.1.call-update) | async-done | bytes 704528 | tf_op jit(solution)/shard_map/reduce_scatter | solution.py:410
  1464.8 44.5 %reduce-scatter.12.cloned.1.call-done = bf16[256,2048]{1,0:T(8,128)(2,1)} async-done(((bf16[1024,2048]{1,0:T(8,128)(2,1)}), bf16[256,2048]{1,0:T(8,128)(2,1)}) %reduce-scatter.12.cloned.1.call-update) | async-done | bytes 1048592 | tf_op jit(solution)/shard_map/reduce_scatter | solution.py:373
  (312 shorter events, 326.3 us)
Async XLA Ops:
  7.2 60.1 %all-gather.18.cloned.1.call-start = ((), (), s32[]{:S(2)}) async-start(), calls=%async_computation.9 | async-start | bytes 5242880 | tf_op jit(solution)/shard_map/all_gather | solution.py:188
  7.9 91.1 %all-gather.20.cloned.1.call-start = ((), (), s32[]{:S(2)}) async-start(), calls=%async_computation.10 | async-start | bytes 2359296 | tf_op jit(solution)/shard_map/all_gather | solution.py:168
  9.8 207.2 %all-gather.32.cloned.1.call-start = ((), (), s32[]{:S(2)}) async-start(), calls=%async_computation.27 | async-start | bytes 2580480 | tf_op jit(solution)/shard_map/all_gather | solution.py:19
  32.7 168.1 %copy-start.35 = (f32[8,1,256]{2,1,0:T(1,128)}, f32[8,1,256]{2,1,0:T(1,128)S(1)}, u32[]{:S(2)}) copy-start(f32[8,1,256]{2,1,0:T(1,128)S(1)} %convert_element_type.431) | copy-start | bytes 24580
  34.4 716.6 %copy-start.43 = (f32[273]{0:T(512)}, f32[273]{0:T(512)S(1)}, u32[]{:S(2)}) copy-start(f32[273]{0:T(512)S(1)} %pad.9.clone) | copy-start | bytes 3280
  67.2 98.0 %copy-start.41 = (f32[1024]{0:T(1024)}, f32[1024]{0:T(1024)S(1)}, u32[]{:S(2)}) copy-start(f32[1024]{0:T(1024)S(1)} %compare_convert_fusion.2) | copy-start | bytes 12292
  70.4 130.5 %copy-start.46 = (f32[1024]{0:T(1024)}, f32[1024]{0:T(1024)S(1)}, u32[]{:S(2)}) copy-start(f32[1024]{0:T(1024)S(1)} %add_rsqrt_fusion.1) | copy-start | bytes 12292
  108.1 122.9 %all-gather.22.cloned.1.call-start = ((), (), s32[]{:S(2)}) async-start(), calls=%async_computation.11 | async-start | bytes 2359296 | tf_op jit(solution)/shard_map/all_gather | solution.py:169
  110.0 170.4 %all-gather.30.cloned.1.call-start = ((), (), s32[]{:S(2)}) async-start(), calls=%async_computation.17 | async-start | bytes 5242880 | tf_op jit(solution)/shard_map/all_gather | solution.py:269
  110.5 231.8 %all-gather.28.cloned.1.call-start = ((), (), s32[]{:S(2)}) async-start(), calls=%async_computation.15 | async-start | bytes 6340608 | tf_op jit(solution)/shard_map/all_gather | solution.py:173
  111.6 316.9 %all-reduce.8.cloned.1.call-start = ((), (), s32[]{:S(2)}) async-start(), calls=%async_computation.12 | async-start | bytes 8388608 | tf_op jit(solution)/shard_map/psum | solution.py:250
  237.5 285.9 %all-gather.24.cloned.1.call-start = ((), (), s32[]{:S(2)}) async-start(), calls=%async_computation.13 | async-start | bytes 6340608 | tf_op jit(solution)/shard_map/all_gather | solution.py:171
  239.9 376.6 %all-gather.26.cloned.1.call-start = ((), (), s32[]{:S(2)}) async-start(), calls=%async_computation.14 | async-start | bytes 6340608 | tf_op jit(solution)/shard_map/all_gather | solution.py:172
  242.2 491.3 %all-reduce.10.cloned.1.call-start = ((), (), s32[]{:S(2)}) async-start(), calls=%async_computation.18 | async-start | bytes 8388608 | tf_op jit(solution)/shard_map/psum | solution.py:284
  649.7 176.3 %all-gather.34.cloned.1.call-start = ((), (), s32[]{:S(2)}) async-start(), calls=%async_computation.28 | async-start | bytes 2580480 | tf_op jit(solution)/shard_map/all_gather | solution.py:43
  757.1 180.5 %reduce-scatter.14.cloned.1.call-start = ((), (), s32[]{:S(2)}) async-start(), calls=%async_computation.20 | async-start | bytes 294912 | tf_op jit(solution)/shard_map/reduce_scatter | solution.py:389
  780.6 188.0 %reduce-scatter.20.cloned.1.call-start = ((), (), s32[]{:S(2)}) async-start(), calls=%async_computation.23 | async-start | bytes 2359296 | tf_op jit(solution)/shard_map/reduce_scatter | solution.py:398
  788.1 220.2 %reduce-scatter.16.cloned.1.call-start = ((), (), s32[]{:S(2)}) async-start(), calls=%async_computation.21 | async-start | bytes 294912 | tf_op jit(solution)/shard_map/reduce_scatter | solution.py:392
  857.6 196.6 %reduce-scatter.10.cloned.1.call-start = ((), (), s32[]{:S(2)}) async-start(), calls=%async_computation.16 | async-start | bytes 5242880 | tf_op jit(solution)/shard_map/reduce_scatter | solution.py:262
  868.7 257.8 %reduce-scatter.18.cloned.1.call-start = ((), (), s32[]{:S(2)}) async-start(), calls=%async_computation.22 | async-start | bytes 2359296 | tf_op jit(solution)/shard_map/reduce_scatter | solution.py:395
  888.0 350.0 %reduce-scatter.22.cloned.1.call-start = ((), (), s32[]{:S(2)}) async-start(), calls=%async_computation.24 | async-start | bytes 6340608 | tf_op jit(solution)/shard_map/reduce_scatter | solution.py:404
  898.3 451.9 %reduce-scatter.24.cloned.1.call-start = ((), (), s32[]{:S(2)}) async-start(), calls=%async_computation.25 | async-start | bytes 6340608 | tf_op jit(solution)/shard_map/reduce_scatter | solution.py:407
  909.9 552.7 %reduce-scatter.26.cloned.1.call-start = ((), (), s32[]{:S(2)}) async-start(), calls=%async_computation.26 | async-start | bytes 6340608 | tf_op jit(solution)/shard_map/reduce_scatter | solution.py:410
  920.2 589.2 %reduce-scatter.12.cloned.1.call-start = ((), (), s32[]{:S(2)}) async-start(), calls=%async_computation.19 | async-start | bytes 5242880 | tf_op jit(solution)/shard_map/reduce_scatter | solution.py:373
  (59 other events, 647.3 us)
Sparse Core Ops, SparseCore 0:
  9.6 37.1 all-gather.17
  49.5 49.5 all-gather.19
  108.2 53.4 all-gather.31
  164.2 49.4 all-gather.21
  215.1 32.6 all-gather.29
  250.3 92.0 all-gather.27
  344.7 83.6 all-reduce.7
  431.2 92.1 all-gather.23
  526.2 90.1 all-gather.25
  649.8 83.6 all-reduce.9
  757.3 51.4 all-gather.33
  812.6 60.2 reduce-scatter.13
  876.4 67.3 reduce-scatter.19
  947.6 60.6 reduce-scatter.15
  1010.6 43.5 reduce-scatter.9
  1058.6 67.8 reduce-scatter.17
  1130.4 107.4 reduce-scatter.21
  1241.9 108.2 reduce-scatter.23
  1354.3 108.2 reduce-scatter.25
  1465.1 44.2 reduce-scatter.11
where the time goes:
time: 1530 us; the launch traced here: 1520 us
  waiting for transfers between devices  933 us (61%)
  blocking collectives  232 us (15%)
  matrix products  214 us (14%)
  other arithmetic  108 us (7%)
  between operations  16.8 us (1%)
  local copies, waits for them, and re-layouts  16.5 us (1%)
    reduce_scatter x1, waiting for transfers between devices, on_device(): lax.psum_scatter(grad_down.astype(jnp.bfloat16), 'seq', scatter_dimension...  110 us
    reduce_scatter x1, waiting for transfers between devices, on_device(): lax.psum_scatter(grad_up_w.astype(jnp.bfloat16), 'seq', scatter_dimension...  110 us
    reduce_scatter x1, waiting for transfers between devices, on_device(): lax.psum_scatter(grad_gate_w.astype(jnp.bfloat16), 'seq', scatter_dimensi...  110 us
    psum x1, waiting for transfers between devices, on_device(): lax.psum(hidden_partial.astype(jnp.bfloat16), 'tp').astype(jnp.float32)  83.8 us
    all_gather x1, waiting for transfers between devices, on_device(): lax.all_gather(lowered[7], 'seq', axis=0, tiled=True)  82.2 us
    all_gather x1, waiting for transfers between devices, on_device(): lax.all_gather(lowered[6], 'seq', axis=0, tiled=True)  80.6 us
    psum x1, waiting for transfers between devices, on_device(): lax.psum(attn_partial.astype(jnp.bfloat16), 'tp').astype(jnp.float32)  75.6 us
    reduce_scatter x1, waiting for transfers between devices, on_device(): lax.psum_scatter(grad_value_w.astype(jnp.bfloat16), 'seq', scatter_dimens...  69.1 us
  transfers between devices with their start and end apart: 20, of which 13 were waited for; matrix products, arithmetic and copies ran while one was open for 17% of the time, Pallas kernels for 0%

commit v1 on v0

v1 whole, which is shorter than its diff:
```python
import jax
import jax.numpy as jnp
from jax import lax
from jax.sharding import PartitionSpec as P

FEAT = 16
VHEAD = 128


epsilon = 1e-05
linear_coef = 0.5
square_coef = 0.17677669529663687
highest = lax.Precision.HIGHEST
f32 = jnp.float32
bf16 = jnp.bfloat16


def ring_order(count):
    planes = 4 if count % 4 == 0 else 2
    columns = count // planes
    order = [z * columns for z in range(planes)]
    for z in reversed(range(planes)):
        xs = list(range(1, columns))
        if (planes - 1 - z) % 2:
            xs.reverse()
        order += [z * columns + x for x in xs]
    return order


def relative_list(count):
    half = count // 2
    out = []
    for j in range(1, half):
        out += [j, count - j]
    return out + [half, 0]


def ring_perms(count):
    ring = ring_order(count)
    fwd = [(ring[i], ring[(i + 1) % count]) for i in range(count)]
    return fwd, [(b, a) for a, b in fwd]


def ring_gather(own, half_rows):
    count = lax.axis_size("seq")
    fwd, bwd = ring_perms(count)
    half = count // 2
    got = {0: own}
    ahead = back = own
    for step in range(1, half):
        ahead = lax.ppermute(ahead, "seq", fwd)
        back = lax.ppermute(back, "seq", bwd)
        got[step] = ahead
        got[count - step] = back
    ahead = lax.ppermute(ahead[:half_rows], "seq", fwd)
    back = lax.ppermute(back[half_rows:], "seq", bwd)
    got[half] = jnp.concatenate([ahead, back], axis=0)
    return got


def ring_scatter(chunks):
    count = lax.axis_size("seq")
    fwd, bwd = ring_perms(count)
    half = chunks[0].shape[0] // 2
    ahead = chunks[1][:half]
    back = chunks[count - 1][half:]
    for step in range(count - 1):
        ahead = lax.ppermute(ahead, "seq", fwd).astype(f32)
        back = lax.ppermute(back, "seq", bwd).astype(f32)
        last = step == count - 2
        ahead = ahead + chunks[0 if last else 2 + step][:half].astype(f32)
        back = back + chunks[0 if last else count - 2 - step][half:].astype(f32)
        if not last:
            ahead = ahead.astype(bf16)
            back = back.astype(bf16)
    return jnp.concatenate([ahead, back], axis=0)


def to_relative(array, index_row, chunk):
    return jnp.concatenate(
        [lax.dynamic_slice_in_dim(array, i * chunk, chunk, 1) for i in index_row], axis=1
    )


def tp_perms(count):
    ys = count // 2
    core = [(i, i ^ 1) for i in range(count)]
    shift = [
        [(i, (((i // 2) + d) % ys) * 2 + i % 2) for i in range(count)] for d in range(ys)
    ]
    return core, shift


def tp_gather(own):
    count = lax.axis_size("tp")
    ys = count // 2
    place = lax.axis_index("tp")
    y, c = place // 2, place % 2
    core, shift = tp_perms(count)
    parts = [own] + [lax.ppermute(own, "tp", shift[d]) for d in range(1, ys)]
    mine = jnp.stack([lax.select_n((y - at + ys) % ys, *parts) for at in range(ys)])
    other = lax.ppermute(mine, "tp", core)
    full = jnp.stack([jnp.where(c == 0, mine, other), jnp.where(c == 0, other, mine)], axis=1)
    return full.reshape((count * own.shape[0],) + own.shape[1:])


def tp_scatter(partial):
    count = lax.axis_size("tp")
    ys = count // 2
    place = lax.axis_index("tp")
    y, c = place // 2, place % 2
    core, shift = tp_perms(count)
    blocks = partial.reshape((ys, 2, partial.shape[0] // count) + partial.shape[1:])
    sent = lax.dynamic_index_in_dim(blocks, 1 - c, 1, False)
    kept = lax.dynamic_index_in_dim(blocks, c, 1, False)
    pair = kept.astype(f32) + lax.ppermute(sent, "tp", core).astype(f32)
    low = pair.astype(bf16)
    own = lax.dynamic_index_in_dim(pair, y, 0, False)
    for d in range(1, ys):
        away = lax.dynamic_index_in_dim(low, (y + d) % ys, 0, False)
        own = own + lax.ppermute(away, "tp", shift[d]).astype(f32)
    return own


def tp_sum(vector):
    count = lax.axis_size("tp")
    core, shift = tp_perms(count)
    vector = vector + lax.ppermute(vector, "tp", core)
    return vector + sum(lax.ppermute(vector, "tp", shift[d]) for d in range(1, count // 2))


def carried(arrays, resets, step):
    count = lax.axis_size("seq")
    place = lax.axis_index("seq")

    def from_near(a, d):
        perm = [(i, i + d * step) for i in range(count) if 0 <= i + d * step < count]
        return lax.ppermute(a.astype(bf16), "seq", perm).astype(f32)

    def reset_within(d):
        at = jnp.arange(count)
        away = (place - at) * step
        return jnp.sum(jnp.where((away >= 1) & (away <= d), resets, 0)) > 0

    arrays = [from_near(a, 1) for a in arrays]
    d = 1
    while d < count - 1:
        keep = 1.0 - reset_within(d).astype(f32)
        arrays = [a + keep * from_near(a, d) for a in arrays]
        d *= 2
    return arrays


def features(vector):
    squares = (vector[..., :, None] * vector[..., None, :]).reshape(
        vector.shape[:-1] + (vector.shape[-1] * vector.shape[-1],)
    )
    return jnp.concatenate(
        [jnp.ones_like(vector[..., :1]), vector * linear_coef, squares * square_coef], axis=-1
    )


def feature_grad(vector, grad_feat):
    feat_width = vector.shape[-1]
    linear_part = grad_feat[..., 1 : 1 + feat_width]
    square_part = grad_feat[..., 1 + feat_width :].reshape(vector.shape + (feat_width,))
    mixed_part = jnp.sum(square_part * vector[..., None, :], axis=-1) + jnp.sum(
        square_part * vector[..., :, None], axis=-2
    )
    return linear_coef * linear_part + square_coef * mixed_part


def segment_masks(anchor, starts, length):
    positions = anchor + jnp.arange(length, dtype=jnp.int32)
    start_le = starts[None, :] <= positions[:, None]
    row_ids = jnp.sum(start_le.astype(jnp.int32), axis=1)
    inside = (starts >= anchor) & (starts < anchor + length)
    carry = jnp.sum(((starts[None, :] >= anchor) & start_le).astype(jnp.int32), axis=1) == 0
    after_last = (
        jnp.sum(
            ((starts[None, :] > positions[:, None]) & inside[None, :]).astype(jnp.int32), axis=1
        )
        == 0
    )
    return (positions, row_ids, carry, after_last)


def rms_scale(values):
    return lax.rsqrt(jnp.mean(values * values, axis=-1, keepdims=True) + epsilon)


def norm_back(grad_out, normed, scale, gain):
    grad_normed = grad_out * gain
    return scale * (grad_normed - normed * jnp.mean(grad_normed * normed, axis=-1, keepdims=True))


def pair_block(query_part, key_heads, row_ids, positions, first_row, span_rows):
    scores = (
        jnp.einsum("thf,shf->hts", query_part, key_heads, preferred_element_type=f32) * 0.25
    )
    rows_here = row_ids[first_row : first_row + span_rows]
    place_here = positions[first_row : first_row + span_rows]
    allowed = (
        (rows_here[:, None] == row_ids[None, :]) & (positions[None, :] <= place_here[:, None])
    ).astype(f32)
    kernel = (1.0 + scores + 0.5 * scores * scores) * allowed[None]
    return (scores, allowed, kernel)


def dot(a, b):
    return jnp.dot(a, b, preferred_element_type=f32)


def dot_t(a, b):
    return lax.dot_general(a, b, (((1,), (1,)), ((), ())), preferred_element_type=f32)


def dot_tt(a, b):
    return lax.dot_general(a, b, (((0,), (0,)), ((), ())), preferred_element_type=f32)


def on_device(
    inputs,
    lengths,
    gain_attn,
    w_query,
    w_key,
    w_value,
    w_out,
    gain_mlp,
    w_gate,
    w_up,
    w_down,
    cotangent,
):
    seq_count = lax.axis_size("seq")
    tp_count = lax.axis_size("tp")
    seq_index = lax.axis_index("seq")
    rows_own, width = inputs.shape
    chunk = width // seq_count
    half = chunk // 2
    block_len = rows_own * tp_count
    anchor = seq_index * block_len
    relative = relative_list(seq_count)
    ring = ring_order(seq_count)
    place_of = [ring.index(s) for s in range(seq_count)]
    to_rel = jnp.array(
        [[ring[(place_of[s] - k) % seq_count] for k in relative] for s in range(seq_count)],
        jnp.int32,
    )[seq_index]
    to_abs = jnp.array(
        [
            [relative.index((place_of[s] - place_of[o]) % seq_count) for o in range(seq_count)]
            for s in range(seq_count)
        ],
        jnp.int32,
    )[seq_index]
    to_rel = [to_rel[j] for j in range(seq_count)]
    to_abs = [to_abs[j] for j in range(seq_count)]

    qk_cols, v_cols, ff_cols = w_query.shape[1], w_value.shape[1], w_gate.shape[1]
    gains = jnp.stack([gain_attn, gain_mlp]).astype(bf16)
    qkv_cols = 2 * qk_cols + v_cols
    qkv_own = jnp.concatenate([w_query, w_key, w_value], axis=1).astype(bf16)
    gain_rows = jnp.zeros((16, qkv_cols), bf16).at[:2, :chunk].set(gains)
    first_own = jnp.concatenate([qkv_own, gain_rows], axis=0)
    out_own = w_out.astype(bf16).T
    gate_up_own = jnp.concatenate([w_gate, w_up], axis=1).astype(bf16)
    down_own = w_down.astype(bf16).T

    first_got = ring_gather(first_own, half)
    out_got = ring_gather(out_own, half)
    gate_up_got = ring_gather(gate_up_own, half)
    down_got = ring_gather(down_own, half)
    w_qkv = jnp.concatenate([first_got[k][:chunk] for k in relative], axis=0)
    gain_first = jnp.concatenate([first_got[k][chunk, :chunk] for k in relative]).astype(f32)
    gain_second = jnp.concatenate([first_got[k][chunk + 1, :chunk] for k in relative]).astype(f32)
    w_out_t = jnp.concatenate([out_got[k] for k in relative], axis=0)
    w_gate_up = jnp.concatenate([gate_up_got[k] for k in relative], axis=0)
    w_down_t = jnp.concatenate([down_got[k] for k in relative], axis=0)

    at = jnp.arange(lengths.shape[0])
    starts = jnp.sum(jnp.where(at[None, :] < at[:, None], lengths[None, :], 0), axis=1)
    positions, row_ids, carry_in, after_last = segment_masks(anchor, starts, block_len)
    carry_mask = carry_in.astype(f32)
    last_mask = after_last.astype(f32)
    resets = (
        jnp.sum(
            ((starts // block_len)[None, :] == jnp.arange(seq_count)[:, None]).astype(jnp.int32),
            axis=1,
        )
        > 0
    ).astype(jnp.int32)

    inputs_own = to_relative(inputs, to_rel, chunk)
    grad_own = to_relative(cotangent, to_rel, chunk)
    inputs_full = tp_gather(inputs_own).astype(f32)
    grad_full = tp_gather(grad_own)
    inputs_own = inputs_own.astype(f32)
    hidden_first = (inputs_full * rms_scale(inputs_full) * gain_first).astype(bf16)
    qkv = dot(hidden_first, w_qkv).astype(bf16)
    queries = qkv[:, :qk_cols]
    key_flat = qkv[:, qk_cols : 2 * qk_cols]
    value_flat = qkv[:, 2 * qk_cols :]
    heads_local = qk_cols // FEAT
    query_heads = queries.reshape(block_len, heads_local, FEAT)
    key_heads = key_flat.reshape(block_len, heads_local, FEAT)
    value_heads = value_flat.reshape(block_len, heads_local, VHEAD)
    query_float = query_heads.astype(f32)
    key_float = key_heads.astype(f32)
    value_float = value_heads.astype(f32)
    key_feat = features(key_float) * last_mask[:, None, None]
    local_state = jnp.einsum("thn,thv->hnv", key_feat, value_float, precision=highest)
    local_sum = jnp.sum(key_feat, axis=0)
    carry_state, carry_sum = carried([local_state, local_sum], resets, 1)
    step_rows = 512
    query_feat = features(query_float)
    carry_weight = carry_mask[:, None]
    numer_parts = []
    denom_parts = []
    for first_row in range(0, block_len, step_rows):
        query_part = query_heads[first_row : first_row + step_rows]
        scores, allowed, kernel = pair_block(
            query_part, key_heads, row_ids, positions, first_row, step_rows
        )
        numer_parts.append(
            jnp.einsum("hts,shv->thv", kernel.astype(bf16), value_heads, preferred_element_type=f32)
        )
        denom_parts.append(jnp.sum(kernel, axis=-1).T)
    numerator = (
        jnp.concatenate(numer_parts, axis=0)
        + jnp.einsum("thn,hnv->thv", query_feat, carry_state, precision=highest)
        * carry_weight[:, :, None]
    )
    denominator = (
        jnp.concatenate(denom_parts, axis=0)
        + jnp.einsum("thn,hn->th", query_feat, carry_sum, precision=highest) * carry_weight
    )
    attended = numerator / denominator[:, :, None]
    attended_low = attended.reshape(block_len, heads_local * VHEAD).astype(bf16)
    attn_partial = dot_t(attended_low, w_out_t).astype(bf16)
    middle_own = inputs_own + tp_scatter(attn_partial)
    scale_second = rms_scale(middle_own)
    normed_second = middle_own * scale_second
    hidden_second = tp_gather((normed_second * gain_second).astype(bf16))
    gate_up = dot(hidden_second, w_gate_up)
    gate_value, upward = gate_up[:, :ff_cols], gate_up[:, ff_cols:]
    sigmoid_gate = jax.nn.sigmoid(gate_value)
    silu_gate = gate_value * sigmoid_gate
    mixed_rows = (silu_gate * upward).astype(bf16)
    grad_down_t = dot_tt(grad_full, mixed_rows).astype(bf16)

    def by_distance(stack):
        return {k: stack[j * chunk : (j + 1) * chunk] for j, k in enumerate(relative)}

    sum_down_t = ring_scatter(by_distance(grad_down_t))
    mlp_own = tp_scatter(dot_t(mixed_rows, w_down_t).astype(bf16))
    block_output = to_relative((middle_own + mlp_own).astype(bf16), to_abs, chunk)

    grad_mixed = dot(grad_full, w_down_t).astype(bf16).astype(f32)
    grad_gate = (
        grad_mixed * upward * sigmoid_gate * (1.0 + gate_value * (1.0 - sigmoid_gate))
    ).astype(bf16)
    grad_upward = (grad_mixed * silu_gate).astype(bf16)
    grad_gate_up = jnp.concatenate([grad_gate, grad_upward], axis=1)
    hidden_partial = dot_t(grad_gate_up, w_gate_up).astype(bf16)
    sum_gate_up = ring_scatter(by_distance(dot_tt(hidden_second, grad_gate_up).astype(bf16)))
    grad_hidden = tp_scatter(hidden_partial)
    grad_middle = grad_own.astype(f32) + norm_back(
        grad_hidden, normed_second, scale_second, gain_second
    )
    grad_branch = tp_gather(grad_middle.astype(bf16))
    sum_out_t = ring_scatter(by_distance(dot_tt(grad_branch, attended_low).astype(bf16)))
    grad_attended = dot(grad_branch, w_out_t).reshape(block_len, heads_local, VHEAD)
    grad_numer = (grad_attended / denominator[:, :, None]).astype(bf16)
    grad_denom = -jnp.sum(grad_attended * attended, axis=-1) / denominator
    grad_numer_carried = grad_numer.astype(f32) * carry_weight[:, :, None]
    grad_denom_carried = grad_denom * carry_weight
    grad_state_in = jnp.einsum("thn,thv->hnv", query_feat, grad_numer_carried, precision=highest)
    grad_sum_in = jnp.einsum("thn,th->hn", query_feat, grad_denom_carried, precision=highest)
    grad_query_feat = (
        jnp.einsum("thv,hnv->thn", grad_numer_carried, carry_state, precision=highest)
        + grad_denom_carried[:, :, None] * carry_sum[None]
    )
    grad_state_out, grad_sum_out = carried([grad_state_in, grad_sum_in], resets, -1)
    grad_key_feat = (
        jnp.einsum("thv,hnv->thn", value_float, grad_state_out, precision=highest)
        + grad_sum_out[None]
    ) * last_mask[:, None, None]
    grad_value_state = jnp.einsum("thn,hnv->thv", key_feat, grad_state_out, precision=highest)
    grad_query_parts = []
    grad_key_inner = jnp.zeros((block_len, heads_local, FEAT), f32)
    grad_value_inner = jnp.zeros((block_len, heads_local, VHEAD), f32)
    for first_row in range(0, block_len, step_rows):
        query_part = query_heads[first_row : first_row + step_rows]
        scores, allowed, kernel = pair_block(
            query_part, key_heads, row_ids, positions, first_row, step_rows
        )
        numer_grad_part = grad_numer[first_row : first_row + step_rows]
        grad_weights = jnp.einsum(
            "thv,shv->hts", numer_grad_part, value_heads, preferred_element_type=f32
        )
        grad_scores = (
            (grad_weights + grad_denom[first_row : first_row + step_rows].T[:, :, None])
            * allowed[None]
            * (1.0 + scores)
        ).astype(bf16)
        grad_query_parts.append(
            jnp.einsum("hts,shf->thf", grad_scores, key_heads, preferred_element_type=f32) * 0.25
        )
        grad_key_inner = (
            grad_key_inner
            + jnp.einsum("hts,thf->shf", grad_scores, query_part, preferred_element_type=f32) * 0.25
        )
        grad_value_inner = grad_value_inner + jnp.einsum(
            "hts,thv->shv", kernel.astype(bf16), numer_grad_part, preferred_element_type=f32
        )
    grad_query = (
        jnp.concatenate(grad_query_parts, axis=0) + feature_grad(query_float, grad_query_feat)
    ).astype(bf16)
    grad_key = (grad_key_inner + feature_grad(key_float, grad_key_feat)).astype(bf16)
    grad_value = (grad_value_inner + grad_value_state).astype(bf16)
    grad_qkv = jnp.concatenate(
        [
            grad_query.reshape(block_len, heads_local * FEAT),
            grad_key.reshape(block_len, heads_local * FEAT),
            grad_value.reshape(block_len, heads_local * VHEAD),
        ],
        axis=1,
    )
    sum_qkv = ring_scatter(by_distance(dot_tt(hidden_first, grad_qkv).astype(bf16)))
    grad_hidden_first = tp_scatter(dot_t(grad_qkv, w_qkv).astype(bf16))
    scale_first = rms_scale(inputs_own)
    normed_first = inputs_own * scale_first
    grad_input = to_relative(
        grad_middle + norm_back(grad_hidden_first, normed_first, scale_first, gain_first),
        to_abs,
        chunk,
    )

    gain_terms = jnp.stack(
        [
            jnp.sum(qkv_own.astype(f32) * sum_qkv, axis=1),
            jnp.sum(gate_up_own.astype(f32) * sum_gate_up, axis=1),
        ]
    )
    gain_sums = tp_sum(gain_terms) / gains.astype(f32)
    return (
        block_output,
        grad_input,
        gain_sums[0],
        sum_qkv[:, :qk_cols],
        sum_qkv[:, qk_cols : 2 * qk_cols],
        sum_qkv[:, 2 * qk_cols :],
        sum_out_t.T,
        gain_sums[1],
        sum_gate_up[:, :ff_cols],
        sum_gate_up[:, ff_cols:],
        sum_down_t.T,
    )


def solution(mesh):
    in_specs = (
        P(("seq", "tp"), None),
        P(),
        P("seq"),
        P("seq", "tp"),
        P("seq", "tp"),
        P("seq", "tp"),
        P("tp", "seq"),
        P("seq"),
        P("seq", "tp"),
        P("seq", "tp"),
        P("tp", "seq"),
        P(("seq", "tp"), None),
    )
    out_specs = (
        P(("seq", "tp"), None),
        P(("seq", "tp"), None),
        P("seq"),
        P("seq", "tp"),
        P("seq", "tp"),
        P("seq", "tp"),
        P("tp", "seq"),
        P("seq"),
        P("seq", "tp"),
        P("seq", "tp"),
        P("tp", "seq"),
    )
    return jax.shard_map(
        on_device, mesh=mesh, in_specs=in_specs, out_specs=out_specs, check_vma=False
    )
```

time: 1530 us -> 841 us (0.55)
  waiting for transfers between devices: 933 us -> 308 us
  blocking collectives: 232 us -> 0 us
  starting transfers between devices: 1.41 us -> 167 us
  local copies, waits for them, and re-layouts: 16.5 us -> 85.7 us
  matrix products: 214 us -> 174 us
  other arithmetic: 108 us -> 80.7 us
    reduce_scatter x9 -> x0, waiting for transfers between devices: 526 us -> none  [the longest x1 110 us: on_device(): lax.psum_scatter(grad_down.astype(jnp.bfloat16), 'seq', scatter_dimension...]
    ppermute x0 -> x122, waiting for transfers between devices: none -> 308 us  [the longest x28 83.6 us: ring_scatter(): ahead = lax.ppermute(ahead, 'seq', fwd).astype(f32)]
    all_gather x9 -> x0, waiting for transfers between devices: 247 us -> none  [the longest x1 82.2 us: on_device(): lax.all_gather(lowered[7], 'seq', axis=0, tiled=True)]
    all_gather x6 -> x0, blocking collectives: 185 us -> none  [the longest x1 38 us: on_device(): lax.all_gather(lowered[5], 'seq', axis=0, tiled=True)]
    ppermute x0 -> x122, starting transfers between devices: none -> 167 us  [the longest x16 43.8 us: from_near(): return lax.ppermute(a.astype(bf16), 'seq', perm).astype(f32)]
    psum x2 -> x0, waiting for transfers between devices: 159 us -> none  [the longest x1 83.8 us: on_device(): lax.psum(hidden_partial.astype(jnp.bfloat16), 'tp').astype(jnp.float32)]
    unnamed x132 -> x286, local copies, waits for them, and re-layouts: 13.7 us -> 66.2 us
    unnamed x3 -> x0, blocking collectives: 47.2 us -> none
  transfers between devices with their start and end apart: 20 -> 122, of which waited for: 13 -> 62; matrix products, arithmetic and copies ran while one was open for 17% -> 29% of each run, Pallas kernels for 0% -> 0%
where the time goes in v1:
time: 841 us; the launch traced here: 833 us
  waiting for transfers between devices  308 us (37%)
  matrix products  174 us (21%)
  starting transfers between devices  167 us (20%)
  local copies, waits for them, and re-layouts  85.7 us (10%)
  other arithmetic  80.7 us (10%)
  between operations  17.4 us (2%)
    ppermute x28, waiting for transfers between devices, ring_scatter(): ahead = lax.ppermute(ahead, 'seq', fwd).astype(f32)  83.6 us
    unnamed x286, local copies, waits for them, and re-layouts  66.2 us
    ppermute x12, waiting for transfers between devices, ring_gather(): back = lax.ppermute(back, 'seq', bwd)  63 us
    dot_general x4, matrix products, dot(): return jnp.dot(a, b, preferred_element_type=f32)  45.3 us
    ppermute x16, starting transfers between devices, from_near(): return lax.ppermute(a.astype(bf16), 'seq', perm).astype(f32)  43.8 us
    ppermute x28, starting transfers between devices, ring_scatter(): ahead = lax.ppermute(ahead, 'seq', fwd).astype(f32)  38.5 us
    dot_general x4, matrix products, dot_t(): lax.dot_general(a, b, (((1,), (1,)), ((), ())), preferred_element_type=f32)  37.8 us
    ppermute x16, waiting for transfers between devices, from_near(): return lax.ppermute(a.astype(bf16), 'seq', perm).astype(f32)  34.7 us
  transfers between devices with their start and end apart: 122, of which 62 were waited for; matrix products, arithmetic and copies ran while one was open for 29% of the time, Pallas kernels for 0%

profile of v1, /device:TPU:0, one launch (start us, length us, event | category | flops | bytes accessed | tf_op | source)
XLA Modules:
  0.0 832.8 jit_solution(3548493533408745136)
XLA Ops:
  61.9 10.2 %collective-permute-done.20 = bf16[256,512]{0,1:T(8,128)(2,1)} collective-permute-done((bf16[256,512]{0,1:T(8,128)(2,1)}, bf16[256,512]{0,1:T(8,128)(2,1)}, u32[]{:S(2)}, u32[]{:S(2)}) %collective-permute-start.20) | collective-permute-done | bytes 262176 | tf_op jit(solution)/shard_map/ppermute | solution.py:51
  99.0 15.3 %collective-permute-done.22 = bf16[256,512]{0,1:T(8,128)(2,1)} collective-permute-done((bf16[256,512]{0,1:T(8,128)(2,1)}, bf16[256,512]{0,1:T(8,128)(2,1)}, u32[]{:S(2)}, u32[]{:S(2)}) %collective-permute-start.22) | collective-permute-done | bytes 262176 | tf_op jit(solution)/shard_map/ppermute | solution.py:51
  122.9 8.8 %collective-permute-done.25 = bf16[128,512]{0,1:T(8,128)(2,1)S(1)} collective-permute-done((bf16[128,512]{0,1:T(8,128)(2,1)S(1)}, bf16[128,512]{0,1:T(8,128)(2,1)S(1)}, u32[]{:S(2)}, u32[]{:S(2)}) %collective-permute-start.25) | collective-permute-done | bytes 131104 | tf_op jit(solution)/shard_map/ppermute | solution.py:56
  134.7 7.0 collective-permute-done.7
  200.4 6.4 collective-permute-start.12
  214.2 6.5 collective-permute-start.13
  246.3 7.0 collective-permute-start.42
  262.6 7.1 collective-permute-done.42
  279.9 27.1 %collective-permute-done.44 = bf16[128,1376]{0,1:T(8,128)(2,1)S(1)} collective-permute-done((bf16[128,1376]{0,1:T(8,128)(2,1)S(1)}, bf16[128,1376]{0,1:T(8,128)(2,1)S(1)}, u32[]{:S(2)}, u32[]{:S(2)}) %collective-permute-start.44) | collective-permute-done | bytes 352288 | tf_op jit(solution)/shard_map/ppermute | solution.py:55
  315.8 24.6 %collective-permute-done.33 = bf16[256,2752]{0,1:T(8,128)(2,1)S(1)} collective-permute-done((bf16[256,2752]{0,1:T(8,128)(2,1)}, bf16[256,2752]{0,1:T(8,128)(2,1)S(1)}, u32[]{:S(2)}, u32[]{:S(2)}) %collective-permute-start.33) | collective-permute-done | bytes 1409056 | tf_op jit(solution)/shard_map/ppermute | solution.py:52
  346.0 26.6 %collective-permute-done.35 = bf16[256,2752]{0,1:T(8,128)(2,1)S(1)} collective-permute-done((bf16[256,2752]{0,1:T(8,128)(2,1)S(1)}, bf16[256,2752]{0,1:T(8,128)(2,1)S(1)}, u32[]{:S(2)}, u32[]{:S(2)}) %collective-permute-start.35) | collective-permute-done | bytes 1409056 | tf_op jit(solution)/shard_map/ppermute | solution.py:52
  377.4 11.6 %collective-permute-done.37 = bf16[128,2752]{0,1:T(8,128)(2,1)S(1)} collective-permute-done((bf16[128,2752]{0,1:T(8,128)(2,1)S(1)}, bf16[128,2752]{0,1:T(8,128)(2,1)S(1)}, u32[]{:S(2)}, u32[]{:S(2)}) %collective-permute-start.37) | collective-permute-done | bytes 704544 | tf_op jit(solution)/shard_map/ppermute | solution.py:56
  393.2 17.8 %fusion.106 = f32[1024,2752]{0,1:T(8,128)} fusion(bf16[1024,2048]{1,0:T(8,128)(2,1)S(1)} %bitcast.266, bf16[2048,2752]{0,1:T(8,128)(2,1)} %constant_dynamic-update-slice_fusion.18), kind=kOutput, calls=%fused_computation.411 | convolution fusion | flops 11542724608 | bytes 26738688 | tf_op jit(solution)/shard_map/dot_general | solution.py:211
  411.0 15.0 %fusion.4 = (bf16[1024,1376]{0,1:T(8,128)(2,1)}, bf16[1024,1376]{0,1:T(8,128)(2,1)}, bf16[1024,1376]{0,1:T(8,128)(2,1)S(1)}) fusion(f32[1024,2752]{0,1:T(8,128)} %fusion.106, bf16[1024,2048]{1,0:T(8,128)(2,1)S(1)} %bitcast.262, bf16[2048,1376]{0,1:T(8,128)(2,1)} %constant_dynamic-update-slice_fusion.27), kind=kOutput, calls=%fused_computation.14 | convolution fusion | flops 5795315712 | bytes 29556736 | tf_op jit(solution)/shard_map/dot_general | solution.py:211
  436.3 17.9 %convolution_convert_fusion = bf16[2048,2752]{0,1:T(8,128)(2,1)} fusion(bf16[1024,2048]{1,0:T(8,128)(2,1)} %bitcast.267, bf16[1024,1376]{0,1:T(8,128)(2,1)} %get-tuple-element.101, bf16[1024,1376]{0,1:T(8,128)(2,1)} %get-tuple-element.100), kind=kOutput, calls=%fused_computation | convolution fusion | flops 11559632896 | bytes 21102592 | tf_op jit(solution)/shard_map/dot_general | solution.py:219
  454.1 18.1 %convolution_convert_fusion.6 = bf16[1024,2048]{1,0:T(8,128)(2,1)} fusion(bf16[2048,2752]{0,1:T(8,128)(2,1)} %constant_dynamic-update-slice_fusion.18, bf16[1024,1376]{0,1:T(8,128)(2,1)} %get-tuple-element.101, bf16[1024,1376]{0,1:T(8,128)(2,1)} %get-tuple-element.100), kind=kOutput, calls=%fused_computation.51 | convolution fusion | flops 11556093952 | bytes 21102592 | tf_op jit(solution)/shard_map/dot_general | solution.py:215
  474.9 9.9 %convolution_convert_fusion.4 = bf16[1024,2048]{1,0:T(8,128)(2,1)S(1)} fusion(bf16[1024,1376]{0,1:T(8,128)(2,1)} %copy-done.97, bf16[2048,1376]{0,1:T(8,128)(2,1)} %constant_dynamic-update-slice_fusion.27), kind=kOutput, calls=%fused_computation.49 | convolution fusion | flops 5773459456 | bytes 12648448 | tf_op jit(solution)/shard_map/dot_general | solution.py:215
  489.8 6.5 collective-permute-done.110
  500.6 10.8 %collective-permute-done.78 = bf16[128,2752]{0,1:T(8,128)(2,1)S(1)} collective-permute-done((bf16[128,2752]{0,1:T(8,128)(2,1)S(1)}, bf16[128,2752]{0,1:T(8,128)(2,1)S(1)}, u32[]{:S(2)}, u32[]{:S(2)}) %collective-permute-start.78) | collective-permute-done | bytes 704544 | tf_op jit(solution)/shard_map/ppermute | solution.py:68
  523.1 10.9 %collective-permute-done.79 = bf16[128,2752]{0,1:T(8,128)(2,1)S(1)} collective-permute-done((bf16[128,2752]{0,1:T(8,128)(2,1)S(1)}, bf16[128,2752]{0,1:T(8,128)(2,1)S(1)}, u32[]{:S(2)}, u32[]{:S(2)}) %collective-permute-start.79) | collective-permute-done | bytes 704544 | tf_op jit(solution)/shard_map/ppermute | solution.py:68
  551.5 8.7 %collective-permute-done.113 = bf16[128,1376]{0,1:T(8,128)(2,1)S(1)} collective-permute-done((bf16[128,1376]{0,1:T(8,128)(2,1)}, bf16[128,1376]{0,1:T(8,128)(2,1)S(1)}, u32[]{:S(2)}, u32[]{:S(2)}) %collective-permute-start.113) | collective-permute-done | bytes 352288 | tf_op jit(solution)/shard_map/ppermute | solution.py:68
  622.7 9.7 %collective-permute-done.84 = bf16[128,2752]{0,1:T(8,128)(2,1)S(1)} collective-permute-done((bf16[128,2752]{0,1:T(8,128)(2,1)S(1)}, bf16[128,2752]{0,1:T(8,128)(2,1)S(1)}, u32[]{:S(2)}, u32[]{:S(2)}) %collective-permute-start.84) | collective-permute-done | bytes 704544 | tf_op jit(solution)/shard_map/ppermute | solution.py:68
  699.2 7.0 collective-permute-done.55
  809.3 16.6 %collective-permute-done.93 = f32[2,256]{1,0:T(2,128)S(1)} collective-permute-done((f32[2,256]{1,0:T(2,128)S(1)}, f32[2,256]{1,0:T(2,128)S(1)}, u32[]{:S(2)}, u32[]{:S(2)}) %collective-permute-start.93) | collective-permute-done | bytes 2080 | tf_op jit(solution)/shard_map/ppermute | solution.py:129
  (716 shorter events, 508.6 us)
Async XLA Ops:
  6.1 47.9 %collective-permute-start.2 = (bf16[272,640]{1,0:T(8,128)(2,1)}, bf16[272,640]{1,0:T(8,128)(2,1)}, u32[]{:S(2)}, u32[]{:S(2)}) collective-permute-start(bf16[272,640]{1,0:T(8,128)(2,1)} %fusion.53), channel_id=1, source_target_pairs={{0,8},{8,16},{16,24},{24,28},{28,20},{20,12},{12,4},{4,0},{1,9},{9... | collective-permute-start | bytes 1044488 | tf_op jit(solution)/shard_map/ppermute | solution.py:51
  9.2 47.0 %collective-permute-start.3 = (bf16[272,640]{1,0:T(8,128)(2,1)}, bf16[272,640]{1,0:T(8,128)(2,1)}, u32[]{:S(2)}, u32[]{:S(2)}) collective-permute-start(bf16[272,640]{1,0:T(8,128)(2,1)} %fusion.53), channel_id=1, source_target_pairs={{8,0},{16,8},{24,16},{28,24},{20,28},{12,20},{4,12},{0,4},{9,1},{1... | collective-permute-start | bytes 1044488 | tf_op jit(solution)/shard_map/ppermute | solution.py:52
  10.9 36.4 %collective-permute-start.18 = (bf16[256,512]{0,1:T(8,128)(2,1)}, bf16[256,512]{0,1:T(8,128)(2,1)}, u32[]{:S(2)}, u32[]{:S(2)}) collective-permute-start(bf16[256,512]{0,1:T(8,128)(2,1)} %convert_bitcast_fusion.1), channel_id=1, source_target_pairs={{0,8},{8,16},{16,24},{24,28},{28,20},{20,12},{12,4},{4,0},{1,9},{9... | collective-permute-start | bytes 786440 | tf_op jit(solution)/shard_map/ppermute | solution.py:51
  12.9 37.8 %collective-permute-start.19 = (bf16[256,512]{0,1:T(8,128)(2,1)}, bf16[256,512]{0,1:T(8,128)(2,1)}, u32[]{:S(2)}, u32[]{:S(2)}) collective-permute-start(bf16[256,512]{0,1:T(8,128)(2,1)} %convert_bitcast_fusion.1), channel_id=1, source_target_pairs={{8,0},{16,8},{24,16},{28,24},{20,28},{12,20},{4,12},{0,4},{9,1},{1... | collective-permute-start | bytes 786440 | tf_op jit(solution)/shard_map/ppermute | solution.py:52
  19.8 70.0 %collective-permute-start = (bf16[256,2048]{1,0:T(8,128)(2,1)S(1)}, bf16[256,2048]{1,0:T(8,128)(2,1)}, u32[]{:S(2)}, u32[]{:S(2)}) collective-permute-start(bf16[256,2048]{1,0:T(8,128)(2,1)S(1)} %constant_dynamic-update-slice_fusion), channel_id=1, source_target_pairs={{0,2},{1,3},{2,0},{3,1},{4,6},{5,7},{6,4},{7,5},{8,10},{9,11},{10,... | collective-permute-start | bytes 3145736 | tf_op jit(solution)/shard_map/ppermute | solution.py:100
  47.4 45.9 %collective-permute-start.38 = (bf16[256,1376]{0,1:T(8,128)(2,1)}, bf16[256,1376]{0,1:T(8,128)(2,1)}, u32[]{:S(2)}, u32[]{:S(2)}) collective-permute-start(bf16[256,1376]{0,1:T(8,128)(2,1)} %convert_bitcast_fusion), channel_id=1, source_target_pairs={{0,8},{8,16},{16,24},{24,28},{28,20},{20,12},{12,4},{4,0},{1,9},{9... | collective-permute-start | bytes 2113544 | tf_op jit(solution)/shard_map/ppermute | solution.py:51
  78.6 176.8 %collective-permute-start.30 = (bf16[256,2752]{0,1:T(8,128)(2,1)}, bf16[256,2752]{0,1:T(8,128)(2,1)}, u32[]{:S(2)}, u32[]{:S(2)}) collective-permute-start(bf16[256,2752]{0,1:T(8,128)(2,1)} %pad_maximum_fusion.12), channel_id=1, source_target_pairs={{0,8},{8,16},{16,24},{24,28},{28,20},{20,12},{12,4},{4,0},{1,9},{9... | collective-permute-start | bytes 4227080 | tf_op jit(solution)/shard_map/ppermute | solution.py:51
  93.3 60.6 %collective-permute-start.1 = (bf16[2,256,2048]{2,1,0:T(8,128)(2,1)}, bf16[2,256,2048]{2,1,0:T(8,128)(2,1)}, u32[]{:S(2)}, u32[]{:S(2)}) collective-permute-start(bf16[2,256,2048]{2,1,0:T(8,128)(2,1)} %pad_maximum_fusion.8), channel_id=1, source_target_pairs={{0,1},{1,0},{2,3},{3,2},{4,5},{5,4},{6,7},{7,6},{8,9},{9,8},{10,11... | collective-permute-start | bytes 6291464 | tf_op jit(solution)/shard_map/ppermute | solution.py:102
  95.5 162.5 %collective-permute-start.31 = (bf16[256,2752]{0,1:T(8,128)(2,1)}, bf16[256,2752]{0,1:T(8,128)(2,1)}, u32[]{:S(2)}, u32[]{:S(2)}) collective-permute-start(bf16[256,2752]{0,1:T(8,128)(2,1)} %pad_maximum_fusion.12), channel_id=1, source_target_pairs={{8,0},{16,8},{24,16},{28,24},{20,28},{12,20},{4,12},{0,4},{9,1},{1... | collective-permute-start | bytes 4227080 | tf_op jit(solution)/shard_map/ppermute | solution.py:52
  148.2 90.8 %collective-permute-start.48 = (bf16[256,2048]{1,0:T(8,128)(2,1)}, bf16[256,2048]{1,0:T(8,128)(2,1)}, u32[]{:S(2)}, u32[]{:S(2)}) collective-permute-start(bf16[256,2048]{1,0:T(8,128)(2,1)} %copy-done.28), channel_id=1, source_target_pairs={{0,2},{1,3},{2,0},{3,1},{4,6},{5,7},{6,4},{7,5},{8,10},{9,11},{10,... | collective-permute-start | bytes 3145736 | tf_op jit(solution)/shard_map/ppermute | solution.py:100
  207.4 36.8 %collective-permute-start.40 = (bf16[256,1376]{0,1:T(8,128)(2,1)}, bf16[256,1376]{0,1:T(8,128)(2,1)}, u32[]{:S(2)}, u32[]{:S(2)}) collective-permute-start(bf16[256,1376]{0,1:T(8,128)(2,1)} %collective-permute-done.38), channel_id=1, source_target_pairs={{0,8},{8,16},{16,24},{24,28},{28,20},{20,12},{12,4},{4,0},{1,9},{9... | collective-permute-start | bytes 2113544 | tf_op jit(solution)/shard_map/ppermute | solution.py:51
  239.0 35.8 %collective-permute-start.26 = (bf16[2,256,2048]{2,1,0:T(8,128)(2,1)}, bf16[2,256,2048]{2,1,0:T(8,128)(2,1)}, u32[]{:S(2)}, u32[]{:S(2)}) collective-permute-start(bf16[2,256,2048]{2,1,0:T(8,128)(2,1)} %dynamic-slice_bitcast_fusion.3), channel_id=1, source_target_pairs={{0,1},{1,0},{2,3},{3,2},{4,5},{5,4},{6,7},{7,6},{8,9},{9,8},{10,11... | collective-permute-start | bytes 6291464 | tf_op jit(solution)/shard_map/ppermute | solution.py:116
  244.2 97.5 %collective-permute-start.49 = (bf16[2,256,2048]{2,1,0:T(8,128)(2,1)}, bf16[2,256,2048]{2,1,0:T(8,128)(2,1)S(1)}, u32[]{:S(2)}, u32[]{:S(2)}) collective-permute-start(bf16[2,256,2048]{2,1,0:T(8,128)(2,1)} %pad_maximum_fusion.10), channel_id=1, source_target_pairs={{0,1},{1,0},{2,3},{3,2},{4,5},{5,4},{6,7},{7,6},{8,9},{9,8},{10,11... | collective-permute-start | bytes 6291464 | tf_op jit(solution)/shard_map/ppermute | solution.py:102
  258.0 51.6 %collective-permute-start.32 = (bf16[256,2752]{0,1:T(8,128)(2,1)}, bf16[256,2752]{0,1:T(8,128)(2,1)S(1)}, u32[]{:S(2)}, u32[]{:S(2)}) collective-permute-start(bf16[256,2752]{0,1:T(8,128)(2,1)} %collective-permute-done.30), channel_id=1, source_target_pairs={{0,8},{8,16},{16,24},{24,28},{28,20},{20,12},{12,4},{4,0},{1,9},{9... | collective-permute-start | bytes 4227080 | tf_op jit(solution)/shard_map/ppermute | solution.py:51
  269.7 37.2 %collective-permute-start.44 = (bf16[128,1376]{0,1:T(8,128)(2,1)S(1)}, bf16[128,1376]{0,1:T(8,128)(2,1)S(1)}, u32[]{:S(2)}, u32[]{:S(2)}) collective-permute-start(bf16[128,1376]{0,1:T(8,128)(2,1)S(1)} %slice.725), channel_id=1, source_target_pairs={{0,8},{8,16},{16,24},{24,28},{28,20},{20,12},{12,4},{4,0},{1,9},{9... | collective-permute-start | bytes 1056776 | tf_op jit(solution)/shard_map/ppermute | solution.py:55
  277.3 34.7 %collective-permute-start.27 = (bf16[256,2048]{1,0:T(8,128)(2,1)S(1)}, bf16[256,2048]{1,0:T(8,128)(2,1)S(1)}, u32[]{:S(2)}, u32[]{:S(2)}) collective-permute-start(bf16[256,2048]{1,0:T(8,128)(2,1)S(1)} %fusion.35), channel_id=1, source_target_pairs={{0,2},{1,3},{2,0},{3,1},{4,6},{5,7},{6,4},{7,5},{8,10},{9,11},{10,... | collective-permute-start | bytes 3145736 | tf_op jit(solution)/shard_map/ppermute | solution.py:121
  309.6 34.3 %collective-permute-start.34 = (bf16[256,2752]{0,1:T(8,128)(2,1)S(1)}, bf16[256,2752]{0,1:T(8,128)(2,1)S(1)}, u32[]{:S(2)}, u32[]{:S(2)}) collective-permute-start(bf16[256,2752]{0,1:T(8,128)(2,1)S(1)} %collective-permute-done.32), channel_id=1, source_target_pairs={{0,8},{8,16},{16,24},{24,28},{28,20},{20,12},{12,4},{4,0},{1,9},{9... | collective-permute-start | bytes 4227080 | tf_op jit(solution)/shard_map/ppermute | solution.py:51
  342.8 49.1 %collective-permute-start.29 = (bf16[2,256,2048]{2,1,0:T(8,128)(2,1)S(1)}, bf16[2,256,2048]{2,1,0:T(8,128)(2,1)S(1)}, u32[]{:S(2)}, u32[]{:S(2)}) collective-permute-start(bf16[2,256,2048]{2,1,0:T(8,128)(2,1)S(1)} %pad_maximum_fusion.9), channel_id=1, source_target_pairs={{0,1},{1,0},{2,3},{3,2},{4,5},{5,4},{6,7},{7,6},{8,9},{9,8},{10,11... | collective-permute-start | bytes 6291464 | tf_op jit(solution)/shard_map/ppermute | solution.py:102
  433.9 38.4 %collective-permute-start.108 = (bf16[128,1376]{0,1:T(8,128)(2,1)S(1)}, bf16[128,1376]{0,1:T(8,128)(2,1)S(1)}, u32[]{:S(2)}, u32[]{:S(2)}) collective-permute-start(bf16[128,1376]{0,1:T(8,128)(2,1)S(1)} %get-tuple-element.133), channel_id=1, source_target_pairs={{0,8},{8,16},{16,24},{24,28},{28,20},{20,12},{12,4},{4,0},{1,9},{9... | collective-permute-start | bytes 1056776 | tf_op jit(solution)/shard_map/ppermute | solution.py:68
  436.1 36.2 %collective-permute-start.115 = (bf16[128,1376]{0,1:T(8,128)(2,1)S(1)}, bf16[128,1376]{0,1:T(8,128)(2,1)S(1)}, u32[]{:S(2)}, u32[]{:S(2)}) collective-permute-start(bf16[128,1376]{0,1:T(8,128)(2,1)S(1)} %get-tuple-element.134), channel_id=1, source_target_pairs={{8,0},{16,8},{24,16},{28,24},{20,28},{12,20},{4,12},{0,4},{9,1},{1... | collective-permute-start | bytes 1056776 | tf_op jit(solution)/shard_map/ppermute | solution.py:69
  489.7 58.5 %collective-permute-start.46 = (bf16[2,256,2048]{2,1,0:T(8,128)(2,1)S(1)}, bf16[2,256,2048]{2,1,0:T(8,128)(2,1)S(1)}, u32[]{:S(2)}, u32[]{:S(2)}) collective-permute-start(bf16[2,256,2048]{2,1,0:T(8,128)(2,1)S(1)} %dynamic-slice_bitcast_fusion.2), channel_id=1, source_target_pairs={{0,1},{1,0},{2,3},{3,2},{4,5},{5,4},{6,7},{7,6},{8,9},{9,8},{10,11... | collective-permute-start | bytes 6291464 | tf_op jit(solution)/shard_map/ppermute | solution.py:116
  549.1 42.7 %collective-permute-start.47 = (bf16[256,2048]{1,0:T(8,128)(2,1)S(1)}, bf16[256,2048]{1,0:T(8,128)(2,1)}, u32[]{:S(2)}, u32[]{:S(2)}) collective-permute-start(bf16[256,2048]{1,0:T(8,128)(2,1)S(1)} %fusion.36), channel_id=1, source_target_pairs={{0,2},{1,3},{2,0},{3,1},{4,6},{5,7},{6,4},{7,5},{8,10},{9,11},{10,... | collective-permute-start | bytes 3145736 | tf_op jit(solution)/shard_map/ppermute | solution.py:121
  668.2 43.8 %collective-permute-start.101 = (bf16[128,512]{1,0:T(8,128)(2,1)S(1)}, bf16[128,512]{1,0:T(8,128)(2,1)S(1)}, u32[]{:S(2)}, u32[]{:S(2)}) collective-permute-start(bf16[128,512]{1,0:T(8,128)(2,1)S(1)} %get-tuple-element.176), channel_id=1, source_target_pairs={{8,0},{16,8},{24,16},{28,24},{20,28},{12,20},{4,12},{0,4},{9,1},{1... | collective-permute-start | bytes 393224 | tf_op jit(solution)/shard_map/ppermute | solution.py:69
  668.6 43.5 %collective-permute-start.94 = (bf16[128,512]{1,0:T(8,128)(2,1)S(1)}, bf16[128,512]{1,0:T(8,128)(2,1)S(1)}, u32[]{:S(2)}, u32[]{:S(2)}) collective-permute-start(bf16[128,512]{1,0:T(8,128)(2,1)S(1)} %get-tuple-element.175), channel_id=1, source_target_pairs={{0,8},{8,16},{16,24},{24,28},{28,20},{20,12},{12,4},{4,0},{1,9},{9... | collective-permute-start | bytes 393224 | tf_op jit(solution)/shard_map/ppermute | solution.py:68
  (203 other events, 3622.4 us)

commit v2 on v1

--- a/solution.py
+++ b/solution.py
@@ -1,6 +1,9 @@
 import jax
 import jax.numpy as jnp
+import numpy as np
 from jax import lax
+from jax.experimental import pallas as pl
+from jax.experimental.pallas import tpu as pltpu
 from jax.sharding import PartitionSpec as P
 
 FEAT = 16
@@ -217,6 +220,1272 @@
 
 def dot_tt(a, b):
     return lax.dot_general(a, b, (((0,), (0,)), ((), ())), preferred_element_type=f32)
+
+
+def ring_place(seq):
+    z, x = seq // 2, seq % 2
+    return z + x * (7 - 2 * z)
+
+
+def ring_seq(place):
+    place = lax.rem(place + 8, 8)
+    far = place // 4
+    return (1 - far) * 2 * place + far * (15 - 2 * place)
+
+
+class Sems:
+    def __init__(self, ref):
+        self.ref, self.used = ref, 0
+
+    def take(self):
+        self.used += 1
+        return self.ref.at[self.used - 1]
+
+
+class Links:
+    def __init__(self, send, recv):
+        self.send, self.recv, self.sent = Sems(send), Sems(recv), []
+
+    def copy(self, src, dst, **to):
+        return pltpu.make_async_remote_copy(
+            src_ref=src,
+            dst_ref=dst,
+            send_sem=self.send.take(),
+            recv_sem=self.recv.take(),
+            device_id=to,
+            device_id_type=pl.DeviceIdType.MESH,
+        )
+
+    def start(self, src, dst, **to):
+        made = self.copy(src, dst, **to)
+        made.start()
+        self.sent.append(made)
+        return made
+
+    def sent_now(self, some):
+        for made in some:
+            made.wait_send()
+        self.sent = [made for made in self.sent if all(made is not other for other in some)]
+
+    def finish(self):
+        for made in self.sent:
+            made.wait_send()
+
+
+class Gather:
+    def __init__(self, links, arrays, split, nearby):
+        self.links, self.arrays, self.split, self.nearby = links, arrays, split, nearby
+        self.at = {k: j for j, k in enumerate(relative_list(8))}
+        self.flying = {}
+        self.events = [
+            (a, step, way, part)
+            for a in range(len(arrays))
+            for step in (1, 2, 3, 4)
+            for part in (0, 1)
+            for way in (0, 1)
+            if step < 4 or way == part
+        ]
+        self.done = 0
+        for part in (0, 1):
+            for way in (0, 1):
+                self.go(0, 1, way, part)
+
+    def rows(self, part):
+        return pl.ds(part * self.split, self.split)
+
+    def go(self, a, step, way, part):
+        own, everyone = self.arrays[a]
+        before, after = (step - 1, step) if way == 0 else ((9 - step) % 8, 8 - step)
+        src = own if step == 1 else everyone.at[self.at[before]]
+        self.flying[a, step, way, part] = self.links.start(
+            src.at[self.rows(part)],
+            everyone.at[self.at[after], self.rows(part)],
+            seq=self.nearby[way],
+        )
+
+    def pump(self, upto):
+        while self.done < min(upto, len(self.events)):
+            a, step, way, part = self.events[self.done]
+            self.flying[a, step, way, part].wait_recv()
+            if step < 3 or (step == 3 and way == part):
+                self.go(a, step + 1, way, part)
+            if step == 3 and a + 1 < len(self.arrays):
+                self.go(a + 1, 1, way, part)
+            self.done += 1
+
+    def pump_array(self, a):
+        self.pump(14 * (a + 1))
+
+
+def greet(peers):
+    barrier = pltpu.get_barrier_semaphore()
+    for peer in peers:
+        pl.semaphore_signal(
+            barrier, inc=1, device_id=peer, device_id_type=pl.DeviceIdType.MESH
+        )
+    pl.semaphore_wait(barrier, len(peers))
+
+
+def places():
+    seq, tp = lax.axis_index("seq"), lax.axis_index("tp")
+    place = ring_place(seq)
+    nearby = (ring_seq(place + 1), ring_seq(place - 1))
+    over_y = lax.rem(tp + 2, 4)
+    over_core = tp + 1 - 2 * (tp % 2)
+    peers = [{"seq": ring_seq(place + k)} for k in range(1, 8)]
+    peers += [{"tp": over_y}, {"tp": over_core}]
+    return seq, tp, place, nearby, over_y, over_core, peers
+
+
+class Rows:
+    def __init__(self, links, own, everyone, tp, over_y, over_core, rows):
+        self.links, self.all, self.tp = links, everyone, tp
+        self.over_y, self.over_core, self.rows = over_y, over_core, rows
+        half = rows // 2
+        self.first = [
+            links.start(
+                own.at[pl.ds(i * half, half)], self.block(tp, i * half, half), tp=over_y
+            )
+            for i in (0, 1)
+        ]
+        self.near = links.start(own, self.block(tp, 0, rows), tp=over_core)
+        self.last = []
+
+    def block(self, owner, offset, size):
+        return self.all.at[pl.ds(pl.multiple_of(owner * self.rows + offset, 16), size)]
+
+    def forward(self, i):
+        half = self.rows // 2
+        self.first[i].wait_recv()
+        came = self.block(self.over_y, i * half, half)
+        self.last.append(self.links.start(came, came, tp=self.over_core))
+
+    def finish(self):
+        self.near.wait_recv()
+        for made in self.last:
+            made.wait_recv()
+
+
+FEATS = 160
+
+
+def phi(heads, h, select_a, select_b, lanes):
+    a = dot(heads, select_a[h]) + lanes[0:1, :]
+    b = dot(heads, select_b[h]) + lanes[1:2, :]
+    return a, b
+
+
+def fwd_kernel(
+    x_ref, tok_ref, line_ref, sa_ref, sb_ref, lanes_ref, hm_ref, coef_ref,
+    gain_ref, q_own, o_own, g_own, u_own, d_own, c_own,
+    wq_all, wo_all, wg_all, wu_all, wd_all, c_all,
+    h1_out, qkv_out, yb_out, den_out, x1_out, h2_out, gate_out, up_out, m_out, sin_out, gain_out,
+    xg, h1, wq, wo, wg, wu, qkv, kq, num, den, yb, sc, rc, sy, ry, x1, h2, gate, up, mm,
+    gains_all, gains, st, st_x, st_t, st_z, s_in, ho,
+    send, recv, local,
+):
+    seq, tp, place, nearby, over_y, over_core, peers = places()
+    z, x = seq // 2, seq % 2
+    at = {k: j for j, k in enumerate(relative_list(8))}
+    rows = x_ref.shape[0]
+    total = 4 * rows
+    links = Links(send, recv)
+    locs = Sems(local)
+    pending = []
+
+    def store(src, dst):
+        made = pltpu.make_async_copy(src, dst, locs.take())
+        made.start()
+        pending.append(made)
+
+    def load(src, dst):
+        made = pltpu.make_async_copy(src, dst, locs.take())
+        made.start()
+        return made
+
+    greet(peers)
+    gain_flying = [
+        links.start(gain_ref, gains_all.at[at[k]], seq=ring_seq(place + k)) for k in range(1, 8)
+    ]
+    ring = Gather(
+        links,
+        [(q_own, wq_all), (o_own, wo_all), (g_own, wg_all), (u_own, wu_all), (d_own, wd_all)],
+        128,
+        nearby,
+    )
+    xrows = Rows(links, x_ref, xg, tp, over_y, over_core, rows)
+    own_in = [
+        load(x_ref, xrows.block(tp, 0, rows)),
+        load(gain_ref, gains_all.at[at[0]]),
+    ]
+    own_kept = [load(own, everyone.at[at[0]]) for own, everyone in ring.arrays]
+    store(c_own, c_all.at[pl.ds(pl.multiple_of(tp * rows, rows), rows)])
+
+    ring.pump(6)
+    xrows.forward(0)
+    for made in gain_flying:
+        made.wait_recv()
+    for made in own_in:
+        made.wait()
+    for j in range(8):
+        chunk = gains_all[j].astype(f32)
+        gains[0:8, j * 256 : (j + 1) * 256] = chunk[0:8]
+    ring.pump(10)
+    xrows.forward(1)
+    ring.pump_array(0)
+    own_kept[0].wait()
+    got = load_weights(load, wq_all, wq)
+    xrows.finish()
+
+    def norm_first(i, _):
+        r = pl.ds(pl.multiple_of(i * 32, 32), 32)
+        v = xg[r, :].astype(f32)
+        s = lax.rsqrt(jnp.mean(v * v, axis=1, keepdims=True) + epsilon)
+        h1[r, :] = (v * s * gains[0:1, :]).astype(bf16)
+        return 0
+
+    lax.fori_loop(0, total // 32, norm_first, 0)
+    store(h1, h1_out)
+    crows = Rows(links, c_own, c_all, tp, over_y, over_core, rows)
+    ring.pump(15)
+    for made in got:
+        made.wait()
+
+    def project(i, _):
+        r = pl.ds(pl.multiple_of(i * 256, 256), 256)
+        res = dot(h1[r, :], wq[...])
+        qkv[r, :] = res.astype(bf16)
+        kq[r, :] = pltpu.roll(res[:, :128], 64, 1).astype(bf16)
+        return 0
+
+    lax.fori_loop(0, total // 256, project, 0)
+    store(qkv, qkv_out)
+    ring.pump(17)
+
+    heads = 4
+
+    def head_v(h):
+        return slice(128 + h * 128, 256 + h * 128)
+
+    for h in range(heads):
+
+        def state(i, c, h=h):
+            s, zz = c
+            r = pl.ds(pl.multiple_of(i * 256, 256), 256)
+            a, b = phi(kq[r, :], h, sa_ref, sb_ref, lanes_ref)
+            f = a * b * lanes_ref[2:3, :] * tok_ref[r, 2:3]
+            s = s + dot_tt(f.astype(bf16), qkv[r, head_v(h)])
+            return s, zz + jnp.sum(f, axis=0, keepdims=True)
+
+        s, zz = lax.fori_loop(
+            0, total // 256, state, (jnp.zeros((256, 128), f32), jnp.zeros((1, 256), f32))
+        )
+        pack_state(st, h, s, zz)
+        ring.pump(18 + h)
+    to_x = links.start(st, st_x, seq=seq + 1 - 2 * x)
+
+    def local_head(h):
+        for i in range(total // 256):
+            r = slice(i * 256, (i + 1) * 256)
+            span = (i + 1) * 256
+            qm = (qkv[r, :128].astype(f32) * hm_ref[h : h + 1, :]).astype(bf16)
+            u = dot_t(qm, kq[:span, :])
+            keep = (line_ref[0:1, :span] >= tok_ref[r, 0:1]) & (
+                line_ref[0:1, :span] <= tok_ref[r, 3:4]
+            )
+            kap = jnp.where(keep, (0.5 * u + 1.0) * u + 1.0, 0.0)
+            den[r, h : h + 1] = jnp.sum(kap, axis=1, keepdims=True)
+            num[r, h * 128 : (h + 1) * 128] = dot(kap.astype(bf16), qkv[:span, head_v(h)])
+
+    local_head(0)
+    ring.pump(23)
+    local_head(1)
+    ring.pump(25)
+    to_x.wait_recv()
+    for h in range(heads):
+        mine, theirs = st[h].astype(f32), st_x[h].astype(f32)
+        early = jnp.where(x == 0, mine, theirs)
+        later = jnp.where(x == 0, theirs, mine)
+        st_t[h] = (later + coef_ref[0:1, :] * early).astype(bf16)
+    to_z = [links.copy(st_t, st_z.at[d - 1], seq=seq + 2 * d) for d in (1, 2, 3)]
+    for d in (1, 2, 3):
+
+        @pl.when(z + d < 4)
+        def _(d=d):
+            to_z[d - 1].start()
+
+    local_head(2)
+    ring.pump(27)
+    local_head(3)
+    ring.pump(28)
+    own_kept[1].wait()
+    got = load_weights(load, wo_all, wo)
+    for h in range(heads):
+        num_in = coef_ref[1:2, :] * st_x[h].astype(f32)
+        s_in[h, 0:176, :] = num_in
+        s_in[h, 176:256, :] = jnp.zeros((80, 128), f32)
+    for d in (1, 2, 3):
+
+        @pl.when(z >= d)
+        def _(d=d):
+            to_z[d - 1].wait_recv()
+            for h in range(heads):
+                s_in[h, 0:176, :] += coef_ref[1 + d : 2 + d, :] * st_z[d - 1, h].astype(f32)
+
+    store(s_in, sin_out)
+    for h in range(heads):
+        z_row = jnp.concatenate([s_in[h, 160:161, :], s_in[h, 161:162, :]], axis=1)
+        feat = jax.lax.broadcasted_iota(jnp.int32, (256, 128), 0)
+        s_low = jnp.where(feat < FEATS, s_in[h], 0.0).astype(bf16)
+
+        def carry(i, _, h=h, z_row=z_row, s_low=s_low):
+            r = pl.ds(pl.multiple_of(i * 256, 256), 256)
+            a, b = phi(qkv[r, 0:128], h, sa_ref, sb_ref, lanes_ref)
+            f = a * b * lanes_ref[2:3, :] * tok_ref[r, 1:2]
+            hv = slice(h * 128, (h + 1) * 128)
+            top = num[r, hv] + dot(f.astype(bf16), s_low)
+            low = den[r, h : h + 1] + jnp.sum(f * z_row, axis=1, keepdims=True)
+            den[r, h : h + 1] = low
+            y = top / low
+            yb[r, hv] = y.astype(bf16)
+            return 0
+
+        lax.fori_loop(0, total // 256, carry, 0)
+        ring.pump(29 + h)
+    store(yb, yb_out)
+    store(den, den_out)
+    for made in got:
+        made.wait()
+
+    y_at, c_at = tp // 2, tp % 2
+
+    def out_rows(block):
+        return yb[pl.ds(pl.multiple_of(block * rows, rows), rows), :]
+
+    cols = 512
+    to_core = []
+    for yy in (0, 1):
+
+        def core_cols(i, _, yy=yy):
+            c = pl.ds(pl.multiple_of(i * cols, cols), cols)
+            sc[yy, :, c] = dot_t(out_rows(yy * 2 + 1 - c_at), wo[c, :]).astype(bf16)
+            return 0
+
+        lax.fori_loop(0, 2048 // cols, core_cols, 0)
+        to_core.append(links.start(sc.at[yy], rc.at[yy], tp=over_core))
+    for made in to_core:
+        made.wait_recv()
+
+    def away_cols(i, _):
+        c = pl.ds(pl.multiple_of(i * cols, cols), cols)
+        part = dot_t(out_rows((1 - y_at) * 2 + c_at), wo[c, :])
+        sy[:, c] = (part + rc[1 - y_at, :, c].astype(f32)).astype(bf16)
+        return 0
+
+    lax.fori_loop(0, 2048 // cols, away_cols, 0)
+    to_y = links.start(sy, ry, tp=over_y)
+
+    def own_cols(i, _):
+        c = pl.ds(pl.multiple_of(i * cols, cols), cols)
+        x1[:, c] = (
+            dot_t(out_rows(tp), wo[c, :]) + rc[y_at, :, c].astype(f32) + x_ref[:, c].astype(f32)
+        )
+        return 0
+
+    lax.fori_loop(0, 2048 // cols, own_cols, 0)
+    ring.pump(34)
+    to_y.wait_recv()
+
+    def norm_second(i, _):
+        r = pl.ds(pl.multiple_of(i * 32, 32), 32)
+        v = x1[r, :] + ry[r, :].astype(f32)
+        x1[r, :] = v
+        s = lax.rsqrt(jnp.mean(v * v, axis=1, keepdims=True) + epsilon)
+        ho[r, :] = (v * s * gains[1:2, :]).astype(bf16)
+        return 0
+
+    lax.fori_loop(0, rows // 32, norm_second, 0)
+    store(x1, x1_out)
+    store(gains, gain_out)
+    hrows = Rows(links, ho, h2, tp, over_y, over_core, rows)
+    own_in = load(ho, hrows.block(tp, 0, rows))
+    ring.pump(36)
+    hrows.forward(0)
+    ring.pump(37)
+    hrows.forward(1)
+    crows.forward(0)
+    crows.forward(1)
+    hrows.finish()
+    crows.finish()
+    own_in.wait()
+    store(h2, h2_out)
+    ring.pump_array(2)
+    own_kept[2].wait()
+    got = load_weights(load, wg_all, wg)
+    ring.pump_array(3)
+    own_kept[3].wait()
+    got += load_weights(load, wu_all, wu)
+    for made in got:
+        made.wait()
+
+    def gate_up(i, _):
+        r = pl.ds(pl.multiple_of(i * 128, 128), 128)
+        g = dot(h2[r, :], wg[...])
+        uu = dot(h2[r, :], wu[...])
+        gate[r, :] = g.astype(bf16)
+        up[r, :] = uu.astype(bf16)
+        mm[r, :] = (g * jax.nn.sigmoid(g) * uu).astype(bf16)
+        return 0
+
+    for quarter in range(4):
+        lax.fori_loop(quarter * total // 512, (quarter + 1) * total // 512, gate_up, 0)
+        ring.pump(58 + 2 * quarter)
+    store(gate, gate_out)
+    store(up, up_out)
+    store(mm, m_out)
+    ring.pump_array(4)
+    own_kept[4].wait()
+    for made in pending:
+        made.wait()
+    links.finish()
+    for d in (1, 2, 3):
+
+        @pl.when(z + d < 4)
+        def _(d=d):
+            to_z[d - 1].wait_send()
+
+
+def pack_state(st, h, s, zz):
+    st[h, 0:FEATS, :] = s[:FEATS].astype(bf16)
+    tail = jnp.concatenate([zz[:, :128], zz[:, 128:], jnp.zeros((14, 128), f32)], axis=0)
+    st[h, FEATS : FEATS + 16, :] = tail.astype(bf16)
+
+
+def load_weights(load, everyone, flat):
+    count, chunk = everyone.shape[0], everyone.shape[1]
+    return [load(everyone.at[j], flat.at[pl.ds(j * chunk, chunk)]) for j in range(count)]
+
+
+class Scatter:
+    def __init__(self, slots, send, recv, nearby):
+        self.slots, self.send, self.recv, self.nearby = slots, send, recv, nearby
+
+    def copy(self, a, step, way, sub, src, slot, width):
+        return pltpu.make_async_remote_copy(
+            src_ref=src,
+            dst_ref=self.piece(slot, way, sub, width),
+            send_sem=self.send.at[a % 2, way, sub],
+            recv_sem=self.recv.at[a % 2, way, sub, step],
+            device_id={"seq": self.nearby[way]},
+            device_id_type=pl.DeviceIdType.MESH,
+        )
+
+    def rows(self, way, sub, base=0):
+        start = base + way * 128 + sub * 64
+        return pl.ds(start if isinstance(start, int) else pl.multiple_of(start, 64), 64)
+
+    def piece(self, slot, way, sub, width):
+        return self.slots.at[slot, self.rows(way, sub), pl.ds(0, width)]
+
+    def begin(self, a, own, width, column=0):
+        for sub in (0, 1):
+            for way in (0, 1):
+                src = own.at[self.rows(way, sub, way * 256), pl.ds(column, width)]
+                self.copy(a, 0, way, sub, src, 7 * (a % 2), width).start()
+
+    def event(self, a, e, own, width, out, column=0):
+        step, sub = e // 2, e % 2
+        is_first, is_last = (6 - step) // 6, step // 6
+        here = is_first * 7 * (a % 2) + (1 - is_first) * step
+        far = (step + 1) // 4
+        place0 = (1 - far) * 2 * (step + 1) + far * (11 - 2 * step) + is_last * 8
+        far = (step + 2) // 4 - is_last
+        place1 = (1 - far) * (3 + 2 * step) + far * (10 - 2 * step) + is_last * 9
+        places = (place0, place1)
+        for way in (0, 1):
+            piece = self.piece(here, way, sub, width)
+            came = self.copy(a, step, way, sub, piece, here, width)
+            came.wait_recv()
+            came.wait_send()
+
+        def summed(way):
+            mine = own[self.rows(way, sub, places[way] * 256), pl.ds(column, width)]
+            came = self.slots[here, self.rows(way, sub), pl.ds(0, width)]
+            return came.astype(f32) + mine.astype(f32)
+
+        def on():
+            for way in (0, 1):
+                self.slots[here, self.rows(way, sub), pl.ds(0, width)] = summed(way).astype(bf16)
+                piece = self.piece(here, way, sub, width)
+                self.copy(a, step + 1, way, sub, piece, step + 1, width).start()
+
+        def end():
+            for way in (0, 1):
+                out[self.rows(way, sub), pl.ds(0, width)] = summed(way)
+
+        if isinstance(e, int):
+            if step < 6:
+                on()
+            else:
+                end()
+        else:
+            pl.when(step < 6)(on)
+            pl.when(step == 6)(end)
+
+
+class TpSum:
+    def __init__(self, part, from_core, from_y, sems, credits, tp, over_y, over_core):
+        self.part, self.from_core, self.from_y = part, from_core, from_y
+        self.sems, self.credits = sems, credits
+        self.tp, self.over_y, self.over_core = tp, over_y, over_core
+        self.y, self.c = tp // 2, tp % 2
+
+    def to_core(self, i, yy):
+        return pltpu.make_async_remote_copy(
+            src_ref=self.part.at[i, yy * 2 + 1 - self.c],
+            dst_ref=self.from_core.at[i, yy],
+            send_sem=self.sems.at[yy, i],
+            recv_sem=self.sems.at[2 + yy, i],
+            device_id={"tp": self.over_core},
+            device_id_type=pl.DeviceIdType.MESH,
+        )
+
+    def to_y(self, i):
+        return pltpu.make_async_remote_copy(
+            src_ref=self.part.at[i, (1 - self.y) * 2 + self.c],
+            dst_ref=self.from_y.at[i],
+            send_sem=self.sems.at[4, i],
+            recv_sem=self.sems.at[5, i],
+            device_id={"tp": self.over_y},
+            device_id_type=pl.DeviceIdType.MESH,
+        )
+
+    def sent(self, i):
+        self.to_core(i, 0).wait_send()
+        self.to_core(i, 1).wait_send()
+        self.to_y(i).wait_send()
+
+    def offer(self, i, turn, value):
+        if turn > 0:
+            self.sent(i)
+        for block in range(4):
+            self.part[i, block] = value[block * 256 : (block + 1) * 256].astype(bf16)
+        if turn > 0:
+            pl.semaphore_wait(self.credits.at[0], 1)
+        for yy in (0, 1):
+            self.to_core(i, yy).start()
+
+    def pass_on(self, i, turn):
+        for yy in (0, 1):
+            self.to_core(i, yy).wait_recv()
+        away = (1 - self.y) * 2 + self.c
+        self.part[i, away] = (
+            self.part[i, away].astype(f32) + self.from_core[i, 1 - self.y].astype(f32)
+        ).astype(bf16)
+        if turn > 0:
+            pl.semaphore_wait(self.credits.at[1], 1)
+        self.to_y(i).start()
+
+    def take(self, i, turn, use):
+        self.to_y(i).wait_recv()
+        use(
+            self.part[i, self.tp].astype(f32)
+            + self.from_core[i, self.y].astype(f32)
+            + self.from_y[i].astype(f32)
+        )
+        if turn < 2:
+            for k, peer in ((0, self.over_core), (1, self.over_y)):
+                pl.semaphore_signal(
+                    self.credits.at[k],
+                    inc=1,
+                    device_id={"tp": peer},
+                    device_id_type=pl.DeviceIdType.MESH,
+                )
+
+
+def col(i, width=256):
+    return pl.ds(i * width if isinstance(i, int) else pl.multiple_of(i * width, width), width)
+
+
+def bwd_kernel(
+    tok_ref, line_ref, sa_ref, sb_ref, lanes_ref, hm_ref, coef_ref, gains, x_in, x1_in, s_in, den,
+    wq_all, wo_all, wg_all, wu_all, wd_all, c_all, h1_all, qkv_all, yb_all, h2_all,
+    gate_all, up_all, m_all,
+    d_out, g_out, u_out, oq_out, block_out, input_out,
+    slots, s1, s2, wo, stream, hs, rows_all, mm, dup, tiles, qkv, kq, yb, dnum, dden, dden_t, dqkv,
+    dq, dk, part, from_core, from_y, acc, x1, bo, fout, st, st_x, st_t, st_z, s_back, own_rows,
+    ring_send, ring_recv, tp_sems, credits, send, recv, local, tile_sems,
+):
+    seq, tp, place, nearby, over_y, over_core, peers = places()
+    z, x = seq // 2, seq % 2
+    rows, width = own_rows.shape
+    total = 4 * rows
+    ff = mm.shape[1]
+    links = Links(send, recv)
+    locs = Sems(local)
+
+    def load(src, dst):
+        made = pltpu.make_async_copy(src, dst, locs.take())
+        made.start()
+        return made
+
+    def whole(everyone, flat):
+        count, chunk = everyone.shape[0], everyone.shape[1]
+        return [load(everyone.at[j], flat.at[pl.ds(j * chunk, chunk)]) for j in range(count)]
+
+    got_c = load(c_all, rows_all)
+    got_m = load(m_all, mm)
+    got_wd = whole(wd_all, s2)
+    greet(peers)
+    got_x1 = load(x1_in, x1)
+    got_qkv = [load(qkv_all, qkv), load(yb_all, yb)]
+    got_wo = whole(wo_all, wo)
+    ring = Scatter(slots, ring_send, ring_recv, nearby)
+    sums = TpSum(part, from_core, from_y, tp_sems, credits, tp, over_y, over_core)
+
+    def run(n, body, pumps=None, lookup=None):
+        def step(i, _):
+            body(i)
+            if pumps:
+                a, first, count = pumps
+                every = n // count
+                pl.when((i + 1) % every == 0)(lambda: event(a, first + (i + 1) // every - 1))
+            return 0
+
+        lax.fori_loop(0, n, step, 0)
+
+    plan = {0: (s1, ff, 0), 1: (s2, ff, 0), 2: (s1, ff, 0), 3: (s2, 1152, 0)}
+
+    def event(a, e):
+        own, wide, column = plan[a]
+        ring.event(a, e, own, wide, fout, column)
+
+    def begin(a):
+        own, wide, column = plan[a]
+        ring.begin(a, own, wide, column)
+
+    def events(a, first, last):
+        lax.fori_loop(first, last, lambda e, _: (event(a, e), 0)[1], 0)
+
+    def chunks_of(source, size, body, pumps=None, count=8):
+        def copies(i, slot):
+            return [
+                pltpu.make_async_copy(a, b, tile_sems.at[k, slot])
+                for k, (a, b) in enumerate(source(i, slot))
+            ]
+
+        for made in copies(0, 0):
+            made.start()
+
+        def step(i):
+            slot = i % 2
+
+            @pl.when(i + 1 < count)
+            def _():
+                for made in copies(i + 1, 1 - slot):
+                    made.start()
+
+            for made in copies(i, slot):
+                made.wait()
+            body(i, slot)
+
+        run(count, step, pumps)
+
+    got_c.wait()
+    got_m.wait()
+
+    def grad_down(j):
+        s1[col(j), :] = dot_tt(rows_all[:, col(j)], mm[...]).astype(bf16)
+
+    run(2, grad_down)
+    begin(0)
+    lax.fori_loop(2, 8, lambda j, _: (grad_down(j), 0)[1], 0)
+    for made in got_wd:
+        made.wait()
+    events(0, 0, 1)
+
+    def mlp(i):
+        sums.offer(i, 0, dot_t(mm[...], s2[col(i), :]))
+        pl.when(i > 0)(lambda: sums.pass_on(i - 1, 0))
+
+    run(8, mlp, (0, 1, 2))
+    sums.pass_on(7, 0)
+
+    def gate_up_tiles(i, slot):
+        r = col(i, 128)
+        return [(gate_all.at[r], tiles.at[slot, 0]), (up_all.at[r], tiles.at[slot, 1])]
+
+    def grad_gate_up(i, slot):
+        r = col(i, 128)
+        dm = dot(rows_all[r, :], s2[...]).astype(bf16).astype(f32)
+        g = tiles[slot, 0].astype(f32)
+        u = tiles[slot, 1].astype(f32)
+        s = jax.nn.sigmoid(g)
+        mm[r, :] = (dm * u * s * (1.0 + g * (1.0 - s))).astype(bf16)
+        dup[r, :] = (dm * (g * s)).astype(bf16)
+
+        def use(value):
+            bo[:, col(i)] = (x1[:, col(i)] + value).astype(bf16)
+
+        sums.take(i, 0, use)
+
+    got_x1.wait()
+    chunks_of(gate_up_tiles, 8, grad_gate_up, (0, 3, 4))
+    pending = [load(bo, block_out)]
+
+    def w_tiles(i, slot):
+        return [(wg_all.at[i], stream.at[slot, 0]), (wu_all.at[i], stream.at[slot, 1])]
+
+    def grad_hidden(i, slot):
+        value = dot_t(mm[...], stream[slot, 0]) + dot_t(dup[...], stream[slot, 1])
+        sums.offer(i, 1, value)
+        pl.when(i > 0)(lambda: sums.pass_on(i - 1, 1))
+
+    chunks_of(w_tiles, 8, grad_hidden, (0, 7, 2))
+    sums.pass_on(7, 1)
+
+    def h_tiles(everyone):
+        return lambda i, slot: [(everyone.at[:, col(i)], hs.at[slot])]
+
+    def grad_gate(i, slot):
+        s2[col(i), :] = dot_tt(hs[slot], mm[...]).astype(bf16)
+
+    chunks_of(h_tiles(h2_all), 8, grad_gate, (0, 9, 2))
+    events(0, 11, 12)
+    begin(1)
+
+    def take_second(i):
+        def use(value):
+            acc[:, col(i)] = value
+
+        sums.take(i, 1, use)
+
+    run(8, take_second, (0, 12, 2))
+    done = load(fout.at[:, pl.ds(0, ff)], d_out)
+
+    def norm_back_second(i, _):
+        r = pl.ds(pl.multiple_of(i * 32, 32), 32)
+        v = x1[r, :]
+        s = lax.rsqrt(jnp.mean(v * v, axis=1, keepdims=True) + epsilon)
+        n = v * s
+        dn = acc[r, :] * gains[1:2, :]
+        own = pl.ds(pl.multiple_of(tp * rows + i * 32, 32), 32)
+        back = rows_all[own, :].astype(f32) + s * (
+            dn - n * jnp.mean(dn * n, axis=1, keepdims=True)
+        )
+        acc[r, :] = back
+        own_rows[r, :] = back.astype(bf16)
+        return 0
+
+    lax.fori_loop(0, rows // 32, norm_back_second, 0)
+    da = Rows(links, own_rows, rows_all, tp, over_y, over_core, rows)
+    own_in = load(own_rows, da.block(tp, 0, rows))
+
+    def grad_up(i, slot):
+        s1[col(i), :] = dot_tt(hs[slot], dup[...]).astype(bf16)
+
+    chunks_of(h_tiles(h2_all), 8, grad_up, (1, 0, 2))
+    da.forward(0)
+    events(1, 2, 5)
+    da.forward(1)
+    for made in got_qkv + got_wo:
+        made.wait()
+    da.finish()
+    own_in.wait()
+    links.sent_now(da.first + [da.near])
+    got_x = load(x_in, own_rows)
+
+    def head_v(h):
+        return slice(128 + h * 128, 256 + h * 128)
+
+    def grad_attended(i):
+        r = col(i, 256)
+        dy = dot(rows_all[r, :], wo[...])
+        kq[r, :] = pltpu.roll(qkv[r, 0:128].astype(f32), 64, 1).astype(bf16)
+        columns = []
+        for h in range(4):
+            hv = slice(h * 128, (h + 1) * 128)
+            under = 1.0 / den[r, h : h + 1]
+            part_h = dy[:, hv]
+            dnum[r, hv] = (part_h * under).astype(bf16)
+            low = jnp.sum(part_h * yb[r, hv].astype(f32), axis=1, keepdims=True)
+            columns.append(-low * under)
+        lane = lax.broadcasted_iota(jnp.int32, (256, 128), 1)
+        packed = jnp.zeros((256, 128), f32)
+        for h in range(4):
+            packed = jnp.where(lane == h, columns[h], packed)
+        dden[r, :] = packed
+        dden_t[i] = packed.T[0:8, :]
+
+    run(4, grad_attended)
+    event(1, 5)
+
+    for h in range(4):
+
+        def state(i, c, h=h):
+            s, zz = c
+            r = col(i, 256)
+            a, b = phi(qkv[r, 0:128], h, sa_ref, sb_ref, lanes_ref)
+            f = a * b * lanes_ref[2:3, :] * tok_ref[r, 1:2]
+            s = s + dot_tt(f.astype(bf16), dnum[r, h * 128 : (h + 1) * 128])
+            return s, zz + jnp.sum(f * dden[r, h : h + 1], axis=0, keepdims=True)
+
+        s, zz = lax.fori_loop(
+            0, 4, state, (jnp.zeros((256, 128), f32), jnp.zeros((1, 256), f32))
+        )
+        pack_state(st, h, s, zz)
+    to_x = links.start(st, st_x, seq=seq + 1 - 2 * x)
+    event(1, 6)
+
+    dq[...] = jnp.zeros(dq.shape, f32)
+
+    def local_head(h):
+        hm = hm_ref[h : h + 1, :]
+        hv = slice(h * 128, (h + 1) * 128)
+        for j in range(total // 256):
+            k_rows = slice(j * 256, (j + 1) * 256)
+            dv_s = jnp.zeros((256, 128), f32)
+            dk_s = jnp.zeros((256, 128), f32)
+            for i in range(j, total // 256):
+                q_rows = slice(i * 256, (i + 1) * 256)
+                qm = (qkv[q_rows, 0:128].astype(f32) * hm).astype(bf16)
+                u = dot_t(kq[k_rows, :], qm)
+                keep = tok_ref[k_rows, 3:4] >= line_ref[1:2, q_rows]
+                if i == j:
+                    keep = keep & (tok_ref[k_rows, 3:4] <= line_ref[0:1, q_rows])
+                kap = jnp.where(keep, (0.5 * u + 1.0) * u + 1.0, 0.0).astype(bf16)
+                dn = dnum[q_rows, hv]
+                grad = dot_t(qkv[k_rows, head_v(h)], dn) + dden_t[i, h : h + 1, :]
+                du = jnp.where(keep, grad * (1.0 + u), 0.0).astype(bf16)
+                dv_s = dv_s + dot(kap, dn)
+                dk_s = dk_s + dot(du, qm)
+                dq[q_rows, :] += dot_tt(du, kq[k_rows, :]) * hm
+            dqkv[k_rows, head_v(h)] = dv_s.astype(bf16)
+            if h == 0:
+                dk[k_rows, :] = dk_s
+            else:
+                dk[k_rows, :] += dk_s
+
+    local_head(0)
+    to_x.wait_recv()
+    for h in range(4):
+        mine, theirs = st[h].astype(f32), st_x[h].astype(f32)
+        first = jnp.where(x == 0, mine, theirs)
+        second = jnp.where(x == 0, theirs, mine)
+        st_t[h] = (first + coef_ref[0:1, :] * second).astype(bf16)
+    to_z = [links.copy(st_t, st_z.at[d - 1], seq=seq - 2 * d) for d in (1, 2, 3)]
+    for d in (1, 2, 3):
+
+        @pl.when(z >= d)
+        def _(d=d):
+            to_z[d - 1].start()
+
+    events(1, 7, 8)
+    local_head(1)
+    events(1, 8, 9)
+    local_head(2)
+    events(1, 9, 10)
+    local_head(3)
+    events(1, 10, 12)
+    begin(2)
+    for h in range(4):
+        s_back[h, 0:176, :] = coef_ref[1:2, :] * st_x[h].astype(f32)
+        s_back[h, 176:256, :] = jnp.zeros((80, 128), f32)
+    for d in (1, 2, 3):
+
+        @pl.when(z + d < 4)
+        def _(d=d):
+            to_z[d - 1].wait_recv()
+            for h in range(4):
+                s_back[h, 0:176, :] += coef_ref[1 + d : 2 + d, :] * st_z[d - 1, h].astype(f32)
+
+    def split_state(ref, h):
+        z_row = jnp.concatenate([ref[h, 160:161, :], ref[h, 161:162, :]], axis=1)
+        feat = lax.broadcasted_iota(jnp.int32, (256, 128), 0)
+        return jnp.where(feat < FEATS, ref[h], 0.0).astype(bf16), z_row
+
+    for h in range(4):
+        s_q, z_q = split_state(s_in, h)
+        s_k, z_k = split_state(s_back, h)
+        hv = slice(h * 128, (h + 1) * 128)
+
+        def through(grad, a, b, h=h):
+            grad = grad * lanes_ref[2:3, :]
+            return dot_t((grad * b).astype(bf16), sa_ref[h]) + dot_t(
+                (grad * a).astype(bf16), sb_ref[h]
+            )
+
+        def carried_part(i, _, h=h, s_q=s_q, z_q=z_q, s_k=s_k, z_k=z_k, hv=hv, through=through):
+            r = col(i, 256)
+            a, b = phi(qkv[r, 0:128], h, sa_ref, sb_ref, lanes_ref)
+            grad = dot_t(dnum[r, hv], s_q) + dden[r, h : h + 1] * z_q
+            dq[r, :] += through(grad * tok_ref[r, 1:2], a, b)
+            a, b = phi(kq[r, :], h, sa_ref, sb_ref, lanes_ref)
+            last = tok_ref[r, 2:3]
+            grad = dot_t(qkv[r, head_v(h)], s_k) + z_k
+            dk[r, :] += through(grad * last, a, b)
+            f = (a * b * lanes_ref[2:3, :] * last).astype(bf16)
+            dqkv[r, head_v(h)] = (dqkv[r, head_v(h)].astype(f32) + dot(f, s_k)).astype(bf16)
+            return 0
+
+        lax.fori_loop(0, 4, carried_part, 0)
+
+    def join(i):
+        r = col(i, 256)
+        dqkv[r, 0:128] = (dq[r, :] + pltpu.roll(dk[r, :], 64, 1)).astype(bf16)
+
+    run(4, join)
+    done.wait()
+    events(1, 12, 14)
+    done = load(fout.at[:, pl.ds(0, ff)], g_out)
+
+    def wq_tiles(i, slot):
+        return [(wq_all.at[i], stream.at[slot, 0, :, pl.ds(0, 640)])]
+
+    def grad_hidden_first(i, slot):
+        sums.offer(i, 2, dot_t(dqkv[...], stream[slot, 0, :, 0:640]))
+        pl.when(i > 0)(lambda: sums.pass_on(i - 1, 2))
+
+    chunks_of(wq_tiles, 8, grad_hidden_first, (2, 0, 2))
+    sums.pass_on(7, 2)
+
+    def grad_out_qkv(i, slot):
+        s2[col(i), 0:512] = dot_tt(rows_all[:, col(i)], yb[...]).astype(bf16)
+        s2[col(i), 512:1152] = dot_tt(hs[slot], dqkv[...]).astype(bf16)
+
+    chunks_of(h_tiles(h1_all), 8, grad_out_qkv, (2, 2, 2))
+    events(2, 4, 6)
+    def take_first(i):
+        def use(value):
+            x1[:, col(i)] = value
+
+        sums.take(i, 2, use)
+
+    run(8, take_first, (2, 6, 2))
+    got_x.wait()
+
+    def norm_back_first(i, _):
+        r = pl.ds(pl.multiple_of(i * 32, 32), 32)
+        v = own_rows[r, :].astype(f32)
+        s = lax.rsqrt(jnp.mean(v * v, axis=1, keepdims=True) + epsilon)
+        n = v * s
+        dn = x1[r, :] * gains[0:1, :]
+        acc[r, :] += s * (dn - n * jnp.mean(dn * n, axis=1, keepdims=True))
+        return 0
+
+    lax.fori_loop(0, rows // 32, norm_back_first, 0)
+    pending.append(load(acc, input_out))
+    events(2, 8, 12)
+    begin(3)
+    done.wait()
+    events(2, 12, 14)
+    done = load(fout.at[:, pl.ds(0, ff)], u_out)
+    events(3, 0, 12)
+    done.wait()
+    events(3, 12, 14)
+    load(fout.at[:, pl.ds(0, 1152)], oq_out).wait()
+    run(8, lambda i: sums.sent(i))
+    for made in pending:
+        made.wait()
+    links.finish()
+    for d in (1, 2, 3):
+
+        @pl.when(z >= d)
+        def _(d=d):
+            to_z[d - 1].wait_send()
+
+
+def feature_tables(heads):
+    first = np.zeros((heads, 128, 256), np.float32)
+    second = np.zeros((heads, 128, 256), np.float32)
+    lanes = np.zeros((8, 256), np.float32)
+    f = 0
+    for i in range(FEAT):
+        for j in range(i, FEAT):
+            for h in range(heads):
+                first[h, h * FEAT + i, f] = 1
+                second[h, h * FEAT + j, f] = 1
+            lanes[2, f] = square_coef if i == j else square_coef * 2**0.5
+            f += 1
+    for i in range(FEAT):
+        for h in range(heads):
+            first[h, h * FEAT + i, f] = 1
+        lanes[1, f] = 1
+        lanes[2, f] = linear_coef
+        f += 1
+    lanes[0, f] = lanes[1, f] = lanes[2, f] = 1
+    mask = np.zeros((8, 128), np.float32)
+    for h in range(heads):
+        mask[h, h * FEAT : (h + 1) * FEAT] = 0.25
+    return first, second, lanes, mask
+
+
+def token_tables(lengths, seq_index, block_len, seq_count):
+    at = jnp.arange(lengths.shape[0])
+    starts = jnp.sum(jnp.where(at[None, :] < at[:, None], lengths[None, :], 0), axis=1)
+    anchor = seq_index * block_len
+    positions = anchor + jnp.arange(block_len, dtype=jnp.int32)
+    begun = starts[None, :] <= positions[:, None]
+    row_start = jnp.max(jnp.where(begun, starts[None, :], 0), axis=1)
+    carry_in = row_start < anchor
+    later = (starts[None, :] > positions[:, None]) & (starts[None, :] < anchor + block_len)
+    after_last = jnp.sum(later.astype(jnp.int32), axis=1) == 0
+    place = jnp.arange(block_len, dtype=jnp.int32)
+    tok = jnp.stack(
+        [
+            jnp.maximum(row_start - anchor, 0).astype(f32),
+            carry_in.astype(f32),
+            after_last.astype(f32),
+            place.astype(f32),
+        ],
+        axis=1,
+    )
+    line = jnp.concatenate([tok[:, 3][None], tok[:, 0][None], jnp.zeros((6, block_len), f32)])
+    resets = (
+        jnp.sum(
+            ((starts // block_len)[None, :] == jnp.arange(seq_count)[:, None]).astype(jnp.int32),
+            axis=1,
+        )
+        > 0
+    ).astype(jnp.int32)
+
+    def clear(first, last):
+        blocks = jnp.arange(seq_count)
+        inside = (blocks >= first) & (blocks <= last)
+        return (jnp.sum(jnp.where(inside, resets, 0)) == 0).astype(f32)
+
+    z, x = seq_index // 2, seq_index % 2
+    coefs = [clear(2 * z + 1, 2 * z + 1), (x == 1).astype(f32)]
+    coefs += [clear(2 * (z - d) + 2, seq_index - 1) for d in (1, 2, 3)]
+    coefs += [jnp.zeros((), f32)] * 3
+    back = [clear(2 * z, 2 * z), (x == 0).astype(f32)]
+    back += [clear(seq_index + 1, 2 * (z + d) - 1) for d in (1, 2, 3)]
+    back += [jnp.zeros((), f32)] * 3
+
+    def wide(values):
+        return jnp.broadcast_to(jnp.stack(values)[:, None], (8, 128))
+
+    return tok, line, wide(coefs), wide(back)
+
+
+def forward_pass(tables, x_own, c_own, gain_own, q_own, o_own, g_own, u_own, d_own):
+    rows, width = x_own.shape
+    total = 4 * rows
+    ff = g_own.shape[1]
+    hbm = pl.BlockSpec(memory_space=pl.ANY)
+    vmem = pl.BlockSpec(memory_space=pltpu.VMEM)
+
+    def shape(*dims, dtype=bf16):
+        return jax.ShapeDtypeStruct(dims, dtype)
+
+    outs = (
+        shape(8, 256, q_own.shape[1]),
+        shape(8, 256, o_own.shape[1]),
+        shape(8, 256, ff),
+        shape(8, 256, ff),
+        shape(8, 256, ff),
+        shape(total, width),
+        shape(total, width),
+        shape(total, q_own.shape[1]),
+        shape(total, 512),
+        shape(total, 128, dtype=f32),
+        shape(rows, width, dtype=f32),
+        shape(total, width),
+        shape(total, ff),
+        shape(total, ff),
+        shape(total, ff),
+        shape(4, 256, 128, dtype=f32),
+        shape(8, width, dtype=f32),
+    )
+    scratch = [
+        pltpu.VMEM((total, width), bf16),
+        pltpu.VMEM((total, width), bf16),
+        pltpu.VMEM((width, q_own.shape[1]), bf16),
+        pltpu.VMEM((width, o_own.shape[1]), bf16),
+        pltpu.VMEM((width, ff), bf16),
+        pltpu.VMEM((width, ff), bf16),
+        pltpu.VMEM((total, q_own.shape[1]), bf16),
+        pltpu.VMEM((total, 128), bf16),
+        pltpu.VMEM((total, 512), f32),
+        pltpu.VMEM((total, 128), f32),
+        pltpu.VMEM((total, 512), bf16),
+        pltpu.VMEM((2, rows, width), bf16),
+        pltpu.VMEM((2, rows, width), bf16),
+        pltpu.VMEM((rows, width), bf16),
+        pltpu.VMEM((rows, width), bf16),
+        pltpu.VMEM((rows, width), f32),
+        pltpu.VMEM((total, width), bf16),
+        pltpu.VMEM((total, ff), bf16),
+        pltpu.VMEM((total, ff), bf16),
+        pltpu.VMEM((total, ff), bf16),
+        pltpu.VMEM((8, 16, 256), bf16),
+        pltpu.VMEM((8, width), f32),
+        pltpu.VMEM((4, 176, 128), bf16),
+        pltpu.VMEM((4, 176, 128), bf16),
+        pltpu.VMEM((4, 176, 128), bf16),
+        pltpu.VMEM((3, 4, 176, 128), bf16),
+        pltpu.VMEM((4, 256, 128), f32),
+        pltpu.VMEM((rows, width), bf16),
+        pltpu.SemaphoreType.DMA((112,)),
+        pltpu.SemaphoreType.DMA((112,)),
+        pltpu.SemaphoreType.DMA((64,)),
+    ]
+    return pl.pallas_call(
+        fwd_kernel,
+        out_shape=outs,
+        in_specs=[vmem] * 8 + [vmem] + [hbm] * 6,
+        out_specs=(hbm,) * len(outs),
+        scratch_shapes=scratch,
+        compiler_params=pltpu.CompilerParams(
+            collective_id=0, has_side_effects=True, vmem_limit_bytes=60 * 2**20
+        ),
+    )(
+        x_own, *tables, gain_own, q_own, o_own, g_own, u_own, d_own, c_own,
+    )
+
+
+def backward_pass(tables, gains, x_own, x1, s_in, den, weights, c_all, acts):
+    rows, width = x_own.shape
+    total = 4 * rows
+    ff = weights[2].shape[2]
+    hbm = pl.BlockSpec(memory_space=pl.ANY)
+    vmem = pl.BlockSpec(memory_space=pltpu.VMEM)
+
+    def shape(*dims, dtype=f32):
+        return jax.ShapeDtypeStruct(dims, dtype)
+
+    outs = (
+        shape(256, ff),
+        shape(256, ff),
+        shape(256, ff),
+        shape(256, 1152),
+        shape(rows, width, dtype=bf16),
+        shape(rows, width),
+    )
+    scratch = [
+        pltpu.VMEM((8, 256, ff), bf16),
+        pltpu.VMEM((width, ff), bf16),
+        pltpu.VMEM((width, ff), bf16),
+        pltpu.VMEM((width, 512), bf16),
+        pltpu.VMEM((2, 2, 256, ff), bf16),
+        pltpu.VMEM((2, total, 256), bf16),
+        pltpu.VMEM((total, width), bf16),
+        pltpu.VMEM((total, ff), bf16),
+        pltpu.VMEM((total, ff), bf16),
+        pltpu.VMEM((2, 2, 128, ff), bf16),
+        pltpu.VMEM((total, 640), bf16),
+        pltpu.VMEM((total, 128), bf16),
+        pltpu.VMEM((total, 512), bf16),
+        pltpu.VMEM((total, 512), bf16),
+        pltpu.VMEM((total, 128), f32),
+        pltpu.VMEM((4, 8, 256), f32),
+        pltpu.VMEM((total, 640), bf16),
+        pltpu.VMEM((total, 128), f32),
+        pltpu.VMEM((total, 128), f32),
+        pltpu.VMEM((8, 4, 256, 256), bf16),
+        pltpu.VMEM((8, 2, 256, 256), bf16),
+        pltpu.VMEM((8, 256, 256), bf16),
+        pltpu.VMEM((rows, width), f32),
+        pltpu.VMEM((rows, width), f32),
+        pltpu.VMEM((rows, width), bf16),
+        pltpu.VMEM((256, ff), f32),
+        pltpu.VMEM((4, 176, 128), bf16),
+        pltpu.VMEM((4, 176, 128), bf16),
+        pltpu.VMEM((4, 176, 128), bf16),
+        pltpu.VMEM((3, 4, 176, 128), bf16),
+        pltpu.VMEM((4, 256, 128), f32),
+        pltpu.VMEM((rows, width), bf16),
+        pltpu.SemaphoreType.DMA((2, 2, 2)),
+        pltpu.SemaphoreType.DMA((2, 2, 2, 7)),
+        pltpu.SemaphoreType.DMA((6, 8)),
+        pltpu.SemaphoreType.REGULAR((2,)),
+        pltpu.SemaphoreType.DMA((16,)),
+        pltpu.SemaphoreType.DMA((16,)),
+        pltpu.SemaphoreType.DMA((48,)),
+        pltpu.SemaphoreType.DMA((2, 2)),
+    ]
+    return pl.pallas_call(
+        bwd_kernel,
+        out_shape=outs,
+        in_specs=[vmem] * 8 + [hbm] * 2 + [vmem] * 2 + [hbm] * 13,
+        out_specs=(hbm,) * len(outs),
+        scratch_shapes=scratch,
+        compiler_params=pltpu.CompilerParams(
+            collective_id=1, has_side_effects=True, vmem_limit_bytes=62 * 2**20
+        ),
+    )(*tables, gains, x_own, x1, s_in, den, *weights, c_all, *acts)
+
+def on_device_rings(
+    inputs, lengths, gain_attn, w_query, w_key, w_value, w_out, gain_mlp, w_gate, w_up, w_down,
+    cotangent,
+):
+    seq_count = 8
+    seq_index = lax.axis_index("seq")
+    rows, width = inputs.shape
+    chunk = width // seq_count
+    relative = relative_list(seq_count)
+    ring = ring_order(seq_count)
+    place_of = [ring.index(s) for s in range(seq_count)]
+    to_rel = jnp.array(
+        [[ring[(place_of[s] - k) % seq_count] for k in relative] for s in range(seq_count)],
+        jnp.int32,
+    )[seq_index]
+    to_abs = jnp.array(
+        [
+            [relative.index((place_of[s] - place_of[o]) % seq_count) for o in range(seq_count)]
+            for s in range(seq_count)
+        ],
+        jnp.int32,
+    )[seq_index]
+    to_rel = [to_rel[j] for j in range(seq_count)]
+    to_abs = [to_abs[j] for j in range(seq_count)]
+
+    gains = jnp.stack([gain_attn, gain_mlp]).astype(bf16)
+    gain_own = jnp.zeros((16, chunk), bf16).at[:2].set(gains)
+    qkv_own = jnp.concatenate([w_query, w_key, w_value], axis=1).astype(bf16)
+    out_own = w_out.astype(bf16).T
+    gate_own, up_own = w_gate.astype(bf16), w_up.astype(bf16)
+    down_own = w_down.astype(bf16).T
+    x_own = to_relative(inputs, to_rel, chunk)
+    c_own = to_relative(cotangent, to_rel, chunk)
+
+    tok, line, coefs, back = token_tables(lengths, seq_index, 4 * rows, seq_count)
+    first, second, lanes, mask = feature_tables(4)
+    tables = (
+        tok, line, jnp.asarray(first, bf16), jnp.asarray(second, bf16), jnp.asarray(lanes),
+        jnp.asarray(mask),
+    )
+    made = forward_pass(
+        (*tables, coefs), x_own, c_own, gain_own, qkv_own, out_own, gate_own, up_own, down_own
+    )
+    weights, (c_all, h1, qkv, yb, den, x1, h2, gate, up, mixed, s_in, gain_all) = made[:5], made[5:]
+    sum_down_t, sum_gate, sum_up, sum_oq, block, grad_input = backward_pass(
+        (*tables, back), gain_all, x_own, x1, s_in, den, weights, c_all,
+        (h1, qkv, yb, h2, gate, up, mixed),
+    )
+
+    sum_qkv = sum_oq[:, 512:]
+    gain_terms = jnp.stack(
+        [
+            jnp.sum(qkv_own.astype(f32) * sum_qkv, axis=1),
+            jnp.sum(gate_own.astype(f32) * sum_gate + up_own.astype(f32) * sum_up, axis=1),
+        ]
+    )
+    gain_sums = tp_sum(gain_terms) / gains.astype(f32)
+    qk_cols = w_query.shape[1]
+    return (
+        to_relative(block, to_abs, chunk),
+        to_relative(grad_input, to_abs, chunk),
+        gain_sums[0],
+        sum_qkv[:, :qk_cols],
+        sum_qkv[:, qk_cols : 2 * qk_cols],
+        sum_qkv[:, 2 * qk_cols :],
+        sum_oq[:, :512].T,
+        gain_sums[1],
+        sum_gate,
+        sum_up,
+        sum_down_t.T,
+    )
 
 
 def on_device(
@@ -488,6 +1757,8 @@
         P("seq", "tp"),
         P("tp", "seq"),
     )
+    small = mesh.shape["seq"] == 8 and mesh.shape["tp"] == 4
+    body = on_device_rings if small else on_device
     return jax.shard_map(
-        on_device, mesh=mesh, in_specs=in_specs, out_specs=out_specs, check_vma=False
-    )
+        body, mesh=mesh, in_specs=in_specs, out_specs=out_specs, check_vma=False
+    )

time: 841 us -> 647 us (0.77)
  Pallas kernels: 0 us -> 548 us
  waiting for transfers between devices: 308 us -> 0.01 us
  matrix products: 174 us -> 0 us
  starting transfers between devices: 167 us -> 1.59 us
  other arithmetic: 80.7 us -> 9.38 us
  local copies, waits for them, and re-layouts: 85.7 us -> 62.3 us
    pallas_call x0 -> x2, Pallas kernels: none -> 548 us  [the longest x1 275 us: forward_pass(): pl.pallas_call(fwd_kernel, out_shape=outs, in_specs=[vmem] * 8 + [vmem] +...]
    ppermute x120 -> x0, waiting for transfers between devices: 291 us -> none  [the longest x28 83.6 us: ring_scatter(): ahead = lax.ppermute(ahead, 'seq', fwd).astype(f32)]
    dot_general x32 -> x0, matrix products: 174 us -> none  [the longest x4 45.3 us: dot(): return jnp.dot(a, b, preferred_element_type=f32)]
    ppermute x120 -> x0, starting transfers between devices: 167 us -> none  [the longest x16 43.8 us: from_near(): return lax.ppermute(a.astype(bf16), 'seq', perm).astype(f32)]
    convert_element_type x43 -> x5, other arithmetic: 20.1 us -> 1.5 us  [the longest x1 1.48 us: on_device_rings(): down_own = w_down.astype(bf16).T]
    unnamed x286 -> x79, local copies, waits for them, and re-layouts: 66.2 us -> 47.6 us
    ppermute x1, waiting for transfers between devices: 16.6 us -> 0.01 us  [tp_sum(): lax.ppermute(vector, 'tp', shift[d])]
    another operation x22 -> x8, other arithmetic: 17.5 us -> 1.71 us  [the longest x8 7.59 us: tp_gather(): jnp.stack([lax.select_n((y - at + ys) % ys, *parts) for at in range(ys)])]
  transfers between devices with their start and end apart: 122 -> 2, of which waited for: 62 -> 0; matrix products, arithmetic and copies ran while one was open for 29% -> 5% of each run, Pallas kernels for 0% -> 0%
where the time goes in v2:
time: 647 us; the launch traced here: 638 us
  Pallas kernels  548 us (85%)
  local copies, waits for them, and re-layouts  62.3 us (10%)
  between operations  17.2 us (3%)
  other arithmetic  9.38 us (1%)
    pallas_call x1, Pallas kernels, forward_pass(): pl.pallas_call(fwd_kernel, out_shape=outs, in_specs=[vmem] * 8 + [vmem] +...  275 us
    pallas_call x1, Pallas kernels, backward_pass(): pl.pallas_call(bwd_kernel, out_shape=outs, in_specs=[vmem] * 8 + [hbm] *...  273 us
    unnamed x79, local copies, waits for them, and re-layouts  47.6 us
  transfers between devices with their start and end apart: 2, of which 0 were waited for; matrix products, arithmetic and copies ran while one was open for 5% of the time, Pallas kernels for 0%

profile of v2, /device:TPU:0, one launch (start us, length us, event | category | flops | bytes accessed | tf_op | source)
XLA Modules:
  0.0 638.0 jit_solution(1469020502653782632)
XLA Ops:
  7.3 1.6 dynamic-slice_dynamic-update-slice_fusion.23
  9.8 1.6 dynamic-slice_dynamic-update-slice_fusion.22
  12.3 1.6 dynamic-slice_dynamic-update-slice_fusion.21
  14.8 1.6 dynamic-slice_dynamic-update-slice_fusion.20
  17.4 1.6 dynamic-slice_dynamic-update-slice_fusion.19
  19.9 1.6 dynamic-slice_dynamic-update-slice_fusion.18
  22.4 1.6 dynamic-slice_dynamic-update-slice_fusion.17
  24.9 1.6 dynamic-slice_dynamic-update-slice_fusion.16.c_own
  34.8 2.5 copy.88.u_own
  46.4 274.5 %shard_map.257 = (bf16[8,256,640]{2,1,0:T(8,128)(2,1)}, bf16[8,256,512]{2,1,0:T(8,128)(2,1)}, bf16[8,256,1376]{2,1,0:T(8,128)(2,1)}, bf16[8,256,1376]{2,1,0:T(8,...) custom-call(bf16[256,2048]{1,0:T(8,128)(2,1)} %copy-done.4, ...), custom_call_target="tpu_custom_call" | custom-call | tf_op jit(solution)/shard_map/pallas_call | solution.py:1333
  321.6 273.0 %shard_map.258 = (f32[256,1376]{1,0:T(8,128)}, f32[256,1376]{1,0:T(8,128)}, f32[256,1376]{1,0:T(8,128)}, f32[256,1152]{1,0:T(8,128)}, bf16[256,2048]{1,0:T(8,128)(2,1)}, /*index=5*/f32[256,2048]{1,0:T(8,128)}) custom-call(f32[1024,4]{1,0:T(8,128)} %copy.91.tok_ref, f32[8,1024]{1,0:T(8,128)} %maximum_maximum_fusion.line_ref, ...), custom_call_target="tpu_custom_call" | custom-call | tf_op jit(solution)/shard_map/pallas_call | solution.py:1407
  596.0 2.3 add_reduce_fusion
  607.3 1.6 dynamic-slice_dynamic-update-slice_fusion.15
  609.6 1.6 dynamic-slice_dynamic-update-slice_fusion.14
  611.9 1.7 dynamic-slice_dynamic-update-slice_fusion.13
  614.3 1.6 dynamic-slice_dynamic-update-slice_fusion.12
  616.5 1.6 dynamic-slice_dynamic-update-slice_fusion.11
  618.8 1.6 dynamic-slice_dynamic-update-slice_fusion.10
  620.4 1.8 dynamic-slice_dynamic-update-slice_fusion.1
  622.2 1.7 dynamic-slice_dynamic-update-slice_fusion
  623.9 1.6 dynamic-slice_dynamic-update-slice_fusion.9
  625.4 1.6 collective-permute-start.1
  627.0 1.6 dynamic-slice_dynamic-update-slice_fusion.8
  632.7 2.9 copy.97
  (111 shorter events, 35.3 us)
Async XLA Ops:
  7.3 20.2 %copy-start.20 = (s32[3]{0:T(128)S(1)}, s32[3]{0:T(128)}, u32[]{:S(2)}) copy-start(s32[3]{0:T(128)} %param.21) | copy-start | bytes 40
  14.8 18.6 %copy-start.12 = (f32[256,64]{0,1:T(8,128)S(1)}, f32[256,64]{0,1:T(8,128)}, u32[]{:S(2)}) copy-start(f32[256,64]{0,1:T(8,128)} %param.23) | copy-start | bytes 196612
  14.8 18.7 %copy-start.13 = (f32[256,64]{0,1:T(8,128)S(1)}, f32[256,64]{0,1:T(8,128)}, u32[]{:S(2)}) copy-start(f32[256,64]{0,1:T(8,128)} %param.24) | copy-start | bytes 196612
  16.4 17.2 %copy-start.18 = (f32[256]{0:T(256)S(1)}, f32[256]{0:T(256)}, u32[]{:S(2)}) copy-start(f32[256]{0:T(256)} %param.22) | copy-start | bytes 3076
  16.4 17.2 %copy-start.19 = (f32[256]{0:T(256)S(1)}, f32[256]{0:T(256)}, u32[]{:S(2)}) copy-start(f32[256]{0:T(256)} %param.27) | copy-start | bytes 3076
  16.4 17.3 %copy-start.8 = (f32[256,1376]{0,1:T(8,128)S(1)}, f32[256,1376]{0,1:T(8,128)}, u32[]{:S(2)}) copy-start(f32[256,1376]{0,1:T(8,128)} %param.28) | copy-start | bytes 4227076
  27.4 9.9 %copy-start.4 = (bf16[256,2048]{1,0:T(8,128)(2,1)}, bf16[256,2048]{1,0:T(8,128)(2,1)S(1)}, u32[]{:S(2)}) copy-start(bf16[256,2048]{1,0:T(8,128)(2,1)S(1)} %dynamic-slice_dynamic-update-slice_fusion.24.x_ref.x_in) | copy-start | bytes 3145732
  33.6 9.8 %copy-start.14 = (bf16[1,256]{1,0:T(2,128)(2,1)}, bf16[1,256]{1,0:T(2,128)(2,1)S(1)}, u32[]{:S(2)}) copy-start(bf16[1,256]{1,0:T(2,128)(2,1)S(1)} %stack.117) | copy-start | bytes 1540
  33.7 9.8 %copy-start.16 = (bf16[1,256]{1,0:T(2,128)(2,1)}, bf16[1,256]{1,0:T(2,128)(2,1)S(1)}, u32[]{:S(2)}) copy-start(bf16[1,256]{1,0:T(2,128)(2,1)S(1)} %stack.118) | copy-start | bytes 1540
  37.3 2.6 copy-start.9
  321.6 274.4 %copy-start = (bf16[256,1376]{1,0:T(8,128)(2,1)S(1)}, bf16[256,1376]{1,0:T(8,128)(2,1)}, u32[]{:S(2)}) copy-start(bf16[256,1376]{1,0:T(8,128)(2,1)} %copy.87.g_own) | copy-start | bytes 2113540
  321.6 274.4 %copy-start.1 = (bf16[256,1376]{1,0:T(8,128)(2,1)S(1)}, bf16[256,1376]{1,0:T(8,128)(2,1)}, u32[]{:S(2)}) copy-start(bf16[256,1376]{1,0:T(8,128)(2,1)} %copy.88.u_own) | copy-start | bytes 2113540
  596.0 8.7 %copy-start.5 = (f32[256,1152]{1,0:T(8,128)S(1)}, f32[256,1152]{1,0:T(8,128)}, u32[]{:S(2)}) copy-start(f32[256,1152]{1,0:T(8,128)} %get-tuple-element.65) | copy-start | bytes 3538948
  598.3 8.3 %copy-start.6 = (f32[256,2048]{1,0:T(8,128)S(1)}, f32[256,2048]{1,0:T(8,128)}, u32[]{:S(2)}) copy-start(f32[256,2048]{1,0:T(8,128)} %get-tuple-element.64) | copy-start | bytes 6291460
  598.9 26.6 %collective-permute-start = (f32[2,256]{1,0:T(2,128)}, f32[2,256]{1,0:T(2,128)S(1)}, u32[]{:S(2)}, u32[]{:S(2)}) collective-permute-start(f32[2,256]{1,0:T(2,128)} %pad_maximum_fusion.2), channel_id=1, source_target_pairs={{0,1},{1,0},{2,3},{3,2},{4,5},{5,4},{6,7},{7,6},{8,9},{9,8},{10,11... | collective-permute-start | bytes 6152 | tf_op jit(solution)/shard_map/ppermute | solution.py:131
  611.9 16.7 %copy-start.3 = (f32[256,1376]{1,0:T(8,128)S(1)}, f32[256,1376]{1,0:T(8,128)}, u32[]{:S(2)}) copy-start(f32[256,1376]{1,0:T(8,128)} %get-tuple-element.121) | copy-start | bytes 4227076
  620.4 9.7 %copy-start.2 = (f32[256,1376]{1,0:T(8,128)S(1)}, f32[256,1376]{1,0:T(8,128)}, u32[]{:S(2)}) copy-start(f32[256,1376]{1,0:T(8,128)} %get-tuple-element.122) | copy-start | bytes 4227076
  625.4 11.5 %collective-permute-start.1 = (f32[2,256]{1,0:T(2,128)S(1)}, f32[2,256]{1,0:T(2,128)S(1)}, u32[]{:S(2)}, u32[]{:S(2)}) collective-permute-start(f32[2,256]{1,0:T(2,128)S(1)} %fusion.8), channel_id=1, source_target_pairs={{0,2},{1,3},{2,0},{3,1},{4,6},{5,7},{6,4},{7,5},{8,10},{9,11},{10,... | collective-permute-start | bytes 6152 | tf_op jit(solution)/shard_map/ppermute | solution.py:132
  630.1 1.5 copy-start.7
  631.6 3.9 copy-start.11
  631.6 4.6 copy-start.10
  631.6 5.3 copy-start.15
  631.6 5.3 copy-start.17

commit v3 on v2

--- a/solution.py
+++ b/solution.py
@@ -369,6 +369,57 @@
 FEATS = 160
 
 
+def fill_tables(lengths, seq, tok, line, coefs, step):
+    total = tok.shape[0]
+    anchor = seq * total
+    starts, at = [], 0
+    for i in range(lengths.shape[0]):
+        starts.append(at)
+        at = at + lengths[i]
+
+    def places_of(shape, axis):
+        pos = lax.broadcasted_iota(jnp.int32, shape, axis)
+        low = jnp.zeros(shape, jnp.int32) - anchor
+        last = jnp.ones(shape, f32)
+        for start in starts:
+            here = start - anchor
+            low = jnp.maximum(low, jnp.where(pos >= here, here, -anchor))
+            last = jnp.where((pos < here) & (here < total), 0.0, last)
+        return pos.astype(f32), low, last
+
+    lane = lax.broadcasted_iota(jnp.int32, (total, 128), 1)
+    pos, low, last = places_of((total, 128), 0)
+    began = jnp.where(low < 0, 1.0, 0.0)
+    first = jnp.maximum(low, 0).astype(f32)
+    tok[...] = jnp.where(
+        lane == 0, first, jnp.where(lane == 1, began, jnp.where(lane == 2, last, pos))
+    )
+    pos, low, last = places_of((8, total), 1)
+    row = lax.broadcasted_iota(jnp.int32, (8, total), 0)
+    line[...] = jnp.where(row == 0, pos, jnp.maximum(low, 0).astype(f32))
+
+    def clear(lo, hi):
+        free = jnp.ones((1, 128), f32)
+        for start in starts:
+            at = jnp.zeros((1, 128), jnp.int32) + start
+            free = jnp.where((at >= lo * total) & (at < (hi + 1) * total), 0.0, free)
+        return free
+
+    z, x = seq // 2, seq % 2
+    one = jnp.ones((1, 128), f32)
+    if step > 0:
+        rows = [clear(2 * z + 1, 2 * z + 1), one * x.astype(f32)]
+        rows += [clear(2 * (z - d) + 2, seq - 1) for d in (1, 2, 3)]
+    else:
+        rows = [clear(2 * z, 2 * z), one * (1 - x).astype(f32)]
+        rows += [clear(seq + 1, 2 * (z + d) - 1) for d in (1, 2, 3)]
+    coefs[...] = jnp.concatenate(rows + [one * 0.0] * 3, axis=0)
+
+
+def ring_columns(place):
+    return [pl.ds(pl.multiple_of(ring_seq(place - k) * 256, 256), 256) for k in relative_list(8)]
+
+
 def phi(heads, h, select_a, select_b, lanes):
     a = dot(heads, select_a[h]) + lanes[0:1, :]
     b = dot(heads, select_b[h]) + lanes[1:2, :]
@@ -376,12 +427,14 @@
 
 
 def fwd_kernel(
-    x_ref, tok_ref, line_ref, sa_ref, sb_ref, lanes_ref, hm_ref, coef_ref,
-    gain_ref, q_own, o_own, g_own, u_own, d_own, c_own,
+    lengths, sa_ref, sb_ref, lanes_ref, hm_ref, gain_first, gain_second,
+    x_in, wq_in, wk_in, wv_in, wo_in, wg_in, wu_in, wd_in, c_in,
     wq_all, wo_all, wg_all, wu_all, wd_all, c_all,
     h1_out, qkv_out, yb_out, den_out, x1_out, h2_out, gate_out, up_out, m_out, sin_out, gain_out,
-    xg, h1, wq, wo, wg, wu, qkv, kq, num, den, yb, sc, rc, sy, ry, x1, h2, gate, up, mm,
-    gains_all, gains, st, st_x, st_t, st_z, s_in, ho,
+    x_ref, tok_ref, line_ref, coef_ref, gain_ref, q_own, o_own, g_own, u_own, d_own,
+    w_small, w_v, w_o, w_d, w_g,
+    xg, h1, wq, wo, wg, wu, qkv, kq, num, den, yb, sc, rc, sy, ry, x1, gate, up, mm,
+    gains_all, gains, st, st_x, st_t, st_z, s_in,
     send, recv, local,
 ):
     seq, tp, place, nearby, over_y, over_core, peers = places()
@@ -403,23 +456,58 @@
         made.start()
         return made
 
+    got_qk = [load(wq_in, w_small.at[0:64]), load(wk_in, w_small.at[64:128]), load(wv_in, w_v)]
+    columns = ring_columns(place)
+    got_x = [load(x_in.at[:, c], x_ref.at[:, col(j)]) for j, c in enumerate(columns)]
+    c_rows = pl.ds(pl.multiple_of(tp * rows, rows), rows)
+    got_c = [load(c_in.at[:, c], c_all.at[c_rows, col(j)]) for j, c in enumerate(columns)]
+    got_o = load(wo_in, w_o)
+    ff = wd_in.shape[0]
+    got_g = load(wg_in, w_g.at[pl.ds(0, ff)])
+    got_d = load(wd_in, w_d.at[pl.ds(0, ff)])
+
+    def turn(src, dst):
+        for i in range(0, ff, 128):
+            size = min(128, ff - i)
+            dst[:, i : i + size] = src[i : i + 128, :].T[:, :size].astype(bf16)
+
+    gain_ref[...] = jnp.concatenate(
+        [gain_first[...], gain_second[...], jnp.zeros((14, 256), f32)], axis=0
+    ).astype(bf16)
     greet(peers)
     gain_flying = [
         links.start(gain_ref, gains_all.at[at[k]], seq=ring_seq(place + k)) for k in range(1, 8)
     ]
+    for made in got_x:
+        made.wait()
+    xrows = Rows(links, x_ref, xg, tp, over_y, over_core, rows)
+    for made in got_qk:
+        made.wait()
+    q_own[:, 0:128] = w_small[...].T.astype(bf16)
+    q_own[:, 128:640] = w_v[...].astype(bf16)
     ring = Gather(
         links,
         [(q_own, wq_all), (o_own, wo_all), (g_own, wg_all), (u_own, wu_all), (d_own, wd_all)],
         128,
         nearby,
     )
-    xrows = Rows(links, x_ref, xg, tp, over_y, over_core, rows)
     own_in = [
         load(x_ref, xrows.block(tp, 0, rows)),
         load(gain_ref, gains_all.at[at[0]]),
     ]
+    got_o.wait()
+    o_own[...] = w_o[...].T.astype(bf16)
+    ring.pump(2)
+    got_g.wait()
+    turn(w_g, g_own)
+    got_u = load(wu_in, w_g.at[pl.ds(0, ff)])
+    ring.pump(4)
+    got_d.wait()
+    turn(w_d, d_own)
+    got_u.wait()
+    turn(w_g, u_own)
     own_kept = [load(own, everyone.at[at[0]]) for own, everyone in ring.arrays]
-    store(c_own, c_all.at[pl.ds(pl.multiple_of(tp * rows, rows), rows)])
+    fill_tables(lengths, seq, tok_ref, line_ref, coef_ref, 1)
 
     ring.pump(6)
     xrows.forward(0)
@@ -445,8 +533,11 @@
         return 0
 
     lax.fori_loop(0, total // 32, norm_first, 0)
+    links.sent_now(xrows.last)
     store(h1, h1_out)
-    crows = Rows(links, c_own, c_all, tp, over_y, over_core, rows)
+    for made in got_c:
+        made.wait()
+    crows = Rows(links, c_all.at[c_rows], c_all, tp, over_y, over_core, rows)
     ring.pump(15)
     for made in got:
         made.wait()
@@ -596,6 +687,9 @@
     ring.pump(34)
     to_y.wait_recv()
 
+    links.sent_now(xrows.first + [xrows.near])
+    ho = x_ref
+
     def norm_second(i, _):
         r = pl.ds(pl.multiple_of(i * 32, 32), 32)
         v = x1[r, :] + ry[r, :].astype(f32)
@@ -607,6 +701,7 @@
     lax.fori_loop(0, rows // 32, norm_second, 0)
     store(x1, x1_out)
     store(gains, gain_out)
+    h2 = xg
     hrows = Rows(links, ho, h2, tp, over_y, over_core, rows)
     own_in = load(ho, hrows.block(tp, 0, rows))
     ring.pump(36)
@@ -808,12 +903,13 @@
 
 
 def bwd_kernel(
-    tok_ref, line_ref, sa_ref, sb_ref, lanes_ref, hm_ref, coef_ref, gains, x_in, x1_in, s_in, den,
-    wq_all, wo_all, wg_all, wu_all, wd_all, c_all, h1_all, qkv_all, yb_all, h2_all,
+    lengths, sa_ref, sb_ref, lanes_ref, hm_ref, gains, s_in, den, gain_first, gain_second,
+    x_in, x1_in, wq_all, wo_all, wg_all, wu_all, wd_all, c_all, h1_all, qkv_all, yb_all, h2_all,
     gate_all, up_all, m_all,
-    d_out, g_out, u_out, oq_out, block_out, input_out,
+    d_out, g_out, u_out, oq_out, block_out, input_out, gain_out,
+    tok_ref, line_ref, coef_ref, terms, terms_core, terms_y,
     slots, s1, s2, wo, stream, hs, rows_all, mm, dup, tiles, qkv, kq, yb, dnum, dden, dden_t, dqkv,
-    dq, dk, part, from_core, from_y, acc, x1, bo, fout, st, st_x, st_t, st_z, s_back, own_rows,
+    dq, dk, part, from_core, from_y, acc, x1, fout, st, st_x, st_t, st_z, s_back, own_rows,
     ring_send, ring_recv, tp_sems, credits, send, recv, local, tile_sems,
 ):
     seq, tp, place, nearby, over_y, over_core, peers = places()
@@ -838,6 +934,8 @@
     got_wd = whole(wd_all, s2)
     greet(peers)
     got_x1 = load(x1_in, x1)
+    fill_tables(lengths, seq, tok_ref, line_ref, coef_ref, -1)
+    columns = ring_columns(place)
     got_qkv = [load(qkv_all, qkv), load(yb_all, yb)]
     got_wo = whole(wo_all, wo)
     ring = Scatter(slots, ring_send, ring_recv, nearby)
@@ -925,13 +1023,14 @@
         dup[r, :] = (dm * (g * s)).astype(bf16)
 
         def use(value):
-            bo[:, col(i)] = (x1[:, col(i)] + value).astype(bf16)
+            own_rows[:, col(i)] = (x1[:, col(i)] + value).astype(bf16)
 
         sums.take(i, 0, use)
 
     got_x1.wait()
     chunks_of(gate_up_tiles, 8, grad_gate_up, (0, 3, 4))
-    pending = [load(bo, block_out)]
+    kept = [load(own_rows.at[:, col(j)], block_out.at[:, c]) for j, c in enumerate(columns)]
+    pending = []
 
     def w_tiles(i, slot):
         return [(wg_all.at[i], stream.at[slot, 0]), (wu_all.at[i], stream.at[slot, 1])]
@@ -962,6 +1061,9 @@
 
     run(8, take_second, (0, 12, 2))
     done = load(fout.at[:, pl.ds(0, ff)], d_out)
+
+    for made in kept:
+        made.wait()
 
     def norm_back_second(i, _):
         r = pl.ds(pl.multiple_of(i * 32, 32), 32)
@@ -993,7 +1095,7 @@
     da.finish()
     own_in.wait()
     links.sent_now(da.first + [da.near])
-    got_x = load(x_in, own_rows)
+    got_x = [load(x_in.at[:, c], own_rows.at[:, col(j)]) for j, c in enumerate(columns)]
 
     def head_v(h):
         return slice(128 + h * 128, 256 + h * 128)
@@ -1138,6 +1240,9 @@
     done.wait()
     events(1, 12, 14)
     done = load(fout.at[:, pl.ds(0, ff)], g_out)
+    own_w = load(wg_all.at[7], stream.at[0, 0])
+    own_w.wait()
+    gain_two = jnp.sum(fout[:, 0:ff] * stream[0, 0].astype(f32), axis=1, keepdims=True)
 
     def wq_tiles(i, slot):
         return [(wq_all.at[i], stream.at[slot, 0, :, pl.ds(0, 640)])]
@@ -1162,7 +1267,8 @@
         sums.take(i, 2, use)
 
     run(8, take_first, (2, 6, 2))
-    got_x.wait()
+    for made in got_x:
+        made.wait()
 
     def norm_back_first(i, _):
         r = pl.ds(pl.multiple_of(i * 32, 32), 32)
@@ -1174,16 +1280,36 @@
         return 0
 
     lax.fori_loop(0, rows // 32, norm_back_first, 0)
-    pending.append(load(acc, input_out))
+    pending += [load(acc.at[:, col(j)], input_out.at[:, c]) for j, c in enumerate(columns)]
     events(2, 8, 12)
     begin(3)
     done.wait()
     events(2, 12, 14)
     done = load(fout.at[:, pl.ds(0, ff)], u_out)
+    own_w = load(wu_all.at[7], stream.at[0, 0])
+    own_q = load(wq_all.at[7], stream.at[1, 0, :, pl.ds(0, 640)])
+    own_w.wait()
+    own_q.wait()
+    gain_two += jnp.sum(fout[:, 0:ff] * stream[0, 0].astype(f32), axis=1, keepdims=True)
     events(3, 0, 12)
     done.wait()
     events(3, 12, 14)
-    load(fout.at[:, pl.ds(0, 1152)], oq_out).wait()
+    pending.append(load(fout.at[:, pl.ds(0, 1152)], oq_out))
+    gain_one = jnp.sum(fout[:, 512:1152] * stream[1, 0, :, 0:640].astype(f32), axis=1, keepdims=True)
+    lane = lax.broadcasted_iota(jnp.int32, (256, 128), 1)
+    both = jnp.where(lane == 0, gain_one, jnp.where(lane == 1, gain_two, 0.0)).T[0:8, :]
+    terms[0] = both
+    over = links.start(terms.at[0], terms_core, tp=over_core)
+    over.wait_recv()
+    both = both + terms_core[...]
+    terms[1] = both
+    over = links.start(terms.at[1], terms_y, tp=over_y)
+    over.wait_recv()
+    own_gains = jnp.concatenate(
+        [gain_first[...], gain_second[...], jnp.ones((6, 256), f32)], axis=0
+    ).astype(bf16)
+    terms[2] = (both + terms_y[...]) / own_gains.astype(f32)
+    pending.append(load(terms.at[2], gain_out))
     run(8, lambda i: sums.sent(i))
     for made in pending:
         made.wait()
@@ -1220,58 +1346,10 @@
     return first, second, lanes, mask
 
 
-def token_tables(lengths, seq_index, block_len, seq_count):
-    at = jnp.arange(lengths.shape[0])
-    starts = jnp.sum(jnp.where(at[None, :] < at[:, None], lengths[None, :], 0), axis=1)
-    anchor = seq_index * block_len
-    positions = anchor + jnp.arange(block_len, dtype=jnp.int32)
-    begun = starts[None, :] <= positions[:, None]
-    row_start = jnp.max(jnp.where(begun, starts[None, :], 0), axis=1)
-    carry_in = row_start < anchor
-    later = (starts[None, :] > positions[:, None]) & (starts[None, :] < anchor + block_len)
-    after_last = jnp.sum(later.astype(jnp.int32), axis=1) == 0
-    place = jnp.arange(block_len, dtype=jnp.int32)
-    tok = jnp.stack(
-        [
-            jnp.maximum(row_start - anchor, 0).astype(f32),
-            carry_in.astype(f32),
-            after_last.astype(f32),
-            place.astype(f32),
-        ],
-        axis=1,
-    )
-    line = jnp.concatenate([tok[:, 3][None], tok[:, 0][None], jnp.zeros((6, block_len), f32)])
-    resets = (
-        jnp.sum(
-            ((starts // block_len)[None, :] == jnp.arange(seq_count)[:, None]).astype(jnp.int32),
-            axis=1,
-        )
-        > 0
-    ).astype(jnp.int32)
-
-    def clear(first, last):
-        blocks = jnp.arange(seq_count)
-        inside = (blocks >= first) & (blocks <= last)
-        return (jnp.sum(jnp.where(inside, resets, 0)) == 0).astype(f32)
-
-    z, x = seq_index // 2, seq_index % 2
-    coefs = [clear(2 * z + 1, 2 * z + 1), (x == 1).astype(f32)]
-    coefs += [clear(2 * (z - d) + 2, seq_index - 1) for d in (1, 2, 3)]
-    coefs += [jnp.zeros((), f32)] * 3
-    back = [clear(2 * z, 2 * z), (x == 0).astype(f32)]
-    back += [clear(seq_index + 1, 2 * (z + d) - 1) for d in (1, 2, 3)]
-    back += [jnp.zeros((), f32)] * 3
-
-    def wide(values):
-        return jnp.broadcast_to(jnp.stack(values)[:, None], (8, 128))
-
-    return tok, line, wide(coefs), wide(back)
-
-
-def forward_pass(tables, x_own, c_own, gain_own, q_own, o_own, g_own, u_own, d_own):
-    rows, width = x_own.shape
+def forward_pass(lengths, constants, gain_first, gain_second, x_in, weights, c_in):
+    rows, width = x_in.shape
     total = 4 * rows
-    ff = g_own.shape[1]
+    ff = weights[4].shape[0]
     hbm = pl.BlockSpec(memory_space=pl.ANY)
     vmem = pl.BlockSpec(memory_space=pltpu.VMEM)
 
@@ -1279,14 +1357,14 @@
         return jax.ShapeDtypeStruct(dims, dtype)
 
     outs = (
-        shape(8, 256, q_own.shape[1]),
-        shape(8, 256, o_own.shape[1]),
+        shape(8, 256, 640),
+        shape(8, 256, 512),
         shape(8, 256, ff),
         shape(8, 256, ff),
         shape(8, 256, ff),
         shape(total, width),
         shape(total, width),
-        shape(total, q_own.shape[1]),
+        shape(total, 640),
         shape(total, 512),
         shape(total, 128, dtype=f32),
         shape(rows, width, dtype=f32),
@@ -1298,13 +1376,28 @@
         shape(8, width, dtype=f32),
     )
     scratch = [
+        pltpu.VMEM((rows, width), bf16),
+        pltpu.VMEM((total, 128), f32),
+        pltpu.VMEM((8, total), f32),
+        pltpu.VMEM((8, 128), f32),
+        pltpu.VMEM((16, 256), bf16),
+        pltpu.VMEM((256, 640), bf16),
+        pltpu.VMEM((256, 512), bf16),
+        pltpu.VMEM((256, ff), bf16),
+        pltpu.VMEM((256, ff), bf16),
+        pltpu.VMEM((256, ff), bf16),
+        pltpu.VMEM((128, 256), f32),
+        pltpu.VMEM((256, 512), f32),
+        pltpu.VMEM((512, 256), f32),
+        pltpu.VMEM((-(-ff // 128) * 128, 256), f32),
+        pltpu.VMEM((-(-ff // 128) * 128, 256), f32),
         pltpu.VMEM((total, width), bf16),
         pltpu.VMEM((total, width), bf16),
-        pltpu.VMEM((width, q_own.shape[1]), bf16),
-        pltpu.VMEM((width, o_own.shape[1]), bf16),
+        pltpu.VMEM((width, 640), bf16),
+        pltpu.VMEM((width, 512), bf16),
         pltpu.VMEM((width, ff), bf16),
         pltpu.VMEM((width, ff), bf16),
-        pltpu.VMEM((total, q_own.shape[1]), bf16),
+        pltpu.VMEM((total, 640), bf16),
         pltpu.VMEM((total, 128), bf16),
         pltpu.VMEM((total, 512), f32),
         pltpu.VMEM((total, 128), f32),
@@ -1314,7 +1407,6 @@
         pltpu.VMEM((rows, width), bf16),
         pltpu.VMEM((rows, width), bf16),
         pltpu.VMEM((rows, width), f32),
-        pltpu.VMEM((total, width), bf16),
         pltpu.VMEM((total, ff), bf16),
         pltpu.VMEM((total, ff), bf16),
         pltpu.VMEM((total, ff), bf16),
@@ -1325,27 +1417,24 @@
         pltpu.VMEM((4, 176, 128), bf16),
         pltpu.VMEM((3, 4, 176, 128), bf16),
         pltpu.VMEM((4, 256, 128), f32),
-        pltpu.VMEM((rows, width), bf16),
         pltpu.SemaphoreType.DMA((112,)),
         pltpu.SemaphoreType.DMA((112,)),
-        pltpu.SemaphoreType.DMA((64,)),
+        pltpu.SemaphoreType.DMA((112,)),
     ]
     return pl.pallas_call(
         fwd_kernel,
         out_shape=outs,
-        in_specs=[vmem] * 8 + [vmem] + [hbm] * 6,
+        in_specs=[pl.BlockSpec(memory_space=pltpu.SMEM)] + [vmem] * 6 + [hbm] * 9,
         out_specs=(hbm,) * len(outs),
         scratch_shapes=scratch,
         compiler_params=pltpu.CompilerParams(
             collective_id=0, has_side_effects=True, vmem_limit_bytes=60 * 2**20
         ),
-    )(
-        x_own, *tables, gain_own, q_own, o_own, g_own, u_own, d_own, c_own,
-    )
-
-
-def backward_pass(tables, gains, x_own, x1, s_in, den, weights, c_all, acts):
-    rows, width = x_own.shape
+    )(lengths, *constants, gain_first, gain_second, x_in, *weights, c_in)
+
+
+def backward_pass(lengths, constants, gains, s_in, den, gain_pair, x_in, x1, weights, c_all, acts):
+    rows, width = x_in.shape
     total = 4 * rows
     ff = weights[2].shape[2]
     hbm = pl.BlockSpec(memory_space=pl.ANY)
@@ -1361,8 +1450,15 @@
         shape(256, 1152),
         shape(rows, width, dtype=bf16),
         shape(rows, width),
+        shape(8, 256),
     )
     scratch = [
+        pltpu.VMEM((total, 128), f32),
+        pltpu.VMEM((8, total), f32),
+        pltpu.VMEM((8, 128), f32),
+        pltpu.VMEM((3, 8, 256), f32),
+        pltpu.VMEM((8, 256), f32),
+        pltpu.VMEM((8, 256), f32),
         pltpu.VMEM((8, 256, ff), bf16),
         pltpu.VMEM((width, ff), bf16),
         pltpu.VMEM((width, ff), bf16),
@@ -1387,7 +1483,6 @@
         pltpu.VMEM((8, 256, 256), bf16),
         pltpu.VMEM((rows, width), f32),
         pltpu.VMEM((rows, width), f32),
-        pltpu.VMEM((rows, width), bf16),
         pltpu.VMEM((256, ff), f32),
         pltpu.VMEM((4, 176, 128), bf16),
         pltpu.VMEM((4, 176, 128), bf16),
@@ -1401,85 +1496,46 @@
         pltpu.SemaphoreType.REGULAR((2,)),
         pltpu.SemaphoreType.DMA((16,)),
         pltpu.SemaphoreType.DMA((16,)),
-        pltpu.SemaphoreType.DMA((48,)),
+        pltpu.SemaphoreType.DMA((80,)),
         pltpu.SemaphoreType.DMA((2, 2)),
     ]
     return pl.pallas_call(
         bwd_kernel,
         out_shape=outs,
-        in_specs=[vmem] * 8 + [hbm] * 2 + [vmem] * 2 + [hbm] * 13,
+        in_specs=[pl.BlockSpec(memory_space=pltpu.SMEM)] + [vmem] * 9 + [hbm] * 15,
         out_specs=(hbm,) * len(outs),
         scratch_shapes=scratch,
         compiler_params=pltpu.CompilerParams(
             collective_id=1, has_side_effects=True, vmem_limit_bytes=62 * 2**20
         ),
-    )(*tables, gains, x_own, x1, s_in, den, *weights, c_all, *acts)
+    )(lengths, *constants, gains, s_in, den, *gain_pair, x_in, x1, *weights, c_all, *acts)
+
 
 def on_device_rings(
     inputs, lengths, gain_attn, w_query, w_key, w_value, w_out, gain_mlp, w_gate, w_up, w_down,
     cotangent,
 ):
-    seq_count = 8
-    seq_index = lax.axis_index("seq")
-    rows, width = inputs.shape
-    chunk = width // seq_count
-    relative = relative_list(seq_count)
-    ring = ring_order(seq_count)
-    place_of = [ring.index(s) for s in range(seq_count)]
-    to_rel = jnp.array(
-        [[ring[(place_of[s] - k) % seq_count] for k in relative] for s in range(seq_count)],
-        jnp.int32,
-    )[seq_index]
-    to_abs = jnp.array(
-        [
-            [relative.index((place_of[s] - place_of[o]) % seq_count) for o in range(seq_count)]
-            for s in range(seq_count)
-        ],
-        jnp.int32,
-    )[seq_index]
-    to_rel = [to_rel[j] for j in range(seq_count)]
-    to_abs = [to_abs[j] for j in range(seq_count)]
-
-    gains = jnp.stack([gain_attn, gain_mlp]).astype(bf16)
-    gain_own = jnp.zeros((16, chunk), bf16).at[:2].set(gains)
-    qkv_own = jnp.concatenate([w_query, w_key, w_value], axis=1).astype(bf16)
-    out_own = w_out.astype(bf16).T
-    gate_own, up_own = w_gate.astype(bf16), w_up.astype(bf16)
-    down_own = w_down.astype(bf16).T
-    x_own = to_relative(inputs, to_rel, chunk)
-    c_own = to_relative(cotangent, to_rel, chunk)
-
-    tok, line, coefs, back = token_tables(lengths, seq_index, 4 * rows, seq_count)
     first, second, lanes, mask = feature_tables(4)
-    tables = (
-        tok, line, jnp.asarray(first, bf16), jnp.asarray(second, bf16), jnp.asarray(lanes),
-        jnp.asarray(mask),
-    )
+    constants = (
+        jnp.asarray(first, bf16), jnp.asarray(second, bf16), jnp.asarray(lanes), jnp.asarray(mask),
+    )
+    gain_pair = (gain_attn.reshape(1, -1), gain_mlp.reshape(1, -1))
     made = forward_pass(
-        (*tables, coefs), x_own, c_own, gain_own, qkv_own, out_own, gate_own, up_own, down_own
+        lengths, constants, *gain_pair, inputs,
+        (w_query.T, w_key.T, w_value, w_out, w_gate.T, w_up.T, w_down), cotangent,
     )
     weights, (c_all, h1, qkv, yb, den, x1, h2, gate, up, mixed, s_in, gain_all) = made[:5], made[5:]
-    sum_down_t, sum_gate, sum_up, sum_oq, block, grad_input = backward_pass(
-        (*tables, back), gain_all, x_own, x1, s_in, den, weights, c_all,
+    sum_down_t, sum_gate, sum_up, sum_oq, block, grad_input, gain_sums = backward_pass(
+        lengths, constants, gain_all, s_in, den, gain_pair, inputs, x1, weights, c_all,
         (h1, qkv, yb, h2, gate, up, mixed),
     )
-
-    sum_qkv = sum_oq[:, 512:]
-    gain_terms = jnp.stack(
-        [
-            jnp.sum(qkv_own.astype(f32) * sum_qkv, axis=1),
-            jnp.sum(gate_own.astype(f32) * sum_gate + up_own.astype(f32) * sum_up, axis=1),
-        ]
-    )
-    gain_sums = tp_sum(gain_terms) / gains.astype(f32)
-    qk_cols = w_query.shape[1]
     return (
-        to_relative(block, to_abs, chunk),
-        to_relative(grad_input, to_abs, chunk),
+        block,
+        grad_input,
         gain_sums[0],
-        sum_qkv[:, :qk_cols],
-        sum_qkv[:, qk_cols : 2 * qk_cols],
-        sum_qkv[:, 2 * qk_cols :],
+        sum_oq[:, 512:576],
+        sum_oq[:, 576:640],
+        sum_oq[:, 640:],
         sum_oq[:, :512].T,
         gain_sums[1],
         sum_gate,

time: 647 us -> 579 us (0.89)
  local copies, waits for them, and re-layouts: 62.3 us -> 16.7 us
  between operations: 17.2 us -> 1.12 us
  other arithmetic: 9.38 us -> 0 us
    unnamed x79 -> x16, local copies, waits for them, and re-layouts: 47.6 us -> 11.5 us
  transfers between devices with their start and end apart: 2 -> 0, of which waited for: 0 -> 0; matrix products, arithmetic and copies ran while one was open for 5% -> 0% of each run, Pallas kernels for 0% -> 0%
where the time goes in v3:
time: 579 us; the launch traced here: 571 us
  Pallas kernels  553 us (96%)
  local copies, waits for them, and re-layouts  16.7 us (3%)
    pallas_call x1, Pallas kernels, backward_pass(): pl.pallas_call(bwd_kernel, out_shape=outs, in_specs=[pl.BlockSpec(memory_...  278 us
    pallas_call x1, Pallas kernels, forward_pass(): pl.pallas_call(fwd_kernel, out_shape=outs, in_specs=[pl.BlockSpec(memory_...  275 us

profile of v3, /device:TPU:0, one launch (start us, length us, event | category | flops | bytes accessed | tf_op | source)
XLA Modules:
  0.0 571.0 jit_solution(1103707617464359530)
XLA Ops:
  0.6 274.8 %shard_map.239 = (bf16[8,256,640]{2,1,0:T(8,128)(2,1)}, bf16[8,256,512]{2,1,0:T(8,128)(2,1)}, bf16[8,256,1376]{2,1,0:T(8,128)(2,1)}, bf16[8,256,1376]{2,1,0:T(8,...) custom-call(s32[3]{0:T(128)} %lengths.3, ...), custom_call_target="tpu_custom_call" | custom-call | tf_op jit(solution)/shard_map/pallas_call | solution.py:1424
  275.5 278.4 %shard_map.240 = (f32[256,1376]{1,0:T(8,128)}, f32[256,1376]{1,0:T(8,128)}, f32[256,1376]{1,0:T(8,128)}, f32[256,1152]{1,0:T(8,128)}, bf16[256,2048]{1,0:T(8,128...) custom-call(s32[3]{0:T(128)} %lengths.3, bf16[4,128,256]{2,1,0:T(8,128)(2,1)} %constant.8.clone.sa_ref, ...), custom_call_target="tpu_custom_call" | custom-call | tf_op jit(solution)/shard_map/pallas_call | solution.py:1502
  553.9 0.0 copy-start.3
  553.9 1.4 fusion.1
  555.3 1.7 fusion
  557.0 2.1 slice_bitcast_fusion
  559.1 0.0 copy-start.2
  559.1 1.0 copy.29
  560.1 1.6 copy.28
  561.7 0.7 copy.27
  562.4 0.0 copy-done.3
  562.4 1.5 copy.30
  563.9 0.0 copy-done.2
  563.9 0.0 copy-start.1
  563.9 1.5 copy.31
  565.4 0.0 copy-done.1
  565.4 0.0 copy-start
  565.4 1.5 copy.32
  567.0 2.3 copy.35
  569.3 0.0 copy-done
  569.3 1.3 copy.36
Async XLA Ops:
  553.9 8.5 %copy-start.3 = (f32[256,1376]{1,0:T(8,128)S(1)}, f32[256,1376]{1,0:T(8,128)}, u32[]{:S(2)}) copy-start(f32[256,1376]{1,0:T(8,128)} %get-tuple-element.67) | copy-start | bytes 4227076
  559.1 4.8 copy-start.2
  563.9 1.5 copy-start.1
  565.4 3.8 copy-start

commit v4 on v3

--- a/solution.py
+++ b/solution.py
@@ -273,22 +273,24 @@
 
 
 class Gather:
-    def __init__(self, links, arrays, split, nearby):
+    def __init__(self, links, arrays, split, nearby, gangs):
         self.links, self.arrays, self.split, self.nearby = links, arrays, split, nearby
         self.at = {k: j for j, k in enumerate(relative_list(8))}
-        self.flying = {}
+        self.flying, self.gangs, self.done = {}, gangs, 0
+        self.gang_of = {a: i for i, gang in enumerate(gangs) for a in gang}
         self.events = [
             (a, step, way, part)
-            for a in range(len(arrays))
+            for gang in gangs
             for step in (1, 2, 3, 4)
+            for a in gang
             for part in (0, 1)
             for way in (0, 1)
             if step < 4 or way == part
         ]
-        self.done = 0
-        for part in (0, 1):
-            for way in (0, 1):
-                self.go(0, 1, way, part)
+        for a in gangs[0]:
+            for part in (0, 1):
+                for way in (0, 1):
+                    self.go(a, 1, way, part)
 
     def rows(self, part):
         return pl.ds(part * self.split, self.split)
@@ -309,12 +311,21 @@
             self.flying[a, step, way, part].wait_recv()
             if step < 3 or (step == 3 and way == part):
                 self.go(a, step + 1, way, part)
-            if step == 3 and a + 1 < len(self.arrays):
-                self.go(a + 1, 1, way, part)
+            i = self.gang_of[a]
+            if step == 3 and i + 1 < len(self.gangs):
+                mine, later = self.gangs[i].index(a), self.gangs[i + 1]
+                if i == 0:
+                    later = later + self.gangs[2]
+                elif i == 1:
+                    later = []
+                last = mine == len(self.gangs[i]) - 1
+                for other in later[mine:] if last else later[mine : mine + 1]:
+                    self.go(other, 1, way, part)
             self.done += 1
 
     def pump_array(self, a):
-        self.pump(14 * (a + 1))
+        gang = self.gang_of[a]
+        self.pump(14 * sum(len(g) for g in self.gangs[: gang + 1]))
 
 
 def greet(peers):
@@ -408,12 +419,46 @@
     z, x = seq // 2, seq % 2
     one = jnp.ones((1, 128), f32)
     if step > 0:
-        rows = [clear(2 * z + 1, 2 * z + 1), one * x.astype(f32)]
-        rows += [clear(2 * (z - d) + 2, seq - 1) for d in (1, 2, 3)]
+        rows = [clear(2 * z + 1, 2 * z + 1), one * x.astype(f32), clear(2 * z, seq - 1)]
     else:
-        rows = [clear(2 * z, 2 * z), one * (1 - x).astype(f32)]
-        rows += [clear(seq + 1, 2 * (z + d) - 1) for d in (1, 2, 3)]
-    coefs[...] = jnp.concatenate(rows + [one * 0.0] * 3, axis=0)
+        rows = [clear(2 * z, 2 * z), one * (1 - x).astype(f32), clear(seq + 1, 2 * z + 1)]
+    rows.append(clear(2 * z, 2 * z + 1))
+    coefs[...] = jnp.concatenate(rows + [one * 0.0] * 4, axis=0)
+
+
+class Chain:
+    def __init__(self, links, st_t, st_z, coefs, seq, z, step):
+        self.st_t, self.st_z, self.coefs = st_t, st_z, coefs
+        self.turn = z if step > 0 else 3 - z
+        self.hop = links.copy(st_t, st_z, seq=seq + 2 * step)
+
+    def move(self, turn):
+        @pl.when(self.turn == turn)
+        def _():
+            if turn > 0:
+                self.hop.wait_recv()
+            if turn < 3:
+                if turn > 0:
+                    for h in range(4):
+                        own = self.st_t[h].astype(f32)
+                        came = self.coefs[3:4, :] * self.st_z[h].astype(f32)
+                        self.st_t[h] = (own + came).astype(bf16)
+                self.hop.start()
+
+    def use(self, states, near):
+        for h in range(4):
+            states[h, 0:176, :] = self.coefs[1:2, :] * near[h].astype(f32)
+            states[h, 176:256, :] = jnp.zeros((80, 128), f32)
+
+        @pl.when(self.turn > 0)
+        def _():
+            for h in range(4):
+                states[h, 0:176, :] += self.coefs[2:3, :] * self.st_z[h].astype(f32)
+
+    def finish(self):
+        @pl.when(self.turn < 3)
+        def _():
+            self.hop.wait_send()
 
 
 def ring_columns(place):
@@ -490,6 +535,7 @@
         [(q_own, wq_all), (o_own, wo_all), (g_own, wg_all), (u_own, wu_all), (d_own, wd_all)],
         128,
         nearby,
+        [[0], [1], [2, 3], [4]],
     )
     own_in = [
         load(x_ref, xrows.block(tp, 0, rows)),
@@ -551,7 +597,7 @@
 
     lax.fori_loop(0, total // 256, project, 0)
     store(qkv, qkv_out)
-    ring.pump(17)
+    ring.pump(16)
 
     heads = 4
 
@@ -572,7 +618,7 @@
             0, total // 256, state, (jnp.zeros((256, 128), f32), jnp.zeros((1, 256), f32))
         )
         pack_state(st, h, s, zz)
-        ring.pump(18 + h)
+        ring.pump(16 + (h + 1) // 2)
     to_x = links.start(st, st_x, seq=seq + 1 - 2 * x)
 
     def local_head(h):
@@ -589,40 +635,25 @@
             num[r, h * 128 : (h + 1) * 128] = dot(kap.astype(bf16), qkv[:span, head_v(h)])
 
     local_head(0)
-    ring.pump(23)
-    local_head(1)
-    ring.pump(25)
+    ring.pump(19)
     to_x.wait_recv()
     for h in range(heads):
         mine, theirs = st[h].astype(f32), st_x[h].astype(f32)
         early = jnp.where(x == 0, mine, theirs)
         later = jnp.where(x == 0, theirs, mine)
         st_t[h] = (later + coef_ref[0:1, :] * early).astype(bf16)
-    to_z = [links.copy(st_t, st_z.at[d - 1], seq=seq + 2 * d) for d in (1, 2, 3)]
-    for d in (1, 2, 3):
-
-        @pl.when(z + d < 4)
-        def _(d=d):
-            to_z[d - 1].start()
-
+    chain = Chain(links, st_t, st_z, coef_ref, seq, z, 1)
+    chain.move(0)
+    local_head(1)
+    chain.move(1)
+    ring.pump(20)
     local_head(2)
-    ring.pump(27)
+    chain.move(2)
+    ring.pump(22)
     local_head(3)
-    ring.pump(28)
-    own_kept[1].wait()
-    got = load_weights(load, wo_all, wo)
-    for h in range(heads):
-        num_in = coef_ref[1:2, :] * st_x[h].astype(f32)
-        s_in[h, 0:176, :] = num_in
-        s_in[h, 176:256, :] = jnp.zeros((80, 128), f32)
-    for d in (1, 2, 3):
-
-        @pl.when(z >= d)
-        def _(d=d):
-            to_z[d - 1].wait_recv()
-            for h in range(heads):
-                s_in[h, 0:176, :] += coef_ref[1 + d : 2 + d, :] * st_z[d - 1, h].astype(f32)
-
+    chain.move(3)
+    ring.pump(24)
+    chain.use(s_in, st_x)
     store(s_in, sin_out)
     for h in range(heads):
         z_row = jnp.concatenate([s_in[h, 160:161, :], s_in[h, 161:162, :]], axis=1)
@@ -642,9 +673,12 @@
             return 0
 
         lax.fori_loop(0, total // 256, carry, 0)
-        ring.pump(29 + h)
+        ring.pump(25 + h)
     store(yb, yb_out)
     store(den, den_out)
+    ring.pump_array(1)
+    own_kept[1].wait()
+    got = load_weights(load, wo_all, wo)
     for made in got:
         made.wait()
 
@@ -666,6 +700,7 @@
         to_core.append(links.start(sc.at[yy], rc.at[yy], tp=over_core))
     for made in to_core:
         made.wait_recv()
+    ring.pump(32)
 
     def away_cols(i, _):
         c = pl.ds(pl.multiple_of(i * cols, cols), cols)
@@ -686,6 +721,7 @@
     lax.fori_loop(0, 2048 // cols, own_cols, 0)
     ring.pump(34)
     to_y.wait_recv()
+    ring.pump(37)
 
     links.sent_now(xrows.first + [xrows.near])
     ho = x_ref
@@ -704,9 +740,9 @@
     h2 = xg
     hrows = Rows(links, ho, h2, tp, over_y, over_core, rows)
     own_in = load(ho, hrows.block(tp, 0, rows))
-    ring.pump(36)
+    ring.pump(40)
     hrows.forward(0)
-    ring.pump(37)
+    ring.pump(43)
     hrows.forward(1)
     crows.forward(0)
     crows.forward(1)
@@ -743,11 +779,7 @@
     for made in pending:
         made.wait()
     links.finish()
-    for d in (1, 2, 3):
-
-        @pl.when(z + d < 4)
-        def _(d=d):
-            to_z[d - 1].wait_send()
+    chain.finish()
 
 
 def pack_state(st, h, s, zz):
@@ -775,6 +807,9 @@
             device_id_type=pl.DeviceIdType.MESH,
         )
 
+    def slot(self, a, step):
+        return (a % 2) * 4 + (a // 2 * 7 + step) % 4
+
     def rows(self, way, sub, base=0):
         start = base + way * 128 + sub * 64
         return pl.ds(start if isinstance(start, int) else pl.multiple_of(start, 64), 64)
@@ -786,12 +821,12 @@
         for sub in (0, 1):
             for way in (0, 1):
                 src = own.at[self.rows(way, sub, way * 256), pl.ds(column, width)]
-                self.copy(a, 0, way, sub, src, 7 * (a % 2), width).start()
+                self.copy(a, 0, way, sub, src, self.slot(a, 0), width).start()
 
     def event(self, a, e, own, width, out, column=0):
         step, sub = e // 2, e % 2
-        is_first, is_last = (6 - step) // 6, step // 6
-        here = is_first * 7 * (a % 2) + (1 - is_first) * step
+        is_last = step // 6
+        here = self.slot(a, step)
         far = (step + 1) // 4
         place0 = (1 - far) * 2 * (step + 1) + far * (11 - 2 * step) + is_last * 8
         far = (step + 2) // 4 - is_last
@@ -812,7 +847,7 @@
             for way in (0, 1):
                 self.slots[here, self.rows(way, sub), pl.ds(0, width)] = summed(way).astype(bf16)
                 piece = self.piece(here, way, sub, width)
-                self.copy(a, step + 1, way, sub, piece, step + 1, width).start()
+                self.copy(a, step + 1, way, sub, piece, self.slot(a, step + 1), width).start()
 
         def end():
             for way in (0, 1):
@@ -906,7 +941,7 @@
     lengths, sa_ref, sb_ref, lanes_ref, hm_ref, gains, s_in, den, gain_first, gain_second,
     x_in, x1_in, wq_all, wo_all, wg_all, wu_all, wd_all, c_all, h1_all, qkv_all, yb_all, h2_all,
     gate_all, up_all, m_all,
-    d_out, g_out, u_out, oq_out, block_out, input_out, gain_out,
+    d_out, g_out, u_out, oq_out, block_out, input_out, gain_out, u_kept,
     tok_ref, line_ref, coef_ref, terms, terms_core, terms_y,
     slots, s1, s2, wo, stream, hs, rows_all, mm, dup, tiles, qkv, kq, yb, dnum, dden, dden_t, dqkv,
     dq, dk, part, from_core, from_y, acc, x1, fout, st, st_x, st_t, st_z, s_back, own_rows,
@@ -941,7 +976,7 @@
     ring = Scatter(slots, ring_send, ring_recv, nearby)
     sums = TpSum(part, from_core, from_y, tp_sems, credits, tp, over_y, over_core)
 
-    def run(n, body, pumps=None, lookup=None):
+    def run(n, body, pumps=None):
         def step(i, _):
             body(i)
             if pumps:
@@ -965,6 +1000,14 @@
     def events(a, first, last):
         lax.fori_loop(first, last, lambda e, _: (event(a, e), 0)[1], 0)
 
+    def both(a, first, b, second, count):
+        def pair(i, _):
+            event(a, first + i)
+            event(b, second + i)
+            return 0
+
+        lax.fori_loop(0, count, pair, 0)
+
     def chunks_of(source, size, body, pumps=None, count=8):
         def copies(i, slot):
             return [
@@ -1011,17 +1054,23 @@
 
     def gate_up_tiles(i, slot):
         r = col(i, 128)
-        return [(gate_all.at[r], tiles.at[slot, 0]), (up_all.at[r], tiles.at[slot, 1])]
+        return [
+            (gate_all.at[r], tiles.at[slot, pl.ds(0, 128)]),
+            (up_all.at[r], tiles.at[slot, pl.ds(128, 128)]),
+        ]
 
     def grad_gate_up(i, slot):
         r = col(i, 128)
         dm = dot(rows_all[r, :], s2[...]).astype(bf16).astype(f32)
-        g = tiles[slot, 0].astype(f32)
-        u = tiles[slot, 1].astype(f32)
+        g = tiles[slot, 0:128].astype(f32)
+        u = tiles[slot, 128:256].astype(f32)
         s = jax.nn.sigmoid(g)
         mm[r, :] = (dm * u * s * (1.0 + g * (1.0 - s))).astype(bf16)
         dup[r, :] = (dm * (g * s)).astype(bf16)
 
+        pl.when(i >= 3)(lambda: take_block(i - 3))
+
+    def take_block(i):
         def use(value):
             own_rows[:, col(i)] = (x1[:, col(i)] + value).astype(bf16)
 
@@ -1029,29 +1078,37 @@
 
     got_x1.wait()
     chunks_of(gate_up_tiles, 8, grad_gate_up, (0, 3, 4))
-    kept = [load(own_rows.at[:, col(j)], block_out.at[:, c]) for j, c in enumerate(columns)]
-    pending = []
 
     def w_tiles(i, slot):
         return [(wg_all.at[i], stream.at[slot, 0]), (wu_all.at[i], stream.at[slot, 1])]
 
     def grad_hidden(i, slot):
+        pl.when(i < 3)(lambda: take_block(5 + i))
         value = dot_t(mm[...], stream[slot, 0]) + dot_t(dup[...], stream[slot, 1])
         sums.offer(i, 1, value)
         pl.when(i > 0)(lambda: sums.pass_on(i - 1, 1))
 
     chunks_of(w_tiles, 8, grad_hidden, (0, 7, 2))
+    kept = [load(own_rows.at[:, col(j)], block_out.at[:, c]) for j, c in enumerate(columns)]
+    pending = []
     sums.pass_on(7, 1)
 
     def h_tiles(everyone):
         return lambda i, slot: [(everyone.at[:, col(i)], hs.at[slot])]
 
-    def grad_gate(i, slot):
+    def keep_up(i, slot):
+        return pltpu.make_async_copy(tiles.at[slot], u_kept.at[col(i)], tile_sems.at[1, slot])
+
+    def grads(i, slot):
         s2[col(i), :] = dot_tt(hs[slot], mm[...]).astype(bf16)
-
-    chunks_of(h_tiles(h2_all), 8, grad_gate, (0, 9, 2))
-    events(0, 11, 12)
-    begin(1)
+        pl.when(i >= 2)(lambda: keep_up(i - 2, slot).wait())
+        tiles[slot] = dot_tt(hs[slot], dup[...]).astype(bf16)
+        keep_up(i, slot).start()
+        pl.when(i == 1)(lambda: begin(1))
+
+    chunks_of(h_tiles(h2_all), 8, grads, (0, 9, 2))
+    keep_up(6, 0).wait()
+    keep_up(7, 1).wait()
 
     def take_second(i):
         def use(value):
@@ -1059,8 +1116,17 @@
 
         sums.take(i, 1, use)
 
-    run(8, take_second, (0, 12, 2))
+    events(0, 11, 12)
+    run(2, take_second)
+    both(1, 0, 0, 12, 2)
     done = load(fout.at[:, pl.ds(0, ff)], d_out)
+    got_up = load(u_kept, s1)
+    lax.fori_loop(2, 5, lambda i, _: (take_second(i), 0)[1], 0)
+    events(1, 2, 3)
+    got_up.wait()
+    begin(2)
+    lax.fori_loop(5, 8, lambda i, _: (take_second(i), 0)[1], 0)
+    both(1, 3, 2, 0, 1)
 
     for made in kept:
         made.wait()
@@ -1083,12 +1149,9 @@
     da = Rows(links, own_rows, rows_all, tp, over_y, over_core, rows)
     own_in = load(own_rows, da.block(tp, 0, rows))
 
-    def grad_up(i, slot):
-        s1[col(i), :] = dot_tt(hs[slot], dup[...]).astype(bf16)
-
-    chunks_of(h_tiles(h2_all), 8, grad_up, (1, 0, 2))
+    both(1, 4, 2, 1, 1)
     da.forward(0)
-    events(1, 2, 5)
+    both(1, 5, 2, 2, 1)
     da.forward(1)
     for made in got_qkv + got_wo:
         made.wait()
@@ -1120,7 +1183,7 @@
         dden_t[i] = packed.T[0:8, :]
 
     run(4, grad_attended)
-    event(1, 5)
+    both(1, 6, 2, 3, 1)
 
     for h in range(4):
 
@@ -1137,7 +1200,7 @@
         )
         pack_state(st, h, s, zz)
     to_x = links.start(st, st_x, seq=seq + 1 - 2 * x)
-    event(1, 6)
+    both(1, 7, 2, 4, 1)
 
     dq[...] = jnp.zeros(dq.shape, f32)
 
@@ -1175,31 +1238,19 @@
         first = jnp.where(x == 0, mine, theirs)
         second = jnp.where(x == 0, theirs, mine)
         st_t[h] = (first + coef_ref[0:1, :] * second).astype(bf16)
-    to_z = [links.copy(st_t, st_z.at[d - 1], seq=seq - 2 * d) for d in (1, 2, 3)]
-    for d in (1, 2, 3):
-
-        @pl.when(z >= d)
-        def _(d=d):
-            to_z[d - 1].start()
-
-    events(1, 7, 8)
+    chain = Chain(links, st_t, st_z, coef_ref, seq, z, -1)
+    chain.move(0)
+    both(1, 8, 2, 5, 1)
     local_head(1)
-    events(1, 8, 9)
+    chain.move(1)
+    both(1, 9, 2, 6, 1)
     local_head(2)
-    events(1, 9, 10)
+    chain.move(2)
+    both(1, 10, 2, 7, 1)
     local_head(3)
-    events(1, 10, 12)
-    begin(2)
-    for h in range(4):
-        s_back[h, 0:176, :] = coef_ref[1:2, :] * st_x[h].astype(f32)
-        s_back[h, 176:256, :] = jnp.zeros((80, 128), f32)
-    for d in (1, 2, 3):
-
-        @pl.when(z + d < 4)
-        def _(d=d):
-            to_z[d - 1].wait_recv()
-            for h in range(4):
-                s_back[h, 0:176, :] += coef_ref[1 + d : 2 + d, :] * st_z[d - 1, h].astype(f32)
+    chain.move(3)
+    both(1, 11, 2, 8, 1)
+    chain.use(s_back, st_x)
 
     def split_state(ref, h):
         z_row = jnp.concatenate([ref[h, 160:161, :], ref[h, 161:162, :]], axis=1)
@@ -1238,7 +1289,7 @@
 
     run(4, join)
     done.wait()
-    events(1, 12, 14)
+    both(1, 12, 2, 9, 2)
     done = load(fout.at[:, pl.ds(0, ff)], g_out)
     own_w = load(wg_all.at[7], stream.at[0, 0])
     own_w.wait()
@@ -1251,22 +1302,26 @@
         sums.offer(i, 2, dot_t(dqkv[...], stream[slot, 0, :, 0:640]))
         pl.when(i > 0)(lambda: sums.pass_on(i - 1, 2))
 
-    chunks_of(wq_tiles, 8, grad_hidden_first, (2, 0, 2))
+    chunks_of(wq_tiles, 8, grad_hidden_first, (2, 11, 1))
     sums.pass_on(7, 2)
 
     def grad_out_qkv(i, slot):
         s2[col(i), 0:512] = dot_tt(rows_all[:, col(i)], yb[...]).astype(bf16)
         s2[col(i), 512:1152] = dot_tt(hs[slot], dqkv[...]).astype(bf16)
 
-    chunks_of(h_tiles(h1_all), 8, grad_out_qkv, (2, 2, 2))
-    events(2, 4, 6)
+        pl.when(i == 1)(lambda: begin(3))
+
+    chunks_of(h_tiles(h1_all), 8, grad_out_qkv, (3, 0, 1))
+    done.wait()
+    both(2, 12, 3, 1, 2)
+    done = load(fout.at[:, pl.ds(0, ff)], u_out)
     def take_first(i):
         def use(value):
             x1[:, col(i)] = value
 
         sums.take(i, 2, use)
 
-    run(8, take_first, (2, 6, 2))
+    run(8, take_first, (3, 3, 4))
     for made in got_x:
         made.wait()
 
@@ -1281,17 +1336,12 @@
 
     lax.fori_loop(0, rows // 32, norm_back_first, 0)
     pending += [load(acc.at[:, col(j)], input_out.at[:, c]) for j, c in enumerate(columns)]
-    events(2, 8, 12)
-    begin(3)
-    done.wait()
-    events(2, 12, 14)
-    done = load(fout.at[:, pl.ds(0, ff)], u_out)
     own_w = load(wu_all.at[7], stream.at[0, 0])
     own_q = load(wq_all.at[7], stream.at[1, 0, :, pl.ds(0, 640)])
     own_w.wait()
     own_q.wait()
     gain_two += jnp.sum(fout[:, 0:ff] * stream[0, 0].astype(f32), axis=1, keepdims=True)
-    events(3, 0, 12)
+    events(3, 7, 12)
     done.wait()
     events(3, 12, 14)
     pending.append(load(fout.at[:, pl.ds(0, 1152)], oq_out))
@@ -1314,11 +1364,7 @@
     for made in pending:
         made.wait()
     links.finish()
-    for d in (1, 2, 3):
-
-        @pl.when(z >= d)
-        def _(d=d):
-            to_z[d - 1].wait_send()
+    chain.finish()
 
 
 def feature_tables(heads):
@@ -1415,7 +1461,7 @@
         pltpu.VMEM((4, 176, 128), bf16),
         pltpu.VMEM((4, 176, 128), bf16),
         pltpu.VMEM((4, 176, 128), bf16),
-        pltpu.VMEM((3, 4, 176, 128), bf16),
+        pltpu.VMEM((4, 176, 128), bf16),
         pltpu.VMEM((4, 256, 128), f32),
         pltpu.SemaphoreType.DMA((112,)),
         pltpu.SemaphoreType.DMA((112,)),
@@ -1451,6 +1497,7 @@
         shape(rows, width, dtype=bf16),
         shape(rows, width),
         shape(8, 256),
+        shape(width, ff, dtype=bf16),
     )
     scratch = [
         pltpu.VMEM((total, 128), f32),
@@ -1468,7 +1515,7 @@
         pltpu.VMEM((total, width), bf16),
         pltpu.VMEM((total, ff), bf16),
         pltpu.VMEM((total, ff), bf16),
-        pltpu.VMEM((2, 2, 128, ff), bf16),
+        pltpu.VMEM((2, 256, ff), bf16),
         pltpu.VMEM((total, 640), bf16),
         pltpu.VMEM((total, 128), bf16),
         pltpu.VMEM((total, 512), bf16),
@@ -1487,7 +1534,7 @@
         pltpu.VMEM((4, 176, 128), bf16),
         pltpu.VMEM((4, 176, 128), bf16),
         pltpu.VMEM((4, 176, 128), bf16),
-        pltpu.VMEM((3, 4, 176, 128), bf16),
+        pltpu.VMEM((4, 176, 128), bf16),
         pltpu.VMEM((4, 256, 128), f32),
         pltpu.VMEM((rows, width), bf16),
         pltpu.SemaphoreType.DMA((2, 2, 2)),
@@ -1525,7 +1572,7 @@
         (w_query.T, w_key.T, w_value, w_out, w_gate.T, w_up.T, w_down), cotangent,
     )
     weights, (c_all, h1, qkv, yb, den, x1, h2, gate, up, mixed, s_in, gain_all) = made[:5], made[5:]
-    sum_down_t, sum_gate, sum_up, sum_oq, block, grad_input, gain_sums = backward_pass(
+    sum_down_t, sum_gate, sum_up, sum_oq, block, grad_input, gain_sums, _ = backward_pass(
         lengths, constants, gain_all, s_in, den, gain_pair, inputs, x1, weights, c_all,
         (h1, qkv, yb, h2, gate, up, mixed),
     )

time: 579 us -> 537 us (0.927)
  Pallas kernels: 553 us -> 512 us
    pallas_call x1, Pallas kernels: 278 us -> 251 us  [backward_pass(): pl.pallas_call(bwd_kernel, out_shape=outs, in_specs=[pl.BlockSpec(memory_...]
    pallas_call x1, Pallas kernels: 275 us -> 261 us  [forward_pass(): pl.pallas_call(fwd_kernel, out_shape=outs, in_specs=[pl.BlockSpec(memory_...]
where the time goes in v4:
time: 537 us; the launch traced here: 530 us
  Pallas kernels  512 us (95%)
  local copies, waits for them, and re-layouts  16.7 us (3%)
    pallas_call x1, Pallas kernels, forward_pass(): pl.pallas_call(fwd_kernel, out_shape=outs, in_specs=[pl.BlockSpec(memory_...  261 us
    pallas_call x1, Pallas kernels, backward_pass(): pl.pallas_call(bwd_kernel, out_shape=outs, in_specs=[pl.BlockSpec(memory_...  251 us
    unnamed x16, local copies, waits for them, and re-layouts  11.5 us

profile of v4, /device:TPU:0, one launch (start us, length us, event | category | flops | bytes accessed | tf_op | source)
XLA Modules:
  0.0 529.5 jit_solution(31899172114826297)
XLA Ops:
  0.6 260.9 %shard_map.239 = (bf16[8,256,640]{2,1,0:T(8,128)(2,1)}, bf16[8,256,512]{2,1,0:T(8,128)(2,1)}, bf16[8,256,1376]{2,1,0:T(8,128)(2,1)}, bf16[8,256,1376]{2,1,0:T(8,...) custom-call(s32[3]{0:T(128)} %lengths.3, ...), custom_call_target="tpu_custom_call" | custom-call | tf_op jit(solution)/shard_map/pallas_call | solution.py:1470
  261.5 250.8 %shard_map.240 = (f32[256,1376]{1,0:T(8,128)}, f32[256,1376]{1,0:T(8,128)}, f32[256,1376]{1,0:T(8,128)}, f32[256,1152]{1,0:T(8,128)}, bf16[256,2048]{1,0:T(8,128...) custom-call(s32[3]{0:T(128)} %lengths.3, bf16[4,128,256]{2,1,0:T(8,128)(2,1)} %constant.8.clone.sa_ref, ...), custom_call_target="tpu_custom_call" | custom-call | tf_op jit(solution)/shard_map/pallas_call | solution.py:1549
  512.4 0.0 copy-start.3
  512.4 1.4 fusion.1
  513.8 1.7 fusion
  515.5 2.1 slice_bitcast_fusion
  517.6 0.0 copy-start.2
  517.6 1.0 copy.29
  518.6 1.6 copy.28
  520.2 0.7 copy.27
  520.9 0.0 copy-done.3
  520.9 1.5 copy.30
  522.4 0.0 copy-done.2
  522.4 0.0 copy-start.1
  522.4 1.5 copy.31
  523.9 0.0 copy-done.1
  524.0 0.0 copy-start
  524.0 1.5 copy.32
  525.5 2.3 copy.35
  527.8 0.0 copy-done
  527.8 1.3 copy.36
Async XLA Ops:
  512.4 8.5 %copy-start.3 = (f32[256,1376]{1,0:T(8,128)S(1)}, f32[256,1376]{1,0:T(8,128)}, u32[]{:S(2)}) copy-start(f32[256,1376]{1,0:T(8,128)} %get-tuple-element.67) | copy-start | bytes 4227076
  517.6 4.8 copy-start.2
  522.4 1.5 copy-start.1
  524.0 3.8 copy-start

commit v5 on v4

--- a/solution.py
+++ b/solution.py
@@ -475,7 +475,7 @@
     lengths, sa_ref, sb_ref, lanes_ref, hm_ref, gain_first, gain_second,
     x_in, wq_in, wk_in, wv_in, wo_in, wg_in, wu_in, wd_in, c_in,
     wq_all, wo_all, wg_all, wu_all, wd_all, c_all,
-    h1_out, qkv_out, yb_out, den_out, x1_out, h2_out, gate_out, up_out, m_out, sin_out, gain_out,
+    h1_out, qkv_out, yb_out, den_out, x1_out, h2_out, gate_out, up_out, m_out, sin_out, gain_out, terms_out,
     x_ref, tok_ref, line_ref, coef_ref, gain_ref, q_own, o_own, g_own, u_own, d_own,
     w_small, w_v, w_o, w_d, w_g,
     xg, h1, wq, wo, wg, wu, qkv, kq, num, den, yb, sc, rc, sy, ry, x1, gate, up, mm,
@@ -580,7 +580,7 @@
 
     lax.fori_loop(0, total // 32, norm_first, 0)
     links.sent_now(xrows.last)
-    store(h1, h1_out)
+    kept_h1 = load(h1, h1_out)
     for made in got_c:
         made.wait()
     crows = Rows(links, c_all.at[c_rows], c_all, tp, over_y, over_core, rows)
@@ -750,6 +750,8 @@
     crows.finish()
     own_in.wait()
     store(h2, h2_out)
+    kept_h1.wait()
+    got_c = load(c_all, h1)
     ring.pump_array(2)
     own_kept[2].wait()
     got = load_weights(load, wg_all, wg)
@@ -774,6 +776,26 @@
     store(gate, gate_out)
     store(up, up_out)
     store(mm, m_out)
+    got_c.wait()
+    links.sent_now([ring.flying[a, 1, way, part] for a in (2, 3) for way in (0, 1) for part in (0, 1)])
+    out_sems = [locs.take(), locs.take()]
+    buffers = [g_own, u_own]
+
+    def keep_terms(j, k):
+        return pltpu.make_async_copy(buffers[k], terms_out.at[col(j)], out_sems[k])
+
+    def grad_down(i, _):
+        for k in (0, 1):
+            pl.when(i > 0)(lambda k=k: keep_terms(2 * i - 2 + k, k).wait())
+            buffers[k][...] = dot_tt(h1[:, col(2 * i + k)], mm[...]).astype(bf16)
+            keep_terms(2 * i + k, k).start()
+        return 0
+
+    lax.fori_loop(0, 2, grad_down, 0)
+    ring.pump(66)
+    lax.fori_loop(2, 4, grad_down, 0)
+    for k in (0, 1):
+        keep_terms(6 + k, k).wait()
     ring.pump_array(4)
     own_kept[4].wait()
     for made in pending:
@@ -940,7 +962,7 @@
 def bwd_kernel(
     lengths, sa_ref, sb_ref, lanes_ref, hm_ref, gains, s_in, den, gain_first, gain_second,
     x_in, x1_in, wq_all, wo_all, wg_all, wu_all, wd_all, c_all, h1_all, qkv_all, yb_all, h2_all,
-    gate_all, up_all, m_all,
+    gate_all, up_all, m_all, terms_all,
     d_out, g_out, u_out, oq_out, block_out, input_out, gain_out, u_kept,
     tok_ref, line_ref, coef_ref, terms, terms_core, terms_y,
     slots, s1, s2, wo, stream, hs, rows_all, mm, dup, tiles, qkv, kq, yb, dnum, dden, dden_t, dqkv,
@@ -964,16 +986,18 @@
         count, chunk = everyone.shape[0], everyone.shape[1]
         return [load(everyone.at[j], flat.at[pl.ds(j * chunk, chunk)]) for j in range(count)]
 
-    got_c = load(c_all, rows_all)
     got_m = load(m_all, mm)
     got_wd = whole(wd_all, s2)
+    got_terms = load(terms_all, s1)
+    got_c = load(c_all, rows_all)
     greet(peers)
+    ring = Scatter(slots, ring_send, ring_recv, nearby)
+    ring.begin(0, terms_all, ff)
     got_x1 = load(x1_in, x1)
     fill_tables(lengths, seq, tok_ref, line_ref, coef_ref, -1)
     columns = ring_columns(place)
     got_qkv = [load(qkv_all, qkv), load(yb_all, yb)]
     got_wo = whole(wo_all, wo)
-    ring = Scatter(slots, ring_send, ring_recv, nearby)
     sums = TpSum(part, from_core, from_y, tp_sems, credits, tp, over_y, over_core)
 
     def run(n, body, pumps=None):
@@ -1032,24 +1056,16 @@
 
         run(count, step, pumps)
 
-    got_c.wait()
     got_m.wait()
-
-    def grad_down(j):
-        s1[col(j), :] = dot_tt(rows_all[:, col(j)], mm[...]).astype(bf16)
-
-    run(2, grad_down)
-    begin(0)
-    lax.fori_loop(2, 8, lambda j, _: (grad_down(j), 0)[1], 0)
     for made in got_wd:
         made.wait()
-    events(0, 0, 1)
+    got_terms.wait()
 
     def mlp(i):
         sums.offer(i, 0, dot_t(mm[...], s2[col(i), :]))
         pl.when(i > 0)(lambda: sums.pass_on(i - 1, 0))
 
-    run(8, mlp, (0, 1, 2))
+    run(8, mlp, (0, 0, 2))
     sums.pass_on(7, 0)
 
     def gate_up_tiles(i, slot):
@@ -1077,7 +1093,8 @@
         sums.take(i, 0, use)
 
     got_x1.wait()
-    chunks_of(gate_up_tiles, 8, grad_gate_up, (0, 3, 4))
+    got_c.wait()
+    chunks_of(gate_up_tiles, 8, grad_gate_up, (0, 2, 4))
 
     def w_tiles(i, slot):
         return [(wg_all.at[i], stream.at[slot, 0]), (wu_all.at[i], stream.at[slot, 1])]
@@ -1088,7 +1105,7 @@
         sums.offer(i, 1, value)
         pl.when(i > 0)(lambda: sums.pass_on(i - 1, 1))
 
-    chunks_of(w_tiles, 8, grad_hidden, (0, 7, 2))
+    chunks_of(w_tiles, 8, grad_hidden, (0, 6, 4))
     kept = [load(own_rows.at[:, col(j)], block_out.at[:, c]) for j, c in enumerate(columns)]
     pending = []
     sums.pass_on(7, 1)
@@ -1106,7 +1123,7 @@
         keep_up(i, slot).start()
         pl.when(i == 1)(lambda: begin(1))
 
-    chunks_of(h_tiles(h2_all), 8, grads, (0, 9, 2))
+    chunks_of(h_tiles(h2_all), 8, grads, (0, 10, 2))
     keep_up(6, 0).wait()
     keep_up(7, 1).wait()
 
@@ -1116,7 +1133,6 @@
 
         sums.take(i, 1, use)
 
-    events(0, 11, 12)
     run(2, take_second)
     both(1, 0, 0, 12, 2)
     done = load(fout.at[:, pl.ds(0, ff)], d_out)
@@ -1420,6 +1436,7 @@
         shape(total, ff),
         shape(4, 256, 128, dtype=f32),
         shape(8, width, dtype=f32),
+        shape(width, ff),
     )
     scratch = [
         pltpu.VMEM((rows, width), bf16),
@@ -1549,13 +1566,78 @@
     return pl.pallas_call(
         bwd_kernel,
         out_shape=outs,
-        in_specs=[pl.BlockSpec(memory_space=pltpu.SMEM)] + [vmem] * 9 + [hbm] * 15,
+        in_specs=[pl.BlockSpec(memory_space=pltpu.SMEM)] + [vmem] * 9 + [hbm] * 16,
         out_specs=(hbm,) * len(outs),
         scratch_shapes=scratch,
         compiler_params=pltpu.CompilerParams(
             collective_id=1, has_side_effects=True, vmem_limit_bytes=62 * 2**20
         ),
     )(lengths, *constants, gains, s_in, den, *gain_pair, x_in, x1, *weights, c_all, *acts)
+
+
+def finish_kernel(
+    d_in, g_in, u_in, oq_in, block_in, input_in,
+    d_out, g_out, u_out, o_out, q_out, k_out, v_out, block_out, input_out,
+    wide, turned, oq, oq_t, sems,
+):
+    keeper = Sems(sems)
+    ff = d_in.shape[1]
+
+    def copy(src, dst):
+        made = pltpu.make_async_copy(src, dst, keeper.take())
+        made.start()
+        return made
+
+    came = [copy(ref, wide.at[i]) for i, ref in enumerate((g_in, u_in, d_in))]
+    came_oq = copy(oq_in, oq)
+    kept = [
+        copy(block_in, block_out),
+        copy(input_in, input_out),
+        copy(oq_in.at[:, pl.ds(640, 512)], v_out),
+    ]
+    came_oq.wait()
+    oq_t[...] = oq[:, 0:640].T
+    kept += [
+        copy(oq_t.at[pl.ds(0, 512)], o_out),
+        copy(oq_t.at[pl.ds(512, 64)], q_out),
+        copy(oq_t.at[pl.ds(576, 64)], k_out),
+    ]
+    for i, out in enumerate((g_out, u_out, d_out)):
+        came[i].wait()
+        for at in range(0, ff, 128):
+            at = min(at, ff - 128)
+            turned[i, at : at + 128, :] = wide[i, :, at : at + 128].T
+        kept.append(copy(turned.at[i], out))
+    for made in kept:
+        made.wait()
+
+
+def finish(d, g, u, oq, block, grad_input):
+    rows, width = block.shape
+    ff = d.shape[1]
+    hbm = pl.BlockSpec(memory_space=pl.ANY)
+
+    def shape(*dims, dtype=f32):
+        return jax.ShapeDtypeStruct(dims, dtype)
+
+    outs = (
+        shape(ff, 256), shape(ff, 256), shape(ff, 256), shape(512, 256), shape(64, 256),
+        shape(64, 256), shape(256, 512), shape(rows, width, dtype=bf16), shape(rows, width),
+    )
+    return pl.pallas_call(
+        finish_kernel,
+        out_shape=outs,
+        in_specs=[hbm] * 6,
+        out_specs=(hbm,) * len(outs),
+        scratch_shapes=[
+            pltpu.VMEM((3, 256, ff), f32),
+            pltpu.VMEM((3, ff, 256), f32),
+            pltpu.VMEM((256, 1152), f32),
+            pltpu.VMEM((640, 256), f32),
+            pltpu.SemaphoreType.DMA((16,)),
+        ],
+        compiler_params=pltpu.CompilerParams(vmem_limit_bytes=40 * 2**20),
+    )(d, g, u, oq, block, grad_input)
 
 
 def on_device_rings(
@@ -1571,23 +1653,27 @@
         lengths, constants, *gain_pair, inputs,
         (w_query.T, w_key.T, w_value, w_out, w_gate.T, w_up.T, w_down), cotangent,
     )
-    weights, (c_all, h1, qkv, yb, den, x1, h2, gate, up, mixed, s_in, gain_all) = made[:5], made[5:]
+    weights = made[:5]
+    c_all, h1, qkv, yb, den, x1, h2, gate, up, mixed, s_in, gain_all, terms = made[5:]
     sum_down_t, sum_gate, sum_up, sum_oq, block, grad_input, gain_sums, _ = backward_pass(
         lengths, constants, gain_all, s_in, den, gain_pair, inputs, x1, weights, c_all,
-        (h1, qkv, yb, h2, gate, up, mixed),
+        (h1, qkv, yb, h2, gate, up, mixed, terms),
+    )
+    d, g_t, u_t, o, q_t, k_t, v, block, grad_input = finish(
+        sum_down_t, sum_gate, sum_up, sum_oq, block, grad_input
     )
     return (
         block,
         grad_input,
         gain_sums[0],
-        sum_oq[:, 512:576],
-        sum_oq[:, 576:640],
-        sum_oq[:, 640:],
-        sum_oq[:, :512].T,
+        q_t.T,
+        k_t.T,
+        v,
+        o,
         gain_sums[1],
-        sum_gate,
-        sum_up,
-        sum_down_t.T,
+        g_t.T,
+        u_t.T,
+        d,
     )
 
 

time: 537 us -> 525 us (0.978)
  local copies, waits for them, and re-layouts: 16.7 us -> 9.51 us
    pallas_call x1, Pallas kernels: 251 us -> 242 us  [backward_pass(): pl.pallas_call(bwd_kernel, out_shape=outs, in_specs=[pl.BlockSpec(memory_...]
    unnamed x16 -> x12, local copies, waits for them, and re-layouts: 11.5 us -> 8.16 us
where the time goes in v5:
time: 525 us; the launch traced here: 518 us
  Pallas kernels  507 us (97%)
  local copies, waits for them, and re-layouts  9.51 us (2%)
    pallas_call x1, Pallas kernels, forward_pass(): pl.pallas_call(fwd_kernel, out_shape=outs, in_specs=[pl.BlockSpec(memory_...  261 us
    pallas_call x1, Pallas kernels, backward_pass(): pl.pallas_call(bwd_kernel, out_shape=outs, in_specs=[pl.BlockSpec(memory_...  242 us

profile of v5, /device:TPU:0, one launch (start us, length us, event | category | flops | bytes accessed | tf_op | source)
XLA Modules:
  0.0 517.6 jit_solution(2417284718160716003)
XLA Ops:
  0.6 260.9 %shard_map.239 = (bf16[8,256,640]{2,1,0:T(8,128)(2,1)}, bf16[8,256,512]{2,1,0:T(8,128)(2,1)}, bf16[8,256,1376]{2,1,0:T(8,128)(2,1)}, bf16[8,256,1376]{2,1,0:T(8,...) custom-call(s32[3]{0:T(128)} %lengths.3, ...), custom_call_target="tpu_custom_call" | custom-call | tf_op jit(solution)/shard_map/pallas_call | solution.py:1487
  261.5 241.6 %shard_map.240 = (f32[256,1376]{1,0:T(8,128)}, f32[256,1376]{1,0:T(8,128)}, f32[256,1376]{1,0:T(8,128)}, f32[256,1152]{1,0:T(8,128)}, bf16[256,2048]{1,0:T(8,128...) custom-call(s32[3]{0:T(128)} %lengths.3, bf16[4,128,256]{2,1,0:T(8,128)(2,1)} %constant.8.clone.sa_ref, ...), custom_call_target="tpu_custom_call" | custom-call | tf_op jit(solution)/shard_map/pallas_call | solution.py:1566
  503.1 0.0 copy-start
  503.1 1.6 copy-done
  504.7 0.0 copy-start.1
  504.7 1.4 copy-done.1
  506.0 0.0 copy-start.2
  506.0 1.4 copy-done.2
  507.4 0.0 copy-start.3
  507.4 1.4 copy-done.3
  508.8 0.0 copy-start.4
  508.8 1.3 copy-done.4
  510.0 0.0 copy-start.5
  510.0 1.2 copy-done.5
  511.3 4.5 shard_map.241
  515.8 1.3 fusion
Async XLA Ops:
  503.1 1.6 copy-start
  504.7 1.4 copy-start.1
  506.0 1.4 copy-start.2
  507.4 1.4 copy-start.3
  508.8 1.3 copy-start.4
  510.0 1.2 copy-start.5

commit v6 on v5

--- a/solution.py
+++ b/solution.py
@@ -314,10 +314,6 @@
             i = self.gang_of[a]
             if step == 3 and i + 1 < len(self.gangs):
                 mine, later = self.gangs[i].index(a), self.gangs[i + 1]
-                if i == 0:
-                    later = later + self.gangs[2]
-                elif i == 1:
-                    later = []
                 last = mine == len(self.gangs[i]) - 1
                 for other in later[mine:] if last else later[mine : mine + 1]:
                     self.go(other, 1, way, part)
@@ -416,49 +412,107 @@
             free = jnp.where((at >= lo * total) & (at < (hi + 1) * total), 0.0, free)
         return free
 
-    z, x = seq // 2, seq % 2
+    z = seq // 2
     one = jnp.ones((1, 128), f32)
-    if step > 0:
-        rows = [clear(2 * z + 1, 2 * z + 1), one * x.astype(f32), clear(2 * z, seq - 1)]
-    else:
-        rows = [clear(2 * z, 2 * z), one * (1 - x).astype(f32), clear(seq + 1, 2 * z + 1)]
-    rows.append(clear(2 * z, 2 * z + 1))
+    first, second = clear(2 * z, 2 * z), clear(2 * z + 1, 2 * z + 1)
+    before = 2 * (z - step)
+    rows = [second, first] if step > 0 else [first, second]
+    rows += [first * second, clear(before, before + 1)]
     coefs[...] = jnp.concatenate(rows + [one * 0.0] * 4, axis=0)
 
 
-class Chain:
-    def __init__(self, links, st_t, st_z, coefs, seq, z, step):
-        self.st_t, self.st_z, self.coefs = st_t, st_z, coefs
+class Exchange:
+    def __init__(self, links, st, near, term, first, second, given, states, coefs, seq, step):
+        z, x = seq // 2, seq % 2
+        self.st, self.near, self.term, self.first, self.second = st, near, term, first, second
+        self.given, self.states, self.coefs, self.x = given, states, coefs, x
         self.turn = z if step > 0 else 3 - z
-        self.hop = links.copy(st_t, st_z, seq=seq + 2 * step)
-
-    def move(self, turn):
-        @pl.when(self.turn == turn)
+        self.late = x if step > 0 else 1 - x
+        over_x = seq + 1 - 2 * x
+        self.half = links.start(st.at[pl.ds(2 * (1 - x), 2)], near, seq=over_x)
+        self.hop = links.copy(term, first, seq=seq + 2 * step)
+        self.on = links.copy(term, second, seq=seq + 2 * step)
+        self.far = links.copy(term, second, seq=seq + 4 * step)
+        self.links, self.over_x = links, over_x
+
+    def coef(self, k):
+        return self.coefs[k : k + 1, :]
+
+    def pair(self):
+        self.half.wait_recv()
+        for i in (0, 1):
+            mine, theirs = self.st[2 * self.x + i].astype(f32), self.near[i].astype(f32)
+            early = jnp.where(self.late == 0, mine, theirs)
+            later = jnp.where(self.late == 0, theirs, mine)
+            self.term[i] = (later + self.coef(0) * early).astype(bf16)
+
+        @pl.when(self.turn % 2 == 0)
         def _():
-            if turn > 0:
-                self.hop.wait_recv()
-            if turn < 3:
-                if turn > 0:
-                    for h in range(4):
-                        own = self.st_t[h].astype(f32)
-                        came = self.coefs[3:4, :] * self.st_z[h].astype(f32)
-                        self.st_t[h] = (own + came).astype(bf16)
-                self.hop.start()
-
-    def use(self, states, near):
-        for h in range(4):
-            states[h, 0:176, :] = self.coefs[1:2, :] * near[h].astype(f32)
-            states[h, 176:256, :] = jnp.zeros((80, 128), f32)
-
-        @pl.when(self.turn > 0)
+            self.hop.start()
+
+    def planes(self):
+        @pl.when(self.turn % 2 == 1)
         def _():
-            for h in range(4):
-                states[h, 0:176, :] += self.coefs[2:3, :] * self.st_z[h].astype(f32)
+            self.hop.wait_recv()
+
+        @pl.when(self.turn == 1)
+        def _():
+            for i in (0, 1):
+                came = self.coef(2) * self.first[i].astype(f32)
+                self.term[i] = (self.term[i].astype(f32) + came).astype(bf16)
+            self.on.start()
+            self.far.start()
+
+    def give(self):
+        x = self.x
+        for i in (0, 1):
+            self.states[2 * x + i] = jnp.zeros((256, 128), f32)
+            self.states[2 * (1 - x) + i] = jnp.zeros((256, 128), f32)
+
+        def enter(i):
+            return self.states.at[2 * x + i, pl.ds(0, 176)]
+
+        @pl.when(self.turn == 1)
+        def _():
+            for i in (0, 1):
+                enter(i)[...] = self.first[i].astype(f32)
+
+        @pl.when(self.turn == 2)
+        def _():
+            self.on.wait_recv()
+            for i in (0, 1):
+                enter(i)[...] = self.second[i].astype(f32)
+
+        @pl.when(self.turn == 3)
+        def _():
+            self.far.wait_recv()
+            for i in (0, 1):
+                older = self.coef(3) * self.second[i].astype(f32)
+                enter(i)[...] = self.first[i].astype(f32) + older
+
+        for i in (0, 1):
+            came = enter(i)[...]
+            mine, theirs = self.st[2 * x + i].astype(f32), self.near[i].astype(f32)
+            early = jnp.where(self.late == 0, mine, theirs)
+            passed = early + self.coef(1) * came
+            self.given[0, i] = jnp.where(self.late == 0, passed, came).astype(bf16)
+            enter(i)[...] = jnp.where(self.late == 0, came, passed)
+        self.back = self.links.start(self.given.at[0], self.given.at[1], seq=self.over_x)
+
+    def take(self):
+        self.back.wait_recv()
+        for i in (0, 1):
+            self.states[2 * (1 - self.x) + i, 0:176, :] = self.given[1, i].astype(f32)
 
     def finish(self):
-        @pl.when(self.turn < 3)
+        @pl.when(self.turn % 2 == 0)
         def _():
             self.hop.wait_send()
+
+        @pl.when(self.turn == 1)
+        def _():
+            self.on.wait_send()
+            self.far.wait_send()
 
 
 def ring_columns(place):
@@ -479,7 +533,7 @@
     x_ref, tok_ref, line_ref, coef_ref, gain_ref, q_own, o_own, g_own, u_own, d_own,
     w_small, w_v, w_o, w_d, w_g,
     xg, h1, wq, wo, wg, wu, qkv, kq, num, den, yb, sc, rc, sy, ry, x1, gate, up, mm,
-    gains_all, gains, st, st_x, st_t, st_z, s_in,
+    gains_all, gains, st, st_x, st_t, st_z, st_y, st_g, s_in,
     send, recv, local,
 ):
     seq, tp, place, nearby, over_y, over_core, peers = places()
@@ -618,8 +672,8 @@
             0, total // 256, state, (jnp.zeros((256, 128), f32), jnp.zeros((1, 256), f32))
         )
         pack_state(st, h, s, zz)
-        ring.pump(16 + (h + 1) // 2)
-    to_x = links.start(st, st_x, seq=seq + 1 - 2 * x)
+        ring.pump(17 + h)
+    moved = Exchange(links, st, st_x, st_t, st_z, st_y, st_g, s_in, coef_ref, seq, 1)
 
     def local_head(h):
         for i in range(total // 256):
@@ -635,25 +689,17 @@
             num[r, h * 128 : (h + 1) * 128] = dot(kap.astype(bf16), qkv[:span, head_v(h)])
 
     local_head(0)
-    ring.pump(19)
-    to_x.wait_recv()
-    for h in range(heads):
-        mine, theirs = st[h].astype(f32), st_x[h].astype(f32)
-        early = jnp.where(x == 0, mine, theirs)
-        later = jnp.where(x == 0, theirs, mine)
-        st_t[h] = (later + coef_ref[0:1, :] * early).astype(bf16)
-    chain = Chain(links, st_t, st_z, coef_ref, seq, z, 1)
-    chain.move(0)
+    ring.pump(22)
+    moved.pair()
     local_head(1)
-    chain.move(1)
-    ring.pump(20)
+    ring.pump(24)
+    moved.planes()
     local_head(2)
-    chain.move(2)
-    ring.pump(22)
+    ring.pump(26)
+    moved.give()
     local_head(3)
-    chain.move(3)
-    ring.pump(24)
-    chain.use(s_in, st_x)
+    ring.pump(28)
+    moved.take()
     store(s_in, sin_out)
     for h in range(heads):
         z_row = jnp.concatenate([s_in[h, 160:161, :], s_in[h, 161:162, :]], axis=1)
@@ -673,7 +719,7 @@
             return 0
 
         lax.fori_loop(0, total // 256, carry, 0)
-        ring.pump(25 + h)
+        ring.pump(28 + (h + 1) // 2)
     store(yb, yb_out)
     store(den, den_out)
     ring.pump_array(1)
@@ -801,7 +847,7 @@
     for made in pending:
         made.wait()
     links.finish()
-    chain.finish()
+    moved.finish()
 
 
 def pack_state(st, h, s, zz):
@@ -966,7 +1012,7 @@
     d_out, g_out, u_out, oq_out, block_out, input_out, gain_out, u_kept,
     tok_ref, line_ref, coef_ref, terms, terms_core, terms_y,
     slots, s1, s2, wo, stream, hs, rows_all, mm, dup, tiles, qkv, kq, yb, dnum, dden, dden_t, dqkv,
-    dq, dk, part, from_core, from_y, acc, x1, fout, st, st_x, st_t, st_z, s_back, own_rows,
+    dq, dk, part, from_core, from_y, acc, x1, fout, st, st_x, st_t, st_z, st_y, st_g, s_back, own_rows,
     ring_send, ring_recv, tp_sems, credits, send, recv, local, tile_sems,
 ):
     seq, tp, place, nearby, over_y, over_core, peers = places()
@@ -1215,7 +1261,7 @@
             0, 4, state, (jnp.zeros((256, 128), f32), jnp.zeros((1, 256), f32))
         )
         pack_state(st, h, s, zz)
-    to_x = links.start(st, st_x, seq=seq + 1 - 2 * x)
+    moved = Exchange(links, st, st_x, st_t, st_z, st_y, st_g, s_back, coef_ref, seq, -1)
     both(1, 7, 2, 4, 1)
 
     dq[...] = jnp.zeros(dq.shape, f32)
@@ -1248,25 +1294,17 @@
                 dk[k_rows, :] += dk_s
 
     local_head(0)
-    to_x.wait_recv()
-    for h in range(4):
-        mine, theirs = st[h].astype(f32), st_x[h].astype(f32)
-        first = jnp.where(x == 0, mine, theirs)
-        second = jnp.where(x == 0, theirs, mine)
-        st_t[h] = (first + coef_ref[0:1, :] * second).astype(bf16)
-    chain = Chain(links, st_t, st_z, coef_ref, seq, z, -1)
-    chain.move(0)
+    moved.pair()
     both(1, 8, 2, 5, 1)
     local_head(1)
-    chain.move(1)
+    moved.planes()
     both(1, 9, 2, 6, 1)
     local_head(2)
-    chain.move(2)
+    moved.give()
     both(1, 10, 2, 7, 1)
     local_head(3)
-    chain.move(3)
     both(1, 11, 2, 8, 1)
-    chain.use(s_back, st_x)
+    moved.take()
 
     def split_state(ref, h):
         z_row = jnp.concatenate([ref[h, 160:161, :], ref[h, 161:162, :]], axis=1)
@@ -1380,7 +1418,7 @@
     for made in pending:
         made.wait()
     links.finish()
-    chain.finish()
+    moved.finish()
 
 
 def feature_tables(heads):
@@ -1476,9 +1514,11 @@
         pltpu.VMEM((8, 16, 256), bf16),
         pltpu.VMEM((8, width), f32),
         pltpu.VMEM((4, 176, 128), bf16),
-        pltpu.VMEM((4, 176, 128), bf16),
-        pltpu.VMEM((4, 176, 128), bf16),
-        pltpu.VMEM((4, 176, 128), bf16),
+        pltpu.VMEM((2, 176, 128), bf16),
+        pltpu.VMEM((2, 176, 128), bf16),
+        pltpu.VMEM((2, 176, 128), bf16),
+        pltpu.VMEM((2, 176, 128), bf16),
+        pltpu.VMEM((2, 2, 176, 128), bf16),
         pltpu.VMEM((4, 256, 128), f32),
         pltpu.SemaphoreType.DMA((112,)),
         pltpu.SemaphoreType.DMA((112,)),
@@ -1549,9 +1589,11 @@
         pltpu.VMEM((rows, width), f32),
         pltpu.VMEM((256, ff), f32),
         pltpu.VMEM((4, 176, 128), bf16),
-        pltpu.VMEM((4, 176, 128), bf16),
-        pltpu.VMEM((4, 176, 128), bf16),
-        pltpu.VMEM((4, 176, 128), bf16),
+        pltpu.VMEM((2, 176, 128), bf16),
+        pltpu.VMEM((2, 176, 128), bf16),
+        pltpu.VMEM((2, 176, 128), bf16),
+        pltpu.VMEM((2, 176, 128), bf16),
+        pltpu.VMEM((2, 2, 176, 128), bf16),
         pltpu.VMEM((4, 256, 128), f32),
         pltpu.VMEM((rows, width), bf16),
         pltpu.SemaphoreType.DMA((2, 2, 2)),
@@ -1636,7 +1678,7 @@
             pltpu.VMEM((640, 256), f32),
             pltpu.SemaphoreType.DMA((16,)),
         ],
-        compiler_params=pltpu.CompilerParams(vmem_limit_bytes=40 * 2**20),
+        compiler_params=pltpu.CompilerParams(vmem_limit_bytes=60 * 2**20),
     )(d, g, u, oq, block, grad_input)
 
 

time: 525 us -> 624 us (1.19)
  Pallas kernels: 507 us -> 614 us
  local copies, waits for them, and re-layouts: 9.51 us -> 1.34 us
    pallas_call x1, Pallas kernels: 4.5 us -> 112 us  [finish(): pl.pallas_call(finish_kernel, out_shape=outs, in_specs=[hbm] * 6, out_spe...]
    unnamed x12 -> x0, local copies, waits for them, and re-layouts: 8.16 us -> none
where the time goes in v6:
time: 624 us; the launch traced here: 616 us
  Pallas kernels  614 us (98%)
    pallas_call x1, Pallas kernels, forward_pass(): pl.pallas_call(fwd_kernel, out_shape=outs, in_specs=[pl.BlockSpec(memory_...  259 us
    pallas_call x1, Pallas kernels, backward_pass(): pl.pallas_call(bwd_kernel, out_shape=outs, in_specs=[pl.BlockSpec(memory_...  242 us
    pallas_call x1, Pallas kernels, finish(): pl.pallas_call(finish_kernel, out_shape=outs, in_specs=[hbm] * 6, out_spe...  112 us

profile of v6, /device:TPU:0, one launch (start us, length us, event | category | flops | bytes accessed | tf_op | source)
XLA Modules:
  0.0 616.1 jit_solution(1061071078446961272)
XLA Ops:
  0.6 258.7 %shard_map.239 = (bf16[8,256,640]{2,1,0:T(8,128)(2,1)}, bf16[8,256,512]{2,1,0:T(8,128)(2,1)}, bf16[8,256,1376]{2,1,0:T(8,128)(2,1)}, bf16[8,256,1376]{2,1,0:T(8,...) custom-call(s32[3]{0:T(128)} %lengths.3, ...), custom_call_target="tpu_custom_call" | custom-call | tf_op jit(solution)/shard_map/pallas_call | solution.py:1527
  259.4 242.5 %shard_map.240 = (f32[256,1376]{1,0:T(8,128)}, f32[256,1376]{1,0:T(8,128)}, f32[256,1376]{1,0:T(8,128)}, f32[256,1152]{1,0:T(8,128)}, bf16[256,2048]{1,0:T(8,128...) custom-call(s32[3]{0:T(128)} %lengths.3, bf16[4,128,256]{2,1,0:T(8,128)(2,1)} %constant.8.clone.sa_ref, ...), custom_call_target="tpu_custom_call" | custom-call | tf_op jit(solution)/shard_map/pallas_call | solution.py:1608
  501.9 112.4 %shard_map.241 = (f32[1376,256]{1,0:T(8,128)}, f32[1376,256]{1,0:T(8,128)}, f32[1376,256]{1,0:T(8,128)}, f32[512,256]{1,0:T(8,128)}, f32[64,256]{1,0:T(8,128)}, ...) custom-call(f32[256,1376]{1,0:T(8,128)} %get-tuple-element.63.d_in, ...), custom_call_target="tpu_custom_call" | custom-call | tf_op jit(solution)/shard_map/pallas_call | solution.py:1669
  614.3 1.3 fusion

commit v7 on v6

--- a/solution.py
+++ b/solution.py
@@ -531,7 +531,7 @@
     wq_all, wo_all, wg_all, wu_all, wd_all, c_all,
     h1_out, qkv_out, yb_out, den_out, x1_out, h2_out, gate_out, up_out, m_out, sin_out, gain_out, terms_out,
     x_ref, tok_ref, line_ref, coef_ref, gain_ref, q_own, o_own, g_own, u_own, d_own,
-    w_small, w_v, w_o, w_d, w_g,
+    w_small, w_v, w_o, w_d, w_g, c_v,
     xg, h1, wq, wo, wg, wu, qkv, kq, num, den, yb, sc, rc, sy, ry, x1, gate, up, mm,
     gains_all, gains, st, st_x, st_t, st_z, st_y, st_g, s_in,
     send, recv, local,
@@ -559,7 +559,7 @@
     columns = ring_columns(place)
     got_x = [load(x_in.at[:, c], x_ref.at[:, col(j)]) for j, c in enumerate(columns)]
     c_rows = pl.ds(pl.multiple_of(tp * rows, rows), rows)
-    got_c = [load(c_in.at[:, c], c_all.at[c_rows, col(j)]) for j, c in enumerate(columns)]
+    got_c = [load(c_in.at[:, c], c_v.at[:, col(j)]) for j, c in enumerate(columns)]
     got_o = load(wo_in, w_o)
     ff = wd_in.shape[0]
     got_g = load(wg_in, w_g.at[pl.ds(0, ff)])
@@ -637,7 +637,8 @@
     kept_h1 = load(h1, h1_out)
     for made in got_c:
         made.wait()
-    crows = Rows(links, c_all.at[c_rows], c_all, tp, over_y, over_core, rows)
+    crows = Rows(links, c_v, c_all, tp, over_y, over_core, rows)
+    kept_c = load(c_v, c_all.at[c_rows])
     ring.pump(15)
     for made in got:
         made.wait()
@@ -797,6 +798,7 @@
     own_in.wait()
     store(h2, h2_out)
     kept_h1.wait()
+    kept_c.wait()
     got_c = load(c_all, h1)
     ring.pump_array(2)
     own_kept[2].wait()
@@ -1492,6 +1494,7 @@
         pltpu.VMEM((512, 256), f32),
         pltpu.VMEM((-(-ff // 128) * 128, 256), f32),
         pltpu.VMEM((-(-ff // 128) * 128, 256), f32),
+        pltpu.VMEM((rows, width), bf16),
         pltpu.VMEM((total, width), bf16),
         pltpu.VMEM((total, width), bf16),
         pltpu.VMEM((width, 640), bf16),
@@ -1620,7 +1623,7 @@
 def finish_kernel(
     d_in, g_in, u_in, oq_in, block_in, input_in,
     d_out, g_out, u_out, o_out, q_out, k_out, v_out, block_out, input_out,
-    wide, turned, oq, oq_t, sems,
+    wide, turned, oq, oq_t, block, grad, sems,
 ):
     keeper = Sems(sems)
     ff = d_in.shape[1]
@@ -1632,14 +1635,11 @@
 
     came = [copy(ref, wide.at[i]) for i, ref in enumerate((g_in, u_in, d_in))]
     came_oq = copy(oq_in, oq)
-    kept = [
-        copy(block_in, block_out),
-        copy(input_in, input_out),
-        copy(oq_in.at[:, pl.ds(640, 512)], v_out),
-    ]
+    came_block, came_grad = copy(block_in, block), copy(input_in, grad)
     came_oq.wait()
     oq_t[...] = oq[:, 0:640].T
-    kept += [
+    kept = [
+        copy(oq.at[:, pl.ds(640, 512)], v_out),
         copy(oq_t.at[pl.ds(0, 512)], o_out),
         copy(oq_t.at[pl.ds(512, 64)], q_out),
         copy(oq_t.at[pl.ds(576, 64)], k_out),
@@ -1650,6 +1650,10 @@
             at = min(at, ff - 128)
             turned[i, at : at + 128, :] = wide[i, :, at : at + 128].T
         kept.append(copy(turned.at[i], out))
+    came_block.wait()
+    kept.append(copy(block, block_out))
+    came_grad.wait()
+    kept.append(copy(grad, input_out))
     for made in kept:
         made.wait()
 
@@ -1676,7 +1680,9 @@
             pltpu.VMEM((3, ff, 256), f32),
             pltpu.VMEM((256, 1152), f32),
             pltpu.VMEM((640, 256), f32),
-            pltpu.SemaphoreType.DMA((16,)),
+            pltpu.VMEM((rows, width), bf16),
+            pltpu.VMEM((rows, width), f32),
+            pltpu.SemaphoreType.DMA((24,)),
         ],
         compiler_params=pltpu.CompilerParams(vmem_limit_bytes=60 * 2**20),
     )(d, g, u, oq, block, grad_input)

time: 624 us -> 518 us (0.83)
  Pallas kernels: 614 us -> 508 us
    pallas_call x1, Pallas kernels: 112 us -> 6.7 us  [finish(): pl.pallas_call(finish_kernel, out_shape=outs, in_specs=[hbm] * 6, out_spe...]
where the time goes in v7:
time: 518 us; the launch traced here: 510 us
  Pallas kernels  508 us (98%)
    pallas_call x1, Pallas kernels, forward_pass(): pl.pallas_call(fwd_kernel, out_shape=outs, in_specs=[pl.BlockSpec(memory_...  259 us
    pallas_call x1, Pallas kernels, backward_pass(): pl.pallas_call(bwd_kernel, out_shape=outs, in_specs=[pl.BlockSpec(memory_...  243 us

profile of v7, /device:TPU:0, one launch (start us, length us, event | category | flops | bytes accessed | tf_op | source)
XLA Modules:
  0.0 510.4 jit_solution(7391013783181050593)
XLA Ops:
  0.6 258.7 %shard_map.239 = (bf16[8,256,640]{2,1,0:T(8,128)(2,1)}, bf16[8,256,512]{2,1,0:T(8,128)(2,1)}, bf16[8,256,1376]{2,1,0:T(8,128)(2,1)}, bf16[8,256,1376]{2,1,0:T(8,...) custom-call(s32[3]{0:T(128)} %lengths.3, ...), custom_call_target="tpu_custom_call" | custom-call | tf_op jit(solution)/shard_map/pallas_call | solution.py:1530
  259.4 242.5 %shard_map.240 = (f32[256,1376]{1,0:T(8,128)}, f32[256,1376]{1,0:T(8,128)}, f32[256,1376]{1,0:T(8,128)}, f32[256,1152]{1,0:T(8,128)}, bf16[256,2048]{1,0:T(8,128...) custom-call(s32[3]{0:T(128)} %lengths.3, bf16[4,128,256]{2,1,0:T(8,128)(2,1)} %constant.8.clone.sa_ref, ...), custom_call_target="tpu_custom_call" | custom-call | tf_op jit(solution)/shard_map/pallas_call | solution.py:1611
  501.9 6.7 %shard_map.241 = (f32[1376,256]{1,0:T(8,128)}, f32[1376,256]{1,0:T(8,128)}, f32[1376,256]{1,0:T(8,128)}, f32[512,256]{1,0:T(8,128)}, f32[64,256]{1,0:T(8,128)}, ...) custom-call(f32[256,1376]{1,0:T(8,128)} %get-tuple-element.63.d_in, ...), custom_call_target="tpu_custom_call" | custom-call | tf_op jit(solution)/shard_map/pallas_call | solution.py:1673
  508.6 1.3 fusion

commit v8 on v7

--- a/solution.py
+++ b/solution.py
@@ -239,6 +239,7 @@
 
     def take(self):
         self.used += 1
+        assert self.used <= self.ref.shape[0]
         return self.ref.at[self.used - 1]
 
 
@@ -273,8 +274,8 @@
 
 
 class Gather:
-    def __init__(self, links, arrays, split, nearby, gangs):
-        self.links, self.arrays, self.split, self.nearby = links, arrays, split, nearby
+    def __init__(self, links, arrays, nearby, gangs):
+        self.links, self.arrays, self.nearby = links, arrays, nearby
         self.at = {k: j for j, k in enumerate(relative_list(8))}
         self.flying, self.gangs, self.done = {}, gangs, 0
         self.gang_of = {a: i for i, gang in enumerate(gangs) for a in gang}
@@ -292,16 +293,17 @@
                 for way in (0, 1):
                     self.go(a, 1, way, part)
 
-    def rows(self, part):
-        return pl.ds(part * self.split, self.split)
+    def rows(self, a, part):
+        first, size = self.arrays[a][2:]
+        return pl.ds(first + part * size, size)
 
     def go(self, a, step, way, part):
-        own, everyone = self.arrays[a]
+        own, everyone = self.arrays[a][:2]
         before, after = (step - 1, step) if way == 0 else ((9 - step) % 8, 8 - step)
         src = own if step == 1 else everyone.at[self.at[before]]
         self.flying[a, step, way, part] = self.links.start(
-            src.at[self.rows(part)],
-            everyone.at[self.at[after], self.rows(part)],
+            src.at[self.rows(a, part)],
+            everyone.at[self.at[after], self.rows(a, part)],
             seq=self.nearby[way],
         )
 
@@ -586,10 +588,17 @@
     q_own[:, 128:640] = w_v[...].astype(bf16)
     ring = Gather(
         links,
-        [(q_own, wq_all), (o_own, wo_all), (g_own, wg_all), (u_own, wu_all), (d_own, wd_all)],
-        128,
+        [
+            (q_own, wq_all, 0, 128),
+            (o_own, wo_all, 0, 128),
+            (g_own, wg_all, 0, 64),
+            (g_own, wg_all, 128, 64),
+            (u_own, wu_all, 0, 64),
+            (u_own, wu_all, 128, 64),
+            (d_own, wd_all, 0, 128),
+        ],
         nearby,
-        [[0], [1], [2, 3], [4]],
+        [[0], [1], [2], [3, 4, 5], [6]],
     )
     own_in = [
         load(x_ref, xrows.block(tp, 0, rows)),
@@ -606,7 +615,8 @@
     turn(w_d, d_own)
     got_u.wait()
     turn(w_g, u_own)
-    own_kept = [load(own, everyone.at[at[0]]) for own, everyone in ring.arrays]
+    pairs = [(q_own, wq_all), (o_own, wo_all), (g_own, wg_all), (u_own, wu_all), (d_own, wd_all)]
+    own_kept = [load(own, everyone.at[at[0]]) for own, everyone in pairs]
     fill_tables(lengths, seq, tok_ref, line_ref, coef_ref, 1)
 
     ring.pump(6)
@@ -720,7 +730,7 @@
             return 0
 
         lax.fori_loop(0, total // 256, carry, 0)
-        ring.pump(28 + (h + 1) // 2)
+        ring.pump(31 + 2 * h)
     store(yb, yb_out)
     store(den, den_out)
     ring.pump_array(1)
@@ -747,7 +757,7 @@
         to_core.append(links.start(sc.at[yy], rc.at[yy], tp=over_core))
     for made in to_core:
         made.wait_recv()
-    ring.pump(32)
+    ring.pump(40)
 
     def away_cols(i, _):
         c = pl.ds(pl.multiple_of(i * cols, cols), cols)
@@ -766,9 +776,9 @@
         return 0
 
     lax.fori_loop(0, 2048 // cols, own_cols, 0)
-    ring.pump(34)
+    ring.pump(44)
     to_y.wait_recv()
-    ring.pump(37)
+    ring.pump(54)
 
     links.sent_now(xrows.first + [xrows.near])
     ho = x_ref
@@ -787,9 +797,9 @@
     h2 = xg
     hrows = Rows(links, ho, h2, tp, over_y, over_core, rows)
     own_in = load(ho, hrows.block(tp, 0, rows))
-    ring.pump(40)
+    ring.pump(56)
     hrows.forward(0)
-    ring.pump(43)
+    ring.pump(63)
     hrows.forward(1)
     crows.forward(0)
     crows.forward(1)
@@ -800,10 +810,9 @@
     kept_h1.wait()
     kept_c.wait()
     got_c = load(c_all, h1)
-    ring.pump_array(2)
+    ring.pump_array(3)
     own_kept[2].wait()
     got = load_weights(load, wg_all, wg)
-    ring.pump_array(3)
     own_kept[3].wait()
     got += load_weights(load, wu_all, wu)
     for made in got:
@@ -820,12 +829,12 @@
 
     for quarter in range(4):
         lax.fori_loop(quarter * total // 512, (quarter + 1) * total // 512, gate_up, 0)
-        ring.pump(58 + 2 * quarter)
+        ring.pump(86 + 2 * quarter)
     store(gate, gate_out)
     store(up, up_out)
     store(mm, m_out)
     got_c.wait()
-    links.sent_now([ring.flying[a, 1, way, part] for a in (2, 3) for way in (0, 1) for part in (0, 1)])
+    links.sent_now([ring.flying[a, 1, way, part] for a in (2, 3, 4, 5) for way in (0, 1) for part in (0, 1)])
     out_sems = [locs.take(), locs.take()]
     buffers = [g_own, u_own]
 
@@ -840,11 +849,11 @@
         return 0
 
     lax.fori_loop(0, 2, grad_down, 0)
-    ring.pump(66)
+    ring.pump(94)
     lax.fori_loop(2, 4, grad_down, 0)
     for k in (0, 1):
         keep_terms(6 + k, k).wait()
-    ring.pump_array(4)
+    ring.pump_array(6)
     own_kept[4].wait()
     for made in pending:
         made.wait()
@@ -1187,10 +1196,8 @@
     got_up = load(u_kept, s1)
     lax.fori_loop(2, 5, lambda i, _: (take_second(i), 0)[1], 0)
     events(1, 2, 3)
-    got_up.wait()
-    begin(2)
     lax.fori_loop(5, 8, lambda i, _: (take_second(i), 0)[1], 0)
-    both(1, 3, 2, 0, 1)
+    events(1, 3, 4)
 
     for made in kept:
         made.wait()
@@ -1213,10 +1220,11 @@
     da = Rows(links, own_rows, rows_all, tp, over_y, over_core, rows)
     own_in = load(own_rows, da.block(tp, 0, rows))
 
-    both(1, 4, 2, 1, 1)
+    events(1, 4, 6)
     da.forward(0)
-    both(1, 5, 2, 2, 1)
+    events(1, 6, 8)
     da.forward(1)
+    events(1, 8, 9)
     for made in got_qkv + got_wo:
         made.wait()
     da.finish()
@@ -1247,7 +1255,7 @@
         dden_t[i] = packed.T[0:8, :]
 
     run(4, grad_attended)
-    both(1, 6, 2, 3, 1)
+    events(1, 9, 10)
 
     for h in range(4):
 
@@ -1264,7 +1272,7 @@
         )
         pack_state(st, h, s, zz)
     moved = Exchange(links, st, st_x, st_t, st_z, st_y, st_g, s_back, coef_ref, seq, -1)
-    both(1, 7, 2, 4, 1)
+    events(1, 10, 11)
 
     dq[...] = jnp.zeros(dq.shape, f32)
 
@@ -1297,15 +1305,19 @@
 
     local_head(0)
     moved.pair()
-    both(1, 8, 2, 5, 1)
+    events(1, 11, 12)
+    got_up.wait()
+    begin(2)
     local_head(1)
     moved.planes()
-    both(1, 9, 2, 6, 1)
+    done.wait()
+    events(1, 12, 14)
+    done = load(fout.at[:, pl.ds(0, ff)], g_out)
     local_head(2)
     moved.give()
-    both(1, 10, 2, 7, 1)
+    events(2, 0, 2)
     local_head(3)
-    both(1, 11, 2, 8, 1)
+    events(2, 2, 3)
     moved.take()
 
     def split_state(ref, h):
@@ -1344,9 +1356,7 @@
         dqkv[r, 0:128] = (dq[r, :] + pltpu.roll(dk[r, :], 64, 1)).astype(bf16)
 
     run(4, join)
-    done.wait()
-    both(1, 12, 2, 9, 2)
-    done = load(fout.at[:, pl.ds(0, ff)], g_out)
+    events(2, 3, 5)
     own_w = load(wg_all.at[7], stream.at[0, 0])
     own_w.wait()
     gain_two = jnp.sum(fout[:, 0:ff] * stream[0, 0].astype(f32), axis=1, keepdims=True)
@@ -1358,7 +1368,7 @@
         sums.offer(i, 2, dot_t(dqkv[...], stream[slot, 0, :, 0:640]))
         pl.when(i > 0)(lambda: sums.pass_on(i - 1, 2))
 
-    chunks_of(wq_tiles, 8, grad_hidden_first, (2, 11, 1))
+    chunks_of(wq_tiles, 8, grad_hidden_first, (2, 5, 2))
     sums.pass_on(7, 2)
 
     def grad_out_qkv(i, slot):
@@ -1367,9 +1377,10 @@
 
         pl.when(i == 1)(lambda: begin(3))
 
-    chunks_of(h_tiles(h1_all), 8, grad_out_qkv, (3, 0, 1))
+    chunks_of(h_tiles(h1_all), 8, grad_out_qkv, (2, 7, 2))
+    both(2, 9, 3, 0, 3)
     done.wait()
-    both(2, 12, 3, 1, 2)
+    both(2, 12, 3, 3, 2)
     done = load(fout.at[:, pl.ds(0, ff)], u_out)
     def take_first(i):
         def use(value):
@@ -1377,7 +1388,7 @@
 
         sums.take(i, 2, use)
 
-    run(8, take_first, (3, 3, 4))
+    run(8, take_first, (3, 5, 4))
     for made in got_x:
         made.wait()
 
@@ -1397,7 +1408,7 @@
     own_w.wait()
     own_q.wait()
     gain_two += jnp.sum(fout[:, 0:ff] * stream[0, 0].astype(f32), axis=1, keepdims=True)
-    events(3, 7, 12)
+    events(3, 9, 12)
     done.wait()
     events(3, 12, 14)
     pending.append(load(fout.at[:, pl.ds(0, 1152)], oq_out))
@@ -1523,9 +1534,9 @@
         pltpu.VMEM((2, 176, 128), bf16),
         pltpu.VMEM((2, 2, 176, 128), bf16),
         pltpu.VMEM((4, 256, 128), f32),
-        pltpu.SemaphoreType.DMA((112,)),
-        pltpu.SemaphoreType.DMA((112,)),
-        pltpu.SemaphoreType.DMA((112,)),
+        pltpu.SemaphoreType.DMA((144,)),
+        pltpu.SemaphoreType.DMA((144,)),
+        pltpu.SemaphoreType.DMA((144,)),
     ]
     return pl.pallas_call(
         fwd_kernel,

time: 518 us -> 523 us (level)
    pallas_call x1, Pallas kernels: 243 us -> 255 us  [backward_pass(): pl.pallas_call(bwd_kernel, out_shape=outs, in_specs=[pl.BlockSpec(memory_...]
    pallas_call x1, Pallas kernels: 259 us -> 251 us  [forward_pass(): pl.pallas_call(fwd_kernel, out_shape=outs, in_specs=[pl.BlockSpec(memory_...]
where the time goes in v8:
time: 523 us; the launch traced here: 516 us
  Pallas kernels  513 us (98%)
    pallas_call x1, Pallas kernels, backward_pass(): pl.pallas_call(bwd_kernel, out_shape=outs, in_specs=[pl.BlockSpec(memory_...  255 us
    pallas_call x1, Pallas kernels, forward_pass(): pl.pallas_call(fwd_kernel, out_shape=outs, in_specs=[pl.BlockSpec(memory_...  251 us

profile of v8, /device:TPU:0, one launch (start us, length us, event | category | flops | bytes accessed | tf_op | source)
XLA Modules:
  0.0 515.7 jit_solution(6663046678124211367)
XLA Ops:
  0.6 251.3 %shard_map.239 = (bf16[8,256,640]{2,1,0:T(8,128)(2,1)}, bf16[8,256,512]{2,1,0:T(8,128)(2,1)}, bf16[8,256,1376]{2,1,0:T(8,128)(2,1)}, bf16[8,256,1376]{2,1,0:T(8,...) custom-call(s32[3]{0:T(128)} %lengths.3, ...), custom_call_target="tpu_custom_call" | custom-call | tf_op jit(solution)/shard_map/pallas_call | solution.py:1541
  251.9 255.3 %shard_map.240 = (f32[256,1376]{1,0:T(8,128)}, f32[256,1376]{1,0:T(8,128)}, f32[256,1376]{1,0:T(8,128)}, f32[256,1152]{1,0:T(8,128)}, bf16[256,2048]{1,0:T(8,128...) custom-call(s32[3]{0:T(128)} %lengths.3, bf16[4,128,256]{2,1,0:T(8,128)(2,1)} %constant.8.clone.sa_ref, ...), custom_call_target="tpu_custom_call" | custom-call | tf_op jit(solution)/shard_map/pallas_call | solution.py:1622
  507.3 6.7 %shard_map.241 = (f32[1376,256]{1,0:T(8,128)}, f32[1376,256]{1,0:T(8,128)}, f32[1376,256]{1,0:T(8,128)}, f32[512,256]{1,0:T(8,128)}, f32[64,256]{1,0:T(8,128)}, ...) custom-call(f32[256,1376]{1,0:T(8,128)} %get-tuple-element.63.d_in, ...), custom_call_target="tpu_custom_call" | custom-call | tf_op jit(solution)/shard_map/pallas_call | solution.py:1684
  514.0 1.3 fusion

commit v9 on v8

--- a/solution.py
+++ b/solution.py
@@ -1196,8 +1196,10 @@
     got_up = load(u_kept, s1)
     lax.fori_loop(2, 5, lambda i, _: (take_second(i), 0)[1], 0)
     events(1, 2, 3)
+    got_up.wait()
+    begin(2)
     lax.fori_loop(5, 8, lambda i, _: (take_second(i), 0)[1], 0)
-    events(1, 3, 4)
+    both(1, 3, 2, 0, 1)
 
     for made in kept:
         made.wait()
@@ -1220,11 +1222,10 @@
     da = Rows(links, own_rows, rows_all, tp, over_y, over_core, rows)
     own_in = load(own_rows, da.block(tp, 0, rows))
 
-    events(1, 4, 6)
+    both(1, 4, 2, 1, 1)
     da.forward(0)
-    events(1, 6, 8)
+    both(1, 5, 2, 2, 1)
     da.forward(1)
-    events(1, 8, 9)
     for made in got_qkv + got_wo:
         made.wait()
     da.finish()
@@ -1255,7 +1256,7 @@
         dden_t[i] = packed.T[0:8, :]
 
     run(4, grad_attended)
-    events(1, 9, 10)
+    both(1, 6, 2, 3, 1)
 
     for h in range(4):
 
@@ -1272,7 +1273,7 @@
         )
         pack_state(st, h, s, zz)
     moved = Exchange(links, st, st_x, st_t, st_z, st_y, st_g, s_back, coef_ref, seq, -1)
-    events(1, 10, 11)
+    both(1, 7, 2, 4, 1)
 
     dq[...] = jnp.zeros(dq.shape, f32)
 
@@ -1305,19 +1306,15 @@
 
     local_head(0)
     moved.pair()
-    events(1, 11, 12)
-    got_up.wait()
-    begin(2)
+    both(1, 8, 2, 5, 1)
     local_head(1)
     moved.planes()
-    done.wait()
-    events(1, 12, 14)
-    done = load(fout.at[:, pl.ds(0, ff)], g_out)
+    both(1, 9, 2, 6, 1)
     local_head(2)
     moved.give()
-    events(2, 0, 2)
+    both(1, 10, 2, 7, 1)
     local_head(3)
-    events(2, 2, 3)
+    both(1, 11, 2, 8, 1)
     moved.take()
 
     def split_state(ref, h):
@@ -1356,8 +1353,18 @@
         dqkv[r, 0:128] = (dq[r, :] + pltpu.roll(dk[r, :], 64, 1)).astype(bf16)
 
     run(4, join)
-    events(2, 3, 5)
+    done.wait()
+    both(1, 12, 2, 9, 2)
+    done = load(fout.at[:, pl.ds(0, ff)], g_out)
     own_w = load(wg_all.at[7], stream.at[0, 0])
+
+    def grad_out_qkv(i, slot):
+        s2[col(i), 0:512] = dot_tt(rows_all[:, col(i)], yb[...]).astype(bf16)
+        s2[col(i), 512:1152] = dot_tt(hs[slot], dqkv[...]).astype(bf16)
+        pl.when(i == 1)(lambda: begin(3))
+
+    chunks_of(h_tiles(h1_all), 8, grad_out_qkv, (2, 11, 1))
+
     own_w.wait()
     gain_two = jnp.sum(fout[:, 0:ff] * stream[0, 0].astype(f32), axis=1, keepdims=True)
 
@@ -1368,27 +1375,19 @@
         sums.offer(i, 2, dot_t(dqkv[...], stream[slot, 0, :, 0:640]))
         pl.when(i > 0)(lambda: sums.pass_on(i - 1, 2))
 
-    chunks_of(wq_tiles, 8, grad_hidden_first, (2, 5, 2))
+    chunks_of(wq_tiles, 8, grad_hidden_first, (3, 0, 1))
     sums.pass_on(7, 2)
-
-    def grad_out_qkv(i, slot):
-        s2[col(i), 0:512] = dot_tt(rows_all[:, col(i)], yb[...]).astype(bf16)
-        s2[col(i), 512:1152] = dot_tt(hs[slot], dqkv[...]).astype(bf16)
-
-        pl.when(i == 1)(lambda: begin(3))
-
-    chunks_of(h_tiles(h1_all), 8, grad_out_qkv, (2, 7, 2))
-    both(2, 9, 3, 0, 3)
     done.wait()
-    both(2, 12, 3, 3, 2)
+    both(2, 12, 3, 1, 2)
     done = load(fout.at[:, pl.ds(0, ff)], u_out)
+
     def take_first(i):
         def use(value):
             x1[:, col(i)] = value
 
         sums.take(i, 2, use)
 
-    run(8, take_first, (3, 5, 4))
+    run(8, take_first, (3, 3, 4))
     for made in got_x:
         made.wait()
 
@@ -1408,7 +1407,7 @@
     own_w.wait()
     own_q.wait()
     gain_two += jnp.sum(fout[:, 0:ff] * stream[0, 0].astype(f32), axis=1, keepdims=True)
-    events(3, 9, 12)
+    events(3, 7, 12)
     done.wait()
     events(3, 12, 14)
     pending.append(load(fout.at[:, pl.ds(0, 1152)], oq_out))

time: 523 us -> 511 us (0.977)
  Pallas kernels: 513 us -> 500 us
    pallas_call x1, Pallas kernels: 255 us -> 242 us  [backward_pass(): pl.pallas_call(bwd_kernel, out_shape=outs, in_specs=[pl.BlockSpec(memory_...]
where the time goes in v9:
time: 511 us; the launch traced here: 503 us
  Pallas kernels  500 us (98%)
    pallas_call x1, Pallas kernels, forward_pass(): pl.pallas_call(fwd_kernel, out_shape=outs, in_specs=[pl.BlockSpec(memory_...  251 us
    pallas_call x1, Pallas kernels, backward_pass(): pl.pallas_call(bwd_kernel, out_shape=outs, in_specs=[pl.BlockSpec(memory_...  242 us

profile of v9, /device:TPU:0, one launch (start us, length us, event | category | flops | bytes accessed | tf_op | source)
XLA Modules:
  0.0 502.9 jit_solution(6568050090481057845)
XLA Ops:
  0.6 251.3 %shard_map.239 = (bf16[8,256,640]{2,1,0:T(8,128)(2,1)}, bf16[8,256,512]{2,1,0:T(8,128)(2,1)}, bf16[8,256,1376]{2,1,0:T(8,128)(2,1)}, bf16[8,256,1376]{2,1,0:T(8,...) custom-call(s32[3]{0:T(128)} %lengths.3, ...), custom_call_target="tpu_custom_call" | custom-call | tf_op jit(solution)/shard_map/pallas_call | solution.py:1540
  251.9 242.5 %shard_map.240 = (f32[256,1376]{1,0:T(8,128)}, f32[256,1376]{1,0:T(8,128)}, f32[256,1376]{1,0:T(8,128)}, f32[256,1152]{1,0:T(8,128)}, bf16[256,2048]{1,0:T(8,128...) custom-call(s32[3]{0:T(128)} %lengths.3, bf16[4,128,256]{2,1,0:T(8,128)(2,1)} %constant.8.clone.sa_ref, ...), custom_call_target="tpu_custom_call" | custom-call | tf_op jit(solution)/shard_map/pallas_call | solution.py:1621
  494.4 6.7 %shard_map.241 = (f32[1376,256]{1,0:T(8,128)}, f32[1376,256]{1,0:T(8,128)}, f32[1376,256]{1,0:T(8,128)}, f32[512,256]{1,0:T(8,128)}, f32[64,256]{1,0:T(8,128)}, ...) custom-call(f32[256,1376]{1,0:T(8,128)} %get-tuple-element.63.d_in, ...), custom_call_target="tpu_custom_call" | custom-call | tf_op jit(solution)/shard_map/pallas_call | solution.py:1683
  501.1 1.3 fusion

commit v10 on v9

--- a/solution.py
+++ b/solution.py
@@ -1068,7 +1068,7 @@
 
         lax.fori_loop(0, n, step, 0)
 
-    plan = {0: (s1, ff, 0), 1: (s2, ff, 0), 2: (s1, ff, 0), 3: (s2, 1152, 0)}
+    plan = {0: (s1, ff, 0), 1: (s2, ff, 0), 2: (s1, ff, 0), 3: (s2, 512, 0), 4: (s2, 640, 512)}
 
     def event(a, e):
         own, wide, column = plan[a]
@@ -1315,6 +1315,15 @@
     both(1, 10, 2, 7, 1)
     local_head(3)
     both(1, 11, 2, 8, 1)
+    done.wait()
+    both(1, 12, 2, 9, 2)
+    done = load(fout.at[:, pl.ds(0, ff)], g_out)
+
+    def grad_out(i):
+        s2[col(i), 0:512] = dot_tt(rows_all[:, col(i)], yb[...]).astype(bf16)
+
+    run(8, grad_out)
+    begin(3)
     moved.take()
 
     def split_state(ref, h):
@@ -1352,21 +1361,22 @@
         r = col(i, 256)
         dqkv[r, 0:128] = (dq[r, :] + pltpu.roll(dk[r, :], 64, 1)).astype(bf16)
 
+    both(2, 11, 3, 0, 1)
     run(4, join)
-    done.wait()
-    both(1, 12, 2, 9, 2)
-    done = load(fout.at[:, pl.ds(0, ff)], g_out)
     own_w = load(wg_all.at[7], stream.at[0, 0])
 
     def grad_out_qkv(i, slot):
-        s2[col(i), 0:512] = dot_tt(rows_all[:, col(i)], yb[...]).astype(bf16)
         s2[col(i), 512:1152] = dot_tt(hs[slot], dqkv[...]).astype(bf16)
-        pl.when(i == 1)(lambda: begin(3))
-
-    chunks_of(h_tiles(h1_all), 8, grad_out_qkv, (2, 11, 1))
+
+    chunks_of(h_tiles(h1_all), 8, grad_out_qkv, (3, 1, 1))
 
     own_w.wait()
     gain_two = jnp.sum(fout[:, 0:ff] * stream[0, 0].astype(f32), axis=1, keepdims=True)
+
+    done.wait()
+    both(2, 12, 3, 2, 2)
+    done = load(fout.at[:, pl.ds(0, ff)], u_out)
+    begin(4)
 
     def wq_tiles(i, slot):
         return [(wq_all.at[i], stream.at[slot, 0, :, pl.ds(0, 640)])]
@@ -1375,11 +1385,9 @@
         sums.offer(i, 2, dot_t(dqkv[...], stream[slot, 0, :, 0:640]))
         pl.when(i > 0)(lambda: sums.pass_on(i - 1, 2))
 
-    chunks_of(wq_tiles, 8, grad_hidden_first, (3, 0, 1))
+    chunks_of(wq_tiles, 8, grad_hidden_first, (3, 4, 2))
     sums.pass_on(7, 2)
-    done.wait()
-    both(2, 12, 3, 1, 2)
-    done = load(fout.at[:, pl.ds(0, ff)], u_out)
+    both(3, 6, 4, 0, 4)
 
     def take_first(i):
         def use(value):
@@ -1387,7 +1395,7 @@
 
         sums.take(i, 2, use)
 
-    run(8, take_first, (3, 3, 4))
+    run(8, take_first, (4, 4, 2))
     for made in got_x:
         made.wait()
 
@@ -1407,11 +1415,15 @@
     own_w.wait()
     own_q.wait()
     gain_two += jnp.sum(fout[:, 0:ff] * stream[0, 0].astype(f32), axis=1, keepdims=True)
-    events(3, 7, 12)
+    both(3, 10, 4, 6, 2)
     done.wait()
     events(3, 12, 14)
-    pending.append(load(fout.at[:, pl.ds(0, 1152)], oq_out))
-    gain_one = jnp.sum(fout[:, 512:1152] * stream[1, 0, :, 0:640].astype(f32), axis=1, keepdims=True)
+    done = load(fout.at[:, pl.ds(0, 512)], oq_out.at[:, pl.ds(0, 512)])
+    events(4, 8, 12)
+    done.wait()
+    events(4, 12, 14)
+    pending.append(load(fout.at[:, pl.ds(0, 640)], oq_out.at[:, pl.ds(512, 640)]))
+    gain_one = jnp.sum(fout[:, 0:640] * stream[1, 0, :, 0:640].astype(f32), axis=1, keepdims=True)
     lane = lax.broadcasted_iota(jnp.int32, (256, 128), 1)
     both = jnp.where(lane == 0, gain_one, jnp.where(lane == 1, gain_two, 0.0)).T[0:8, :]
     terms[0] = both

time: 511 us -> 529 us (1.035)
  Pallas kernels: 500 us -> 519 us
    pallas_call x1, Pallas kernels: 242 us -> 261 us  [backward_pass(): pl.pallas_call(bwd_kernel, out_shape=outs, in_specs=[pl.BlockSpec(memory_...]
where the time goes in v10:
time: 529 us; the launch traced here: 522 us
  Pallas kernels  519 us (98%)
    pallas_call x1, Pallas kernels, backward_pass(): pl.pallas_call(bwd_kernel, out_shape=outs, in_specs=[pl.BlockSpec(memory_...  261 us
    pallas_call x1, Pallas kernels, forward_pass(): pl.pallas_call(fwd_kernel, out_shape=outs, in_specs=[pl.BlockSpec(memory_...  251 us

profile of v10, /device:TPU:0, one launch (start us, length us, event | category | flops | bytes accessed | tf_op | source)
XLA Modules:
  0.0 521.8 jit_solution(9475873378282324331)
XLA Ops:
  0.6 251.3 %shard_map.239 = (bf16[8,256,640]{2,1,0:T(8,128)(2,1)}, bf16[8,256,512]{2,1,0:T(8,128)(2,1)}, bf16[8,256,1376]{2,1,0:T(8,128)(2,1)}, bf16[8,256,1376]{2,1,0:T(8,...) custom-call(s32[3]{0:T(128)} %lengths.3, ...), custom_call_target="tpu_custom_call" | custom-call | tf_op jit(solution)/shard_map/pallas_call | solution.py:1552
  251.9 261.4 %shard_map.240 = (f32[256,1376]{1,0:T(8,128)}, f32[256,1376]{1,0:T(8,128)}, f32[256,1376]{1,0:T(8,128)}, f32[256,1152]{1,0:T(8,128)}, bf16[256,2048]{1,0:T(8,128...) custom-call(s32[3]{0:T(128)} %lengths.3, bf16[4,128,256]{2,1,0:T(8,128)(2,1)} %constant.8.clone.sa_ref, ...), custom_call_target="tpu_custom_call" | custom-call | tf_op jit(solution)/shard_map/pallas_call | solution.py:1633
  513.3 6.7 %shard_map.241 = (f32[1376,256]{1,0:T(8,128)}, f32[1376,256]{1,0:T(8,128)}, f32[1376,256]{1,0:T(8,128)}, f32[512,256]{1,0:T(8,128)}, f32[64,256]{1,0:T(8,128)}, ...) custom-call(f32[256,1376]{1,0:T(8,128)} %get-tuple-element.63.d_in, ...), custom_call_target="tpu_custom_call" | custom-call | tf_op jit(solution)/shard_map/pallas_call | solution.py:1695
  520.0 1.3 fusion
